TPU v7x, 32 devices: a whole 2x2x4 slice. The times are simulated.
32 devices in a mesh: level: 4 (over y, x), blk: 8 (over z, core).
Axes of the slice: x: 2, y: 2, z: 4, core: 2. Of those that a mesh axis runs over, the one named last changes fastest.
Arguments:
- right_sides: float32 [4, 512, 2048], P('level', None, 'blk'), may hold values from -6 to 6
- leaf_gen: float32 [4, 2048, 256], P('level', 'blk'), may hold values from -1 to 1, as said below
- leaf_inverse: float32 [4, 1024, 128], P('level', 'blk'), may hold values from -0.5 to 0.5
- leaf_lower: float32 [4, 1024, 128], P('level', 'blk'), may hold values from -0.5 to 0.5
- node_gen: float32 [4, 8, 3, 256, 256], P('level', 'blk'), may hold values from -1 to 1, as said below
- node_inverse: float32 [4, 8, 3, 128, 128], P('level', 'blk'), may hold values from -1 to 1, as said below
- node_lower: float32 [4, 8, 3, 128, 128], P('level', 'blk'), may hold values from -1 to 1, as said below
- coupling: float32 [4, 128, 256], P('level'), may hold values from -0.5 to 0.5
- child_leaf: int32 [4], P('level'), may hold values from 0 to 7
Outputs:
- leaf_solution: float32 [4, 512, 1024], P('level', None, 'blk')
- node_solution: float32 [4, 8, 3, 512, 128], P('level', 'blk')
- root_skeleton: float32 [4, 512, 128], P('level')
Inputs may be any that keep to these rules, and one draw needn't show every extreme that they name: `leaf_gen`: each leaf's 256 x 256 block is orthogonal. node_gen[p, i, h] is orthogonal and equal for all leaves i with the same i >> (h + 1). node_inverse[p, i, h] is equal for all leaves i with the same i >> (h + 1). node_lower[p, i, h] is equal for all leaves i with the same i >> (h + 1).
All inputs are finite; a program needn't handle non-finite values.
Results may differ from a plain program's by a relative error of at most 0.0003.
Values sent between devices are 32-bit elements; how exact they have to be, the bound alone decides.
No kernel may reach another device: no remote copies, remote signals or barrier semaphores. Data moves between devices by JAX's collectives and lax.ppermute only.
A program may use at most 64 MiB of HBM per device.

v0:
```python
import functools

import jax
import jax.numpy as jnp
from jax import lax
from jax.experimental import pallas as pl
from jax.experimental.pallas import tpu as pltpu
from jax.sharding import PartitionSpec as P


f32 = jnp.float32
bf16 = jnp.bfloat16
VMEM_LIMIT = 12 << 20


def split(value):
    high = value.astype(bf16)
    return high, (value - high.astype(f32)).astype(bf16)


def wide_left(value):
    high, low = split(value)
    return jnp.concatenate([high, low, high], axis=1)


def wide_right(value):
    high, low = split(value)
    return jnp.concatenate([high, high, low], axis=0)


def wide_dot(left, right):
    return jnp.dot(left, right, preferred_element_type=f32)


def product(left, right):
    return wide_dot(wide_left(left), wide_right(right))


def call(kernel, out_shape, args, flops, in_specs=None, out_specs=None, scratch_shapes=()):
    size = lambda s: s.size * s.dtype.itemsize
    vmem = pl.BlockSpec(memory_space=pltpu.VMEM)
    moved = sum(size(a) for a in args) + sum(size(o) for o in jax.tree.leaves(out_shape))
    return pl.pallas_call(
        kernel,
        out_shape=out_shape,
        in_specs=in_specs or [vmem] * len(args),
        out_specs=out_specs or jax.tree.map(lambda _: vmem, out_shape),
        scratch_shapes=scratch_shapes,
        compiler_params=pltpu.CompilerParams(vmem_limit_bytes=VMEM_LIMIT),
        cost_estimate=pl.CostEstimate(flops=flops, bytes_accessed=moved, transcendentals=0),
    )(*args)


def span(index, length):
    return pl.ds(pl.multiple_of(index * length, 8), length)


def leaf_kernel(
    right, generator, inverse, lower, coupling, *refs
):
    later, (away, home, solve_map), refs = refs[:3], refs[3:6], refs[6:]
    (right_here, coupling_here, *later_here), refs = refs[:5], refs[5:]
    generator_here, inverse_here, lower_here, sems = refs
    core = lax.axis_index("blk") & 1
    half, k_half = right.shape[0] // 2, coupling.shape[0] // 2
    copies = [
        pltpu.make_async_copy(source, target, sems.at[i])
        for i, (source, target) in enumerate(
            [
                (generator, generator_here),
                (inverse, inverse_here),
                (lower, lower_here),
                (right.at[span(1 - core, half)], right_here.at[0]),
                (coupling, coupling_here),
                (right.at[span(core, half)], right_here.at[1]),
                *zip(later, later_here),
            ]
        )
    ]
    for copy in copies[:6]:
        copy.start()
    for copy in copies[:2]:
        copy.wait()
    for copy in copies[6:]:
        copy.start()
    solved = product(generator_here[:, : inverse.shape[0]], inverse_here[...])
    solve_map[...] = solved
    copies[2].wait()
    parts = wide_right(generator_here[:, inverse.shape[0] :] - product(solved, lower_here[...]))
    copies[3].wait()
    away[:half, :] = wide_dot(wide_left(right_here[0]), parts)
    copies[4].wait()
    away[half:, :] = wide_dot(wide_left(coupling_here[span(1 - core, k_half), :]), parts)
    home[half:, :] = wide_dot(wide_left(coupling_here[span(core, k_half), :]), parts)
    copies[5].wait()
    home[:half, :] = wide_dot(wide_left(right_here[1]), parts)
    for copy in copies[6:]:
        copy.wait()


def leaf_solve_kernel(child, right, coupling, solve_map, solved, leaf_map):
    parts = wide_right(solve_map[...])
    for part in range(2):
        solved[part] = wide_dot(wide_left(right[1 - part]), parts)
    on_target = lax.axis_index("blk") == child[0]
    leaf_map[...] = jnp.where(on_target, wide_dot(wide_left(coupling[...]), parts), 0.0)


def fold_kernel(first, last, generator, inverse, lower, *refs):
    if first == 0:
        home, other_maps, base, both, mine_maps = refs
    else:
        mine_maps, other_maps, both = refs[-3:]
    size = inverse.shape[1]
    for tier in range(first, last):
        solve_map = product(generator[tier, :, :size], inverse[tier])
        both[:, :size] = solve_map
        both[:, size:] = generator[tier, :, size:] - product(solve_map, lower[tier])
        upper = (lax.axis_index("blk") >> tier) & 1
        mine_maps[tier - first] = wide_right(both[span(upper, size), :])
        other_maps[tier - first] = wide_right(both[span(1 - upper, size), :])
    if first == 0:
        base[...] = wide_dot(wide_left(home[...]), mine_maps[0])


def base_kernel(index, home, mine_maps, base):
    base[...] = wide_dot(wide_left(home[...]), mine_maps[index])


def merge_kernel(index, base, away, other_maps, *refs):
    node, skeleton = refs[-2:]
    size = away.shape[1]
    both = base[...] + wide_dot(wide_left(away[...]), other_maps[index])
    skeleton[...] = both[:, size:]
    node[...] = both[:, :size]


def first_merge_kernel(half, child, base, away, other_maps, node, skeleton, carried):
    size = away.shape[1]
    position = lax.axis_index("blk")
    both = base[:half, :] + wide_dot(wide_left(away[:half, :]), other_maps[0])
    skeleton[...] = both[:, size:]
    node[...] = both[:, :size]
    carried[...] = jnp.where(position == child[0], base[half:, :], 0.0) + jnp.where(
        position ^ 1 == child[0], wide_dot(wide_left(away[half:, :]), other_maps[0]), 0.0
    )


def climb_kernel(index, carried, mine_maps, climb):
    size = carried.shape[1]
    climb[...] = wide_dot(wide_left(carried[...]), mine_maps[index, :, size:])


def relay_kernel(carried, climb, far, out):
    for i, value in enumerate((carried, climb, far)):
        out[i] = value[...]


def pair_kernel(index, home, away, mine_maps, other_maps, out):
    out[...] = wide_dot(wide_left(home[...]), mine_maps[index]) + wide_dot(
        wide_left(away[...]), other_maps[index]
    )


def top_kernel(index, tails, home, away, mine_maps, other_maps, out):
    size = tails.shape[2]
    count = tails.shape[0]
    out[:count] = tails[...]
    out[count] = wide_dot(wide_left(home[0]), mine_maps[index, :, :size]) + wide_dot(
        wide_left(away[0]), other_maps[index, :, :size]
    )
    both = wide_dot(wide_left(home[1] + away[1]), mine_maps[index + 1]) + wide_dot(
        wide_left(home[2] + away[2]), other_maps[index + 1]
    )
    out[count + 1] = both[:, :size]
    out[count + 2] = both[:, size:]


def last_merge_kernel(index, base, away, other_maps, tails, *refs):
    node, root = refs[-2:]
    half, size = away.shape
    both = base[...] + wide_dot(wide_left(away[...]), other_maps[index])
    root[:half, :] = both[:, size:]
    root[half:, :] = tails[tails.shape[0] - 1]
    node[...] = both[:, :size]


def maps_kernel(leaf_map, home, away, *refs):
    wide_maps, maps = refs[-2:]
    k_half, size = home.shape[1:]
    core = lax.axis_index("blk") & 1
    maps[:, :size] = leaf_map[...]
    for i in range(home.shape[0]):
        columns = slice((i + 1) * size, (i + 2) * size)
        maps[span(core, k_half), columns] = home[i]
        maps[span(1 - core, k_half), columns] = away[i]
    wide_maps[...] = wide_right(maps[...])


def final_kernel(fronts, height, solved, wide_maps, *refs):
    nodes, refs = refs[: 2 * height], refs[2 * height :]
    roots, refs = refs[: 2 * fronts], refs[2 * fronts :]
    leaf_out, node_out, root_out, root_maps, incoming, result, sems = refs
    core, level = lax.axis_index("blk") & 1, lax.axis_index("level")
    half, size = solved.shape[1:]
    k_half = root_maps.shape[1] // 2
    for front in range(1, fronts):
        root_maps[front, span(core, k_half), :] = roots[2 * front][half:, :]
        root_maps[front, span(1 - core, k_half), :] = roots[2 * front + 1][half:, :]

    @pl.when(level == 0)
    def _():
        incoming[...] = jnp.zeros_like(incoming)

    for here in range(1, fronts):

        @pl.when(level == here)
        def _():
            for part in range(2):
                value = roots[2 * here + part][:half, :]
                for front in range(1, here):
                    value = roots[2 * (here ^ front) + part][:half, :] + product(
                        value, root_maps[here ^ front]
                    )
                incoming[part] = value

    copies = []
    for part, which in ((0, core), (1, 1 - core)):
        rows = span(which, half)
        change = wide_dot(wide_left(incoming[part]), wide_maps[...])
        bases = (
            [solved[part]]
            + [nodes[2 * tier + part][...] for tier in range(height)]
            + [roots[part][:half, :]]
        )
        targets = (
            [leaf_out.at[rows]] + [node_out.at[tier, rows] for tier in range(height)] + [root_out.at[rows]]
        )
        for i, (base, target) in enumerate(zip(bases, targets)):
            result[part, i] = base + change[:, i * size : (i + 1) * size]
            copies.append(pltpu.make_async_copy(result.at[part, i], target, sems.at[part, i]))
            copies[-1].start()
    for copy in copies:
        copy.wait()


def shards(
    right_sides,
    leaf_gen,
    leaf_inverse,
    leaf_lower,
    node_gen,
    node_inverse,
    node_lower,
    coupling,
    child_leaf,
):
    rows, leaf_size = right_sides.shape[1:]
    size = leaf_lower.shape[2]
    k_rows = coupling.shape[1]
    height = node_gen.shape[2]
    fronts = lax.axis_size("level")
    leaves = lax.axis_size("blk")
    half = rows // 2
    part = half + k_rows // 2
    smem = pl.BlockSpec(memory_space=pltpu.SMEM)
    vmem = pl.BlockSpec(memory_space=pltpu.VMEM)
    hbm = pl.BlockSpec(memory_space=pltpu.HBM)
    anywhere = pl.BlockSpec(memory_space=pl.ANY)
    array = lambda *shape: jax.ShapeDtypeStruct(shape, f32)

    def blk_swap(value, mask):
        return lax.ppermute(value, "blk", [(i, i ^ mask) for i in range(leaves)])

    def level_swap(value, mask):
        return lax.ppermute(value, "level", [(i, i ^ mask) for i in range(fronts)])

    away, home, leaf_solve, right_here, coupling_here, *node_params = call(
        leaf_kernel,
        (
            array(part, size),
            array(part, size),
            array(leaf_size, size),
            array(2, half, leaf_size),
            array(k_rows, leaf_size),
            array(*node_gen.shape[2:]),
            array(*node_inverse.shape[2:]),
            array(*node_lower.shape[2:]),
        ),
        tuple(
            pltpu.with_memory_space_constraint(value, pltpu.HBM)
            for value in (
                right_sides[0],
                leaf_gen[0],
                leaf_inverse[0],
                leaf_lower[0],
                coupling[0],
                node_gen[0, 0],
                node_inverse[0, 0],
                node_lower[0, 0],
            )
        ),
        6 * (rows + k_rows + leaf_size) * leaf_size * size,
        in_specs=[hbm] * 8,
        scratch_shapes=[
            pltpu.VMEM((leaf_size, leaf_size), f32),
            pltpu.VMEM((size, size), f32),
            pltpu.VMEM((size, size), f32),
            pltpu.SemaphoreType.DMA((9,)),
        ],
    )

    def folds(first, last, *home):
        maps = jax.ShapeDtypeStruct((last - first, 3 * size, 2 * size), bf16)
        return call(
            functools.partial(fold_kernel, first, last),
            (maps, array(part, 2 * size)) if home else (maps, maps),
            (*node_params, *home),
            (last - first) * 6 * 4 * size * size * size,
            scratch_shapes=[pltpu.VMEM((2 * size, 2 * size), f32)]
            + [pltpu.VMEM(maps.shape, bf16)] * len(home),
        )

    home, child_leaf = lax.optimization_barrier((home, child_leaf))
    other_maps, base = folds(0, 1, home)
    away = blk_swap(away, 1)
    k_half = k_rows // 2
    merge_flops = 6 * half * 2 * size * size
    node, skeleton, carried = call(
        functools.partial(first_merge_kernel, half),
        (array(half, size), array(half, size), array(k_half, 2 * size)),
        (child_leaf, base, away, other_maps),
        merge_flops,
        in_specs=[smem] + [vmem] * 3,
    )
    nodes, tails, carried = [node], [carried[:, :size]], carried[:, size:]
    for tier in range(1, height):
        away = blk_swap(skeleton, 1 << tier)
        after = ()
        if tier == 1:
            mine_maps, other_maps = folds(1, height)
        if tier < height - 2:
            both = call(
                functools.partial(pair_kernel, tier - 1),
                array(k_half, 2 * size),
                (carried, blk_swap(carried, 1 << tier), mine_maps, other_maps),
                6 * k_half * 4 * size * size,
            )
            tails.append(both[:, :size])
            carried = both[:, size:]
        if tier == height - 2:
            climb = call(
                functools.partial(climb_kernel, tier - 1),
                array(k_half, size),
                (carried, mine_maps),
                6 * k_half * size * size,
            )
            far = blk_swap(climb, 2 << tier)
            after = (climb,)
        if tier == height - 1:
            relay = call(relay_kernel, array(3, k_half, size), (carried, climb, far), k_half * size)
            relayed = blk_swap(relay, 1 << (tier - 1))
            tails = call(
                functools.partial(top_kernel, tier - 2),
                array(height + 1, k_half, size),
                (jnp.stack(tails), relay, relayed, mine_maps, other_maps),
                6 * k_half * 6 * size * size,
            )
            solved, leaf_map = call(
                leaf_solve_kernel,
                (array(2, half, size), array(k_rows, size)),
                (child_leaf, right_here, coupling_here, leaf_solve),
                6 * (rows + k_rows) * leaf_size * size,
                in_specs=[smem] + [vmem] * 3,
            )
            after = (solved,)
        base = call(
            functools.partial(base_kernel, tier - 1),
            array(half, 2 * size),
            (skeleton, mine_maps),
            merge_flops,
        )
        last = tier == height - 1
        node, skeleton = call(
            functools.partial(last_merge_kernel if last else merge_kernel, tier - 1),
            (array(half, size), array(part if last else half, size)),
            (base, away, other_maps) + ((tails,) if last else ()) + after,
            merge_flops,
            in_specs=[vmem] * (4 if last else 3) + [anywhere] * len(after),
        )
        nodes.append(node)
    received = [level_swap(skeleton, mask) for mask in range(1, fronts)]
    roots = [skeleton, blk_swap(skeleton, 1)]
    for value in received:
        roots += [value, blk_swap(value, 1)]
    pairs = []
    for value in nodes:
        pairs += [value, blk_swap(value, 1)]
    after = (*pairs[1::2], roots[1])
    wide_maps = call(
        maps_kernel,
        jax.ShapeDtypeStruct((3 * k_rows, size * (height + 2)), bf16),
        (leaf_map, tails, blk_swap(tails, 1), *after),
        k_rows * size * (height + 2) * 4,
        in_specs=[vmem] * 3 + [anywhere] * len(after),
        scratch_shapes=[pltpu.VMEM((k_rows, size * (height + 2)), f32)],
    )
    leaf_out, node_out, root_out = call(
        functools.partial(final_kernel, fronts, height),
        (array(rows, size), array(height, rows, size), array(rows, size)),
        (solved, wide_maps, *pairs, *roots),
        6 * rows * size * size * (height + 2),
        out_specs=(hbm,) * 3,
        scratch_shapes=[
            pltpu.VMEM((fronts, k_rows, size), f32),
            pltpu.VMEM((2, half, size), f32),
            pltpu.VMEM((2, height + 2, half, size), f32),
            pltpu.SemaphoreType.DMA((2, height + 2)),
        ],
    )
    return (leaf_out[None], node_out[None, None], root_out[None])


def solution(mesh):
    in_specs = (
        P("level", None, "blk"),
        P("level", "blk", None),
        P("level", "blk", None),
        P("level", "blk", None),
        P("level", "blk", None, None, None),
        P("level", "blk", None, None, None),
        P("level", "blk", None, None, None),
        P("level", None, None),
        P("level"),
    )
    out_specs = (
        P("level", None, "blk"),
        P("level", "blk", None, None, None),
        P("level", None, None),
    )

    return jax.shard_map(shards, mesh=mesh, in_specs=in_specs, out_specs=out_specs, check_vma=False)
```

profile of v0, /device:TPU:0, one launch (start us, length us, event | category | flops | bytes accessed | tf_op | source)
XLA Modules:
  0.0 34.4 jit_solution(13489314694994104885)
XLA Ops:
  0.6 2.3 %shard_map.112 = (f32[320,128]{1,0:T(8,128)S(1)}, f32[320,128]{1,0:T(8,128)S(1)}, f32[256,128]{1,0:T(8,128)S(1)}, f32[2,256,256]{2,1,0:T(8,128)S(1)}, f32[128,25...) custom-call(f32[512,256]{1,0:T(8,128)} %bitcast.14, ...), custom_call_target="tpu_custom_call" | custom-call | flops 176160768 | bytes 4521984 | tf_op jit(solution)/shard_map/pallas_call | solution.py:43
  2.9 0.6 %collective-permute-start = (f32[320,128]{1,0:T(8,128)S(1)}, f32[320,128]{1,0:T(8,128)S(1)}, u32[]{:S(2)}, u32[]{:S(2)}) collective-permute-start(f32[320,128]{1,0:T(8,128)S(1)} %get-tuple-element.41), channel_id=1, source_target_pairs={{0,1},{1,0},{2,3},{3,2},{4,5},{5,4},{6,7},{7,6},{8,9},{9,8},{10,11... | collective-permute-start | bytes 491528 | tf_op jit(solution)/shard_map/ppermute | solution.py:273
  4.2 0.6 %shard_map.114 = (bf16[1,384,256]{2,1,0:T(8,128)(2,1)S(1)}, f32[320,256]{1,0:T(8,128)S(1)}) custom-call(f32[3,256,256]{2,1,0:T(8,128)S(1)} %get-tuple-element.36.generator, f32[3,128,128]{2,1,0:T(8,128)S(1)} %get-tuple-element.37.inverse, f32[3,128,128]{2,1,0:T(8,128)S(1)} %get-tuple-element.38.lower, f32[320,128]{1,0:T(8,128)S(1)} %get-tuple-element.39.refs_0_), custom_call_target="tpu_custom_call" | custom-call | flops 50331648 | bytes 1867776 | tf_op jit(solution)/shard_map/pallas_call | solution.py:43
  4.8 0.6 %shard_map.116 = (bf16[2,384,256]{2,1,0:T(8,128)(2,1)S(1)}, bf16[2,384,256]{2,1,0:T(8,128)(2,1)S(1)}) custom-call(f32[3,256,256]{2,1,0:T(8,128)S(1)} %get-tuple-element.36.generator, f32[3,128,128]{2,1,0:T(8,128)S(1)} %get-tuple-element.37.inverse, f32[3,128,128]{2,1,0:T(8,128)S(1)} %get-tuple-element.38.lower), custom_call_target="tpu_custom_call" | custom-call | flops 100663296 | bytes 1966080 | tf_op jit(solution)/shard_map/pallas_call | solution.py:43
  5.4 0.2 shard_map.115
  5.7 2.6 %collective-permute-start.5 = (f32[256,128]{1,0:T(8,128)S(1)}, f32[256,128]{1,0:T(8,128)S(1)}, u32[]{:S(2)}, u32[]{:S(2)}) collective-permute-start(f32[256,128]{1,0:T(8,128)S(1)} %get-tuple-element.47.home), channel_id=1, source_target_pairs={{0,2},{1,3},{2,0},{3,1},{4,6},{5,7},{6,4},{7,5},{8,10},{9,11},{10,... | collective-permute-start | bytes 393224 | tf_op jit(solution)/shard_map/ppermute | solution.py:273
  8.4 2.7 %collective-permute-start.1 = (f32[64,128]{1,0:T(8,128)S(1)}, f32[64,128]{1,0:T(8,128)S(1)}, u32[]{:S(2)}, u32[]{:S(2)}) collective-permute-start(f32[64,128]{1,0:T(8,128)S(1)} %shard_map.117.climb.refs_0_), channel_id=1, source_target_pairs={{0,4},{1,5},{2,6},{3,7},{4,0},{5,1},{6,2},{7,3},{8,12},{9,13},{10,... | collective-permute-start | bytes 98312 | tf_op jit(solution)/shard_map/ppermute | solution.py:273
  11.3 1.5 %collective-permute-done.5.away = f32[256,128]{1,0:T(8,128)S(1)} collective-permute-done((f32[256,128]{1,0:T(8,128)S(1)}, f32[256,128]{1,0:T(8,128)S(1)}, u32[]{:S(2)}, u32[]{:S(2)}) %collective-permute-start.5) | collective-permute-done | bytes 131104 | tf_op jit(solution)/shard_map/ppermute | solution.py:273
  13.0 2.8 %collective-permute-start.7 = (f32[256,128]{1,0:T(8,128)S(1)}, f32[256,128]{1,0:T(8,128)S(1)}, u32[]{:S(2)}, u32[]{:S(2)}) collective-permute-start(f32[256,128]{1,0:T(8,128)S(1)} %get-tuple-element.49.home), channel_id=1, source_target_pairs={{0,4},{1,5},{2,6},{3,7},{4,0},{5,1},{6,2},{7,3},{8,12},{9,13},{10,... | collective-permute-start | bytes 393224 | tf_op jit(solution)/shard_map/ppermute | solution.py:273
  15.9 2.0 %collective-permute-start.2 = (f32[3,64,128]{2,1,0:T(8,128)S(1)}, f32[3,64,128]{2,1,0:T(8,128)S(1)}, u32[]{:S(2)}, u32[]{:S(2)}) collective-permute-start(f32[3,64,128]{2,1,0:T(8,128)S(1)} %shard_map.118.home), channel_id=1, source_target_pairs={{0,2},{1,3},{2,0},{3,1},{4,6},{5,7},{6,4},{7,5},{8,10},{9,11},{10,... | collective-permute-start | bytes 294920 | tf_op jit(solution)/shard_map/ppermute | solution.py:273
  17.9 0.4 %shard_map.113 = (f32[2,256,128]{2,1,0:T(8,128)S(1)}, f32[128,128]{1,0:T(8,128)S(1)}) custom-call(s32[1]{0:T(128)S(6)} %copy.12.child, f32[2,256,256]{2,1,0:T(8,128)S(1)} %get-tuple-element.31.right, f32[128,256]{1,0:T(8,128)S(1)} %get-tuple-element.32.coupling, f32[256,128]{1,0:T(8,128)S(1)} %get-tuple-element.33.solve_map), custom_call_target="tpu_custom_call" | custom-call | flops 125829120 | bytes 1114116 | tf_op jit(solution)/shard_map/pallas_call | solution.py:43
  18.3 0.2 shard_map.122.base
  18.5 2.9 %collective-permute-done.2.away = f32[3,64,128]{2,1,0:T(8,128)S(1)} collective-permute-done((f32[3,64,128]{2,1,0:T(8,128)S(1)}, f32[3,64,128]{2,1,0:T(8,128)S(1)}, u32[]{:S(2)}, u32[]{:S(2)}) %collective-permute-start.2) | collective-permute-done | bytes 98336 | tf_op jit(solution)/shard_map/ppermute | solution.py:273
  21.4 0.2 shard_map.119.tails.home
  22.0 2.6 %collective-permute-start.14 = (f32[320,128]{1,0:T(8,128)S(1)}, f32[320,128]{1,0:T(8,128)S(1)}, u32[]{:S(2)}, u32[]{:S(2)}) collective-permute-start(f32[320,128]{1,0:T(8,128)S(1)} %get-tuple-element.51.refs_6_), channel_id=1, source_target_pairs={{0,24},{8,16},{16,8},{24,0},{1,25},{9,17},{17,9},{25,1},{2,26},{10... | collective-permute-start | bytes 491528 | tf_op jit(solution)/shard_map/ppermute | solution.py:276
  24.7 0.5 %collective-permute-start.12 = (f32[320,128]{1,0:T(8,128)S(1)}, f32[320,128]{1,0:T(8,128)S(1)}, u32[]{:S(2)}, u32[]{:S(2)}) collective-permute-start(f32[320,128]{1,0:T(8,128)S(1)} %get-tuple-element.51.refs_6_), channel_id=1, source_target_pairs={{0,16},{8,24},{16,0},{24,8},{1,17},{9,25},{17,1},{25,9},{2,18},{10... | collective-permute-start | bytes 491528 | tf_op jit(solution)/shard_map/ppermute | solution.py:276
  25.2 0.4 %collective-permute-start.10 = (f32[320,128]{1,0:T(8,128)S(1)}, f32[320,128]{1,0:T(8,128)S(1)}, u32[]{:S(2)}, u32[]{:S(2)}) collective-permute-start(f32[320,128]{1,0:T(8,128)S(1)} %get-tuple-element.51.refs_6_), channel_id=1, source_target_pairs={{0,8},{8,0},{16,24},{24,16},{1,9},{9,1},{17,25},{25,17},{2,10},{10... | collective-permute-start | bytes 491528 | tf_op jit(solution)/shard_map/ppermute | solution.py:276
  25.6 0.5 %collective-permute-start.6 = (f32[256,128]{1,0:T(8,128)S(1)}, f32[256,128]{1,0:T(8,128)S(1)}, u32[]{:S(2)}, u32[]{:S(2)}) collective-permute-start(f32[256,128]{1,0:T(8,128)S(1)} %get-tuple-element.48.refs_2_), channel_id=1, source_target_pairs={{0,1},{1,0},{2,3},{3,2},{4,5},{5,4},{6,7},{7,6},{8,9},{9,8},{10,11... | collective-permute-start | bytes 393224 | tf_op jit(solution)/shard_map/ppermute | solution.py:273
  26.1 0.8 %collective-permute-done.3.away = f32[4,64,128]{2,1,0:T(8,128)S(1)} collective-permute-done((f32[4,64,128]{2,1,0:T(8,128)S(1)}, f32[4,64,128]{2,1,0:T(8,128)S(1)}, u32[]{:S(2)}, u32[]{:S(2)}) %collective-permute-start.3) | collective-permute-done | bytes 131104 | tf_op jit(solution)/shard_map/ppermute | solution.py:273
  27.1 2.6 %collective-permute-done.14.refs_12_ = f32[320,128]{1,0:T(8,128)S(1)} collective-permute-done((f32[320,128]{1,0:T(8,128)S(1)}, f32[320,128]{1,0:T(8,128)S(1)}, u32[]{:S(2)}, u32[]{:S(2)}) %collective-permute-start.14) | collective-permute-done | bytes 163872 | tf_op jit(solution)/shard_map/ppermute | solution.py:276
  29.7 1.2 %collective-permute-done.12.refs_10_ = f32[320,128]{1,0:T(8,128)S(1)} collective-permute-done((f32[320,128]{1,0:T(8,128)S(1)}, f32[320,128]{1,0:T(8,128)S(1)}, u32[]{:S(2)}, u32[]{:S(2)}) %collective-permute-start.12) | collective-permute-done | bytes 163872 | tf_op jit(solution)/shard_map/ppermute | solution.py:276
  30.9 0.5 %collective-permute-start.11 = (f32[320,128]{1,0:T(8,128)S(1)}, f32[320,128]{1,0:T(8,128)S(1)}, u32[]{:S(2)}, u32[]{:S(2)}) collective-permute-start(f32[320,128]{1,0:T(8,128)S(1)} %collective-permute-done.10.refs_8_), channel_id=1, source_target_pairs={{0,1},{1,0},{2,3},{3,2},{4,5},{5,4},{6,7},{7,6},{8,9},{9,8},{10,11... | collective-permute-start | bytes 491528 | tf_op jit(solution)/shard_map/ppermute | solution.py:273
  31.5 1.3 %collective-permute-done.8.refs_2_.refs_5_ = f32[256,128]{1,0:T(8,128)S(1)} collective-permute-done((f32[256,128]{1,0:T(8,128)S(1)}, f32[256,128]{1,0:T(8,128)S(1)}, u32[]{:S(2)}, u32[]{:S(2)}) %collective-permute-start.8) | collective-permute-done | bytes 131104 | tf_op jit(solution)/shard_map/ppermute | solution.py:273
  32.9 1.5 %shard_map.125 = (f32[512,128]{1,0:T(8,128)}, f32[3,512,128]{2,1,0:T(8,128)}, f32[512,128]{1,0:T(8,128)}) custom-call(f32[2,256,128]{2,1,0:T(8,128)S(1)} %get-tuple-element.34.refs_0_.solved, bf16[384,640]{1,0:T(8,128)(2,1)S(1)} %shard_map.124.wide_maps, f32[256,128]{1,0:T(8,128)S(1)} %get-tuple-element.46.refs_0_, ...), custom_call_target="tpu_custom_call" | custom-call | flops 251658240 | bytes 4161536 | tf_op jit(solution)/shard_map/pallas_call | solution.py:43
  (23 shorter events, 1.3 us)
Async XLA Ops:
  2.9 2.5 %collective-permute-start = (f32[320,128]{1,0:T(8,128)S(1)}, f32[320,128]{1,0:T(8,128)S(1)}, u32[]{:S(2)}, u32[]{:S(2)}) collective-permute-start(f32[320,128]{1,0:T(8,128)S(1)} %get-tuple-element.41), channel_id=1, source_target_pairs={{0,1},{1,0},{2,3},{3,2},{4,5},{5,4},{6,7},{7,6},{8,9},{9,8},{10,11... | collective-permute-start | bytes 491528 | tf_op jit(solution)/shard_map/ppermute | solution.py:273
  5.7 7.2 %collective-permute-start.5 = (f32[256,128]{1,0:T(8,128)S(1)}, f32[256,128]{1,0:T(8,128)S(1)}, u32[]{:S(2)}, u32[]{:S(2)}) collective-permute-start(f32[256,128]{1,0:T(8,128)S(1)} %get-tuple-element.47.home), channel_id=1, source_target_pairs={{0,2},{1,3},{2,0},{3,1},{4,6},{5,7},{6,4},{7,5},{8,10},{9,11},{10,... | collective-permute-start | bytes 393224 | tf_op jit(solution)/shard_map/ppermute | solution.py:273
  8.4 7.4 %collective-permute-start.1 = (f32[64,128]{1,0:T(8,128)S(1)}, f32[64,128]{1,0:T(8,128)S(1)}, u32[]{:S(2)}, u32[]{:S(2)}) collective-permute-start(f32[64,128]{1,0:T(8,128)S(1)} %shard_map.117.climb.refs_0_), channel_id=1, source_target_pairs={{0,4},{1,5},{2,6},{3,7},{4,0},{5,1},{6,2},{7,3},{8,12},{9,13},{10,... | collective-permute-start | bytes 98312 | tf_op jit(solution)/shard_map/ppermute | solution.py:273
  13.0 8.8 %collective-permute-start.7 = (f32[256,128]{1,0:T(8,128)S(1)}, f32[256,128]{1,0:T(8,128)S(1)}, u32[]{:S(2)}, u32[]{:S(2)}) collective-permute-start(f32[256,128]{1,0:T(8,128)S(1)} %get-tuple-element.49.home), channel_id=1, source_target_pairs={{0,4},{1,5},{2,6},{3,7},{4,0},{5,1},{6,2},{7,3},{8,12},{9,13},{10,... | collective-permute-start | bytes 393224 | tf_op jit(solution)/shard_map/ppermute | solution.py:273
  15.9 5.5 %collective-permute-start.2 = (f32[3,64,128]{2,1,0:T(8,128)S(1)}, f32[3,64,128]{2,1,0:T(8,128)S(1)}, u32[]{:S(2)}, u32[]{:S(2)}) collective-permute-start(f32[3,64,128]{2,1,0:T(8,128)S(1)} %shard_map.118.home), channel_id=1, source_target_pairs={{0,2},{1,3},{2,0},{3,1},{4,6},{5,7},{6,4},{7,5},{8,10},{9,11},{10,... | collective-permute-start | bytes 294920 | tf_op jit(solution)/shard_map/ppermute | solution.py:273
  17.9 7.7 %collective-permute-start.4 = (f32[256,128]{1,0:T(8,128)S(1)}, f32[256,128]{1,0:T(8,128)S(1)}, u32[]{:S(2)}, u32[]{:S(2)}) collective-permute-start(f32[256,128]{1,0:T(8,128)S(1)} %get-tuple-element.46.refs_0_), channel_id=1, source_target_pairs={{0,1},{1,0},{2,3},{3,2},{4,5},{5,4},{6,7},{7,6},{8,9},{9,8},{10,11... | collective-permute-start | bytes 393224 | tf_op jit(solution)/shard_map/ppermute | solution.py:273
  22.0 7.6 %collective-permute-start.14 = (f32[320,128]{1,0:T(8,128)S(1)}, f32[320,128]{1,0:T(8,128)S(1)}, u32[]{:S(2)}, u32[]{:S(2)}) collective-permute-start(f32[320,128]{1,0:T(8,128)S(1)} %get-tuple-element.51.refs_6_), channel_id=1, source_target_pairs={{0,24},{8,16},{16,8},{24,0},{1,25},{9,17},{17,9},{25,1},{2,26},{10... | collective-permute-start | bytes 491528 | tf_op jit(solution)/shard_map/ppermute | solution.py:276
  24.7 6.2 %collective-permute-start.12 = (f32[320,128]{1,0:T(8,128)S(1)}, f32[320,128]{1,0:T(8,128)S(1)}, u32[]{:S(2)}, u32[]{:S(2)}) collective-permute-start(f32[320,128]{1,0:T(8,128)S(1)} %get-tuple-element.51.refs_6_), channel_id=1, source_target_pairs={{0,16},{8,24},{16,0},{24,8},{1,17},{9,25},{17,1},{25,9},{2,18},{10... | collective-permute-start | bytes 491528 | tf_op jit(solution)/shard_map/ppermute | solution.py:276
  25.2 5.7 %collective-permute-start.10 = (f32[320,128]{1,0:T(8,128)S(1)}, f32[320,128]{1,0:T(8,128)S(1)}, u32[]{:S(2)}, u32[]{:S(2)}) collective-permute-start(f32[320,128]{1,0:T(8,128)S(1)} %get-tuple-element.51.refs_6_), channel_id=1, source_target_pairs={{0,8},{8,0},{16,24},{24,16},{1,9},{9,1},{17,25},{25,17},{2,10},{10... | collective-permute-start | bytes 491528 | tf_op jit(solution)/shard_map/ppermute | solution.py:276
  25.6 1.3 %collective-permute-start.3 = (f32[4,64,128]{2,1,0:T(8,128)S(1)}, f32[4,64,128]{2,1,0:T(8,128)S(1)}, u32[]{:S(2)}, u32[]{:S(2)}) collective-permute-start(f32[4,64,128]{2,1,0:T(8,128)S(1)} %shard_map.119.tails.home), channel_id=1, source_target_pairs={{0,1},{1,0},{2,3},{3,2},{4,5},{5,4},{6,7},{7,6},{8,9},{9,8},{10,11... | collective-permute-start | bytes 393224 | tf_op jit(solution)/shard_map/ppermute | solution.py:273
  25.6 5.8 %collective-permute-start.6 = (f32[256,128]{1,0:T(8,128)S(1)}, f32[256,128]{1,0:T(8,128)S(1)}, u32[]{:S(2)}, u32[]{:S(2)}) collective-permute-start(f32[256,128]{1,0:T(8,128)S(1)} %get-tuple-element.48.refs_2_), channel_id=1, source_target_pairs={{0,1},{1,0},{2,3},{3,2},{4,5},{5,4},{6,7},{7,6},{8,9},{9,8},{10,11... | collective-permute-start | bytes 393224 | tf_op jit(solution)/shard_map/ppermute | solution.py:273
  26.9 5.8 %collective-permute-start.9 = (f32[320,128]{1,0:T(8,128)S(1)}, f32[320,128]{1,0:T(8,128)S(1)}, u32[]{:S(2)}, u32[]{:S(2)}) collective-permute-start(f32[320,128]{1,0:T(8,128)S(1)} %get-tuple-element.51.refs_6_), channel_id=1, source_target_pairs={{0,1},{1,0},{2,3},{3,2},{4,5},{5,4},{6,7},{7,6},{8,9},{9,8},{10,11... | collective-permute-start | bytes 491528 | tf_op jit(solution)/shard_map/ppermute | solution.py:273
  29.7 3.2 %collective-permute-start.15 = (f32[320,128]{1,0:T(8,128)S(1)}, f32[320,128]{1,0:T(8,128)S(1)}, u32[]{:S(2)}, u32[]{:S(2)}) collective-permute-start(f32[320,128]{1,0:T(8,128)S(1)} %collective-permute-done.14.refs_12_), channel_id=1, source_target_pairs={{0,1},{1,0},{2,3},{3,2},{4,5},{5,4},{6,7},{7,6},{8,9},{9,8},{10,11... | collective-permute-start | bytes 491528 | tf_op jit(solution)/shard_map/ppermute | solution.py:273
  30.9 2.0 %collective-permute-start.13 = (f32[320,128]{1,0:T(8,128)S(1)}, f32[320,128]{1,0:T(8,128)S(1)}, u32[]{:S(2)}, u32[]{:S(2)}) collective-permute-start(f32[320,128]{1,0:T(8,128)S(1)} %collective-permute-done.12.refs_10_), channel_id=1, source_target_pairs={{0,1},{1,0},{2,3},{3,2},{4,5},{5,4},{6,7},{7,6},{8,9},{9,8},{10,11... | collective-permute-start | bytes 491528 | tf_op jit(solution)/shard_map/ppermute | solution.py:273
  30.9 2.0 %collective-permute-start.11 = (f32[320,128]{1,0:T(8,128)S(1)}, f32[320,128]{1,0:T(8,128)S(1)}, u32[]{:S(2)}, u32[]{:S(2)}) collective-permute-start(f32[320,128]{1,0:T(8,128)S(1)} %collective-permute-done.10.refs_8_), channel_id=1, source_target_pairs={{0,1},{1,0},{2,3},{3,2},{4,5},{5,4},{6,7},{7,6},{8,9},{9,8},{10,11... | collective-permute-start | bytes 491528 | tf_op jit(solution)/shard_map/ppermute | solution.py:273
  31.4 1.3 %collective-permute-start.8 = (f32[256,128]{1,0:T(8,128)S(1)}, f32[256,128]{1,0:T(8,128)S(1)}, u32[]{:S(2)}, u32[]{:S(2)}) collective-permute-start(f32[256,128]{1,0:T(8,128)S(1)} %get-tuple-element.50.refs_4_), channel_id=1, source_target_pairs={{0,1},{1,0},{2,3},{3,2},{4,5},{5,4},{6,7},{7,6},{8,9},{9,8},{10,11... | collective-permute-start | bytes 393224 | tf_op jit(solution)/shard_map/ppermute | solution.py:273
where the time goes:
time: 35 us; the launch traced here: 34.4 us
  starting transfers between devices  15.5 us (44%)
  waiting for transfers between devices  10.5 us (30%)
  Pallas kernels  7.06 us (20%)
  between operations  1.41 us (4%)
    ppermute x13, starting transfers between devices, blk_swap(): return lax.ppermute(value, 'blk', [(i, i ^ mask) for i in range(leaves)])  11.9 us
    pallas_call x14, Pallas kernels, call(): pl.pallas_call(kernel, out_shape=out_shape, in_specs=in_specs or [vmem] *...  7.06 us
    ppermute x13, waiting for transfers between devices, blk_swap(): return lax.ppermute(value, 'blk', [(i, i ^ mask) for i in range(leaves)])  6.65 us
    ppermute x3, waiting for transfers between devices, level_swap(): return lax.ppermute(value, 'level', [(i, i ^ mask) for i in range(fronts)])  3.83 us
    ppermute x3, starting transfers between devices, level_swap(): return lax.ppermute(value, 'level', [(i, i ^ mask) for i in range(fronts)])  3.55 us
  transfers between devices with their start and end apart: 16, of which 7 were waited for; matrix products, arithmetic and copies ran while one was open for 0% of the time, Pallas kernels for 9%

commit v1 on v0

--- a/solution.py
+++ b/solution.py
@@ -55,14 +55,13 @@
     return pl.ds(pl.multiple_of(index * length, 8), length)
 
 
-def leaf_kernel(
-    right, generator, inverse, lower, coupling, *refs
-):
-    later, (away, home, solve_map), refs = refs[:3], refs[3:6], refs[6:]
+def leaf_kernel(right, generator, inverse, lower, coupling, *refs):
+    later, (away, solve_map, skeleton_map), refs = refs[:3], refs[3:6], refs[6:]
     (right_here, coupling_here, *later_here), refs = refs[:5], refs[5:]
     generator_here, inverse_here, lower_here, sems = refs
     core = lax.axis_index("blk") & 1
     half, k_half = right.shape[0] // 2, coupling.shape[0] // 2
+    size = inverse.shape[0]
     copies = [
         pltpu.make_async_copy(source, target, sems.at[i])
         for i, (source, target) in enumerate(
@@ -73,28 +72,24 @@
                 (right.at[span(1 - core, half)], right_here.at[0]),
                 (coupling, coupling_here),
                 (right.at[span(core, half)], right_here.at[1]),
-                *zip(later, later_here),
+                *((source.at[0], target) for source, target in zip(later, later_here)),
             ]
         )
     ]
-    for copy in copies[:6]:
+    for copy in copies:
         copy.start()
     for copy in copies[:2]:
         copy.wait()
-    for copy in copies[6:]:
-        copy.start()
-    solved = product(generator_here[:, : inverse.shape[0]], inverse_here[...])
+    solved = product(generator_here[:, :size], inverse_here[...])
     solve_map[...] = solved
     copies[2].wait()
-    parts = wide_right(generator_here[:, inverse.shape[0] :] - product(solved, lower_here[...]))
+    parts = wide_right(generator_here[:, size:] - product(solved, lower_here[...]))
+    skeleton_map[...] = parts
     copies[3].wait()
     away[:half, :] = wide_dot(wide_left(right_here[0]), parts)
     copies[4].wait()
     away[half:, :] = wide_dot(wide_left(coupling_here[span(1 - core, k_half), :]), parts)
-    home[half:, :] = wide_dot(wide_left(coupling_here[span(core, k_half), :]), parts)
-    copies[5].wait()
-    home[:half, :] = wide_dot(wide_left(right_here[1]), parts)
-    for copy in copies[6:]:
+    for copy in copies[5:]:
         copy.wait()
 
 
@@ -106,21 +101,31 @@
     leaf_map[...] = jnp.where(on_target, wide_dot(wide_left(coupling[...]), parts), 0.0)
 
 
-def fold_kernel(first, last, generator, inverse, lower, *refs):
-    if first == 0:
-        home, other_maps, base, both, mine_maps = refs
-    else:
-        mine_maps, other_maps, both = refs[-3:]
-    size = inverse.shape[1]
-    for tier in range(first, last):
-        solve_map = product(generator[tier, :, :size], inverse[tier])
-        both[:, :size] = solve_map
-        both[:, size:] = generator[tier, :, size:] - product(solve_map, lower[tier])
-        upper = (lax.axis_index("blk") >> tier) & 1
-        mine_maps[tier - first] = wide_right(both[span(upper, size), :])
-        other_maps[tier - first] = wide_right(both[span(1 - upper, size), :])
-    if first == 0:
-        base[...] = wide_dot(wide_left(home[...]), mine_maps[0])
+def fold(tier, generator, inverse, lower, both):
+    size = inverse.shape[0]
+    solve_map = product(generator[:, :size], inverse)
+    both[:, :size] = solve_map
+    both[:, size:] = generator[:, size:] - product(solve_map, lower)
+    upper = (lax.axis_index("blk") >> tier) & 1
+    return wide_right(both[span(upper, size), :]), wide_right(both[span(1 - upper, size), :])
+
+
+def first_fold_kernel(
+    generator, inverse, lower, right, coupling, skeleton_map, mine_maps, other_maps, base, home, both
+):
+    core = lax.axis_index("blk") & 1
+    k_half = home.shape[0]
+    value = wide_dot(wide_left(right[1]), skeleton_map[...])
+    home[...] = wide_dot(wide_left(coupling[span(core, k_half), :]), skeleton_map[...])
+    mine_maps[0], other_maps[0] = fold(0, generator[...], inverse[...], lower[...], both)
+    base[...] = wide_dot(wide_left(value), mine_maps[0])
+
+
+def fold_kernel(generator, inverse, lower, mine_maps, other_maps, both):
+    for tier in range(1, generator.shape[0]):
+        mine_maps[tier - 1], other_maps[tier - 1] = fold(
+            tier, generator[tier], inverse[tier], lower[tier], both
+        )
 
 
 def base_kernel(index, home, mine_maps, base):
@@ -135,15 +140,21 @@
     node[...] = both[:, :size]
 
 
-def first_merge_kernel(half, child, base, away, other_maps, node, skeleton, carried):
-    size = away.shape[1]
-    position = lax.axis_index("blk")
-    both = base[:half, :] + wide_dot(wide_left(away[:half, :]), other_maps[0])
+def first_merge_kernel(base, away, other_maps, node, skeleton):
+    half, size = node.shape
+    both = base[...] + wide_dot(wide_left(away[:half, :]), other_maps[0])
     skeleton[...] = both[:, size:]
     node[...] = both[:, :size]
-    carried[...] = jnp.where(position == child[0], base[half:, :], 0.0) + jnp.where(
-        position ^ 1 == child[0], wide_dot(wide_left(away[half:, :]), other_maps[0]), 0.0
-    )
+
+
+def carry_kernel(child, home, away, mine_maps, other_maps, tail, carried):
+    k_half, size = home.shape
+    position = lax.axis_index("blk")
+    mine = wide_dot(wide_left(home[...]), mine_maps[0])
+    other = wide_dot(wide_left(away[away.shape[0] - k_half :, :]), other_maps[0])
+    both = jnp.where(position == child[0], mine, 0.0) + jnp.where(position ^ 1 == child[0], other, 0.0)
+    tail[...] = both[:, :size]
+    carried[...] = both[:, size:]
 
 
 def climb_kernel(index, carried, mine_maps, climb):
@@ -208,6 +219,9 @@
         root_maps[front, span(core, k_half), :] = roots[2 * front][half:, :]
         root_maps[front, span(1 - core, k_half), :] = roots[2 * front + 1][half:, :]
 
+    def both_rows(mask):
+        return jnp.concatenate([roots[2 * mask][:half, :], roots[2 * mask + 1][:half, :]], axis=0)
+
     @pl.when(level == 0)
     def _():
         incoming[...] = jnp.zeros_like(incoming)
@@ -216,29 +230,29 @@
 
         @pl.when(level == here)
         def _():
-            for part in range(2):
-                value = roots[2 * here + part][:half, :]
-                for front in range(1, here):
-                    value = roots[2 * (here ^ front) + part][:half, :] + product(
-                        value, root_maps[here ^ front]
-                    )
-                incoming[part] = value
+            value = both_rows(here)
+            for front in range(1, here):
+                value = both_rows(here ^ front) + product(value, root_maps[here ^ front])
+            incoming[...] = value
 
     copies = []
-    for part, which in ((0, core), (1, 1 - core)):
-        rows = span(which, half)
-        change = wide_dot(wide_left(incoming[part]), wide_maps[...])
+    step = half // 2
+    for chunk in range(4):
+        part, first = chunk // 2, chunk % 2 * step
+        inner = slice(first, first + step)
+        rows = pl.ds(pl.multiple_of((core if part == 0 else 1 - core) * half + first, 8), step)
+        change = wide_dot(wide_left(incoming[chunk * step : (chunk + 1) * step, :]), wide_maps[...])
         bases = (
-            [solved[part]]
-            + [nodes[2 * tier + part][...] for tier in range(height)]
-            + [roots[part][:half, :]]
+            [solved[part, inner, :]]
+            + [nodes[2 * tier + part][inner, :] for tier in range(height)]
+            + [roots[part][inner, :]]
         )
         targets = (
             [leaf_out.at[rows]] + [node_out.at[tier, rows] for tier in range(height)] + [root_out.at[rows]]
         )
         for i, (base, target) in enumerate(zip(bases, targets)):
-            result[part, i] = base + change[:, i * size : (i + 1) * size]
-            copies.append(pltpu.make_async_copy(result.at[part, i], target, sems.at[part, i]))
+            result[chunk, i] = base + change[:, i * size : (i + 1) * size]
+            copies.append(pltpu.make_async_copy(result.at[chunk, i], target, sems.at[chunk, i]))
             copies[-1].start()
     for copy in copies:
         copy.wait()
@@ -275,17 +289,17 @@
     def level_swap(value, mask):
         return lax.ppermute(value, "level", [(i, i ^ mask) for i in range(fronts)])
 
-    away, home, leaf_solve, right_here, coupling_here, *node_params = call(
+    k_half = k_rows // 2
+    node_params = (node_gen[0, 0], node_inverse[0, 0], node_lower[0, 0])
+    away, leaf_solve, leaf_skeleton, right_here, coupling_here, *first_params = call(
         leaf_kernel,
         (
             array(part, size),
-            array(part, size),
             array(leaf_size, size),
+            jax.ShapeDtypeStruct((3 * leaf_size, size), bf16),
             array(2, half, leaf_size),
             array(k_rows, leaf_size),
-            array(*node_gen.shape[2:]),
-            array(*node_inverse.shape[2:]),
-            array(*node_lower.shape[2:]),
+            *(array(*value.shape[1:]) for value in node_params),
         ),
         tuple(
             pltpu.with_memory_space_constraint(value, pltpu.HBM)
@@ -295,12 +309,10 @@
                 leaf_inverse[0],
                 leaf_lower[0],
                 coupling[0],
-                node_gen[0, 0],
-                node_inverse[0, 0],
-                node_lower[0, 0],
+                *node_params,
             )
         ),
-        6 * (rows + k_rows + leaf_size) * leaf_size * size,
+        6 * (part + leaf_size) * leaf_size * size,
         in_specs=[hbm] * 8,
         scratch_shapes=[
             pltpu.VMEM((leaf_size, leaf_size), f32),
@@ -309,36 +321,46 @@
             pltpu.SemaphoreType.DMA((9,)),
         ],
     )
-
-    def folds(first, last, *home):
-        maps = jax.ShapeDtypeStruct((last - first, 3 * size, 2 * size), bf16)
-        return call(
-            functools.partial(fold_kernel, first, last),
-            (maps, array(part, 2 * size)) if home else (maps, maps),
-            (*node_params, *home),
-            (last - first) * 6 * 4 * size * size * size,
-            scratch_shapes=[pltpu.VMEM((2 * size, 2 * size), f32)]
-            + [pltpu.VMEM(maps.shape, bf16)] * len(home),
-        )
-
-    home, child_leaf = lax.optimization_barrier((home, child_leaf))
-    other_maps, base = folds(0, 1, home)
+    merge_flops = 6 * half * 2 * size * size
+    fold_flops = 6 * 4 * size * size * size
+    wide = lambda count: jax.ShapeDtypeStruct((count, 3 * size, 2 * size), bf16)
+    both = pltpu.VMEM((2 * size, 2 * size), f32)
+    first_mine, first_other, base, home = call(
+        first_fold_kernel,
+        (wide(1), wide(1), array(half, 2 * size), array(k_half, size)),
+        (*first_params, right_here, coupling_here, leaf_skeleton),
+        fold_flops + 6 * part * (leaf_size + 2 * size) * size,
+        scratch_shapes=[both],
+    )
+    *node_params, away = lax.optimization_barrier((*node_params, away))
     away = blk_swap(away, 1)
-    k_half = k_rows // 2
-    merge_flops = 6 * half * 2 * size * size
-    node, skeleton, carried = call(
-        functools.partial(first_merge_kernel, half),
-        (array(half, size), array(half, size), array(k_half, 2 * size)),
-        (child_leaf, base, away, other_maps),
+    node, skeleton = call(
+        first_merge_kernel,
+        (array(half, size), array(half, size)),
+        (base, away, first_other),
         merge_flops,
-        in_specs=[smem] + [vmem] * 3,
-    )
-    nodes, tails, carried = [node], [carried[:, :size]], carried[:, size:]
+    )
+    nodes, away_first = [node], away
+    child_leaf, skeleton = lax.optimization_barrier((child_leaf, skeleton))
     for tier in range(1, height):
         away = blk_swap(skeleton, 1 << tier)
         after = ()
         if tier == 1:
-            mine_maps, other_maps = folds(1, height)
+            mine_maps, other_maps = call(
+                fold_kernel,
+                (wide(height - 1),) * 2,
+                tuple(node_params),
+                (height - 1) * fold_flops,
+                scratch_shapes=[both],
+            )
+            tail, carried = call(
+                carry_kernel,
+                (array(k_half, size),) * 2,
+                (child_leaf, home, away_first, first_mine, first_other),
+                6 * k_half * 4 * size * size,
+                in_specs=[smem] + [vmem] * 4,
+            )
+            tails = [tail]
         if tier < height - 2:
             both = call(
                 functools.partial(pair_kernel, tier - 1),
@@ -413,9 +435,9 @@
         out_specs=(hbm,) * 3,
         scratch_shapes=[
             pltpu.VMEM((fronts, k_rows, size), f32),
-            pltpu.VMEM((2, half, size), f32),
-            pltpu.VMEM((2, height + 2, half, size), f32),
-            pltpu.SemaphoreType.DMA((2, height + 2)),
+            pltpu.VMEM((rows, size), f32),
+            pltpu.VMEM((4, height + 2, rows // 4, size), f32),
+            pltpu.SemaphoreType.DMA((4, height + 2)),
         ],
     )
     return (leaf_out[None], node_out[None, None], root_out[None])

time: 35 us -> 35.3 us (level); the launches traced: 34.4 us -> 35.2 us
  waiting for transfers between devices: 10.5 us -> 12 us
  starting transfers between devices: 15.5 us -> 14.7 us
    ppermute x3, waiting for transfers between devices: 3.83 us -> 4.9 us  [level_swap(): return lax.ppermute(value, 'level', [(i, i ^ mask) for i in range(fronts)])]
    ppermute x13, starting transfers between devices: 11.9 us -> 11.1 us  [blk_swap(): return lax.ppermute(value, 'blk', [(i, i ^ mask) for i in range(leaves)])]
    ppermute x13, waiting for transfers between devices: 6.65 us -> 7.1 us  [blk_swap(): return lax.ppermute(value, 'blk', [(i, i ^ mask) for i in range(leaves)])]
    pallas_call x14 -> x15, Pallas kernels: 7.06 us -> 7.04 us  [call(): pl.pallas_call(kernel, out_shape=out_shape, in_specs=in_specs or [vmem] *...]
  transfers between devices with their start and end apart: 16 -> 16, of which waited for: 7 -> 7; matrix products, arithmetic and copies ran while one was open for 0% -> 0% of each run, Pallas kernels for 9% -> 10%
where the time goes in v1:
time: 35.3 us; the launch traced here: 35.2 us
  starting transfers between devices  14.7 us (42%)
  waiting for transfers between devices  12 us (34%)
  Pallas kernels  7.04 us (20%)
  between operations  1.45 us (4%)
    ppermute x13, starting transfers between devices, blk_swap(): return lax.ppermute(value, 'blk', [(i, i ^ mask) for i in range(leaves)])  11.1 us
    ppermute x13, waiting for transfers between devices, blk_swap(): return lax.ppermute(value, 'blk', [(i, i ^ mask) for i in range(leaves)])  7.1 us
    pallas_call x15, Pallas kernels, call(): pl.pallas_call(kernel, out_shape=out_shape, in_specs=in_specs or [vmem] *...  7.04 us
    ppermute x3, waiting for transfers between devices, level_swap(): return lax.ppermute(value, 'level', [(i, i ^ mask) for i in range(fronts)])  4.9 us
    ppermute x3, starting transfers between devices, level_swap(): return lax.ppermute(value, 'level', [(i, i ^ mask) for i in range(fronts)])  3.55 us
  transfers between devices with their start and end apart: 16, of which 7 were waited for; matrix products, arithmetic and copies ran while one was open for 0% of the time, Pallas kernels for 10%

profile of v1, /device:TPU:0, one launch (start us, length us, event | category | flops | bytes accessed | tf_op | source)
XLA Modules:
  0.0 35.2 jit_solution(15320030648279783525)
XLA Ops:
  0.6 1.9 %shard_map.112 = (f32[320,128]{1,0:T(8,128)S(1)}, f32[256,128]{1,0:T(8,128)S(1)}, bf16[768,128]{1,0:T(8,128)(2,1)S(1)}, f32[2,256,256]{2,1,0:T(8,128)S(1)}, f32[...) custom-call(f32[512,256]{1,0:T(8,128)} %bitcast.19, ...), custom_call_target="tpu_custom_call" | custom-call | flops 113246208 | bytes 3768320 | tf_op jit(solution)/shard_map/pallas_call | solution.py:43
  2.6 0.6 %collective-permute-start = (f32[320,128]{1,0:T(8,128)S(1)}, f32[320,128]{1,0:T(8,128)S(1)}, u32[]{:S(2)}, u32[]{:S(2)}) collective-permute-start(f32[320,128]{1,0:T(8,128)S(1)} %get-tuple-element.44), channel_id=1, source_target_pairs={{0,1},{1,0},{2,3},{3,2},{4,5},{5,4},{6,7},{7,6},{8,9},{9,8},{10,11... | collective-permute-start | bytes 491528 | tf_op jit(solution)/shard_map/ppermute | solution.py:287
  3.1 0.8 %shard_map.113 = (bf16[1,384,256]{2,1,0:T(8,128)(2,1)S(1)}, bf16[1,384,256]{2,1,0:T(8,128)(2,1)S(1)}, f32[256,256]{1,0:T(8,128)S(1)}, f32[64,128]{1,0:T(8,128)S(1)}) custom-call(f32[256,256]{1,0:T(8,128)S(1)} %get-tuple-element.36.generator, f32[128,128]{1,0:T(8,128)S(1)} %get-tuple-element.37.inverse, f32[128,128]{1,0:T(8,128)S(1)} %get-tuple-element.38.lower, ...), custom_call_target="tpu_custom_call" | custom-call | flops 176160768 | bytes 1933312 | tf_op jit(solution)/shard_map/pallas_call | solution.py:43
  3.9 0.3 collective-permute-done.away
  4.4 3.0 %collective-permute-start.5 = (f32[256,128]{1,0:T(8,128)S(1)}, f32[256,128]{1,0:T(8,128)S(1)}, u32[]{:S(2)}, u32[]{:S(2)}) collective-permute-start(f32[256,128]{1,0:T(8,128)S(1)} %get-tuple-element.61.home), channel_id=1, source_target_pairs={{0,2},{1,3},{2,0},{3,1},{4,6},{5,7},{6,4},{7,5},{8,10},{9,11},{10,... | collective-permute-start | bytes 393224 | tf_op jit(solution)/shard_map/ppermute | solution.py:287
  8.1 0.6 %shard_map.117 = (bf16[2,384,256]{2,1,0:T(8,128)(2,1)S(1)}, bf16[2,384,256]{2,1,0:T(8,128)(2,1)S(1)}) custom-call(f32[3,256,256]{2,1,0:T(8,128)S(1)} %bitcast.13, f32[3,128,128]{2,1,0:T(8,128)S(1)} %bitcast.15, f32[3,128,128]{2,1,0:T(8,128)S(1)} %bitcast.17), custom_call_target="tpu_custom_call" | custom-call | flops 100663296 | bytes 1966080 | tf_op jit(solution)/shard_map/pallas_call | solution.py:43
  9.1 2.6 %collective-permute-start.1 = (f32[64,128]{1,0:T(8,128)S(1)}, f32[64,128]{1,0:T(8,128)S(1)}, u32[]{:S(2)}, u32[]{:S(2)}) collective-permute-start(f32[64,128]{1,0:T(8,128)S(1)} %shard_map.118.climb.refs_0_), channel_id=1, source_target_pairs={{0,4},{1,5},{2,6},{3,7},{4,0},{5,1},{6,2},{7,3},{8,12},{9,13},{10,... | collective-permute-start | bytes 98312 | tf_op jit(solution)/shard_map/ppermute | solution.py:287
  11.9 0.2 shard_map.122
  12.2 2.4 %collective-permute-start.7 = (f32[256,128]{1,0:T(8,128)S(1)}, f32[256,128]{1,0:T(8,128)S(1)}, u32[]{:S(2)}, u32[]{:S(2)}) collective-permute-start(f32[256,128]{1,0:T(8,128)S(1)} %get-tuple-element.63.home), channel_id=1, source_target_pairs={{0,4},{1,5},{2,6},{3,7},{4,0},{5,1},{6,2},{7,3},{8,12},{9,13},{10,... | collective-permute-start | bytes 393224 | tf_op jit(solution)/shard_map/ppermute | solution.py:287
  14.6 1.3 %collective-permute-start.2 = (f32[3,64,128]{2,1,0:T(8,128)S(1)}, f32[3,64,128]{2,1,0:T(8,128)S(1)}, u32[]{:S(2)}, u32[]{:S(2)}) collective-permute-start(f32[3,64,128]{2,1,0:T(8,128)S(1)} %shard_map.119.home), channel_id=1, source_target_pairs={{0,2},{1,3},{2,0},{3,1},{4,6},{5,7},{6,4},{7,5},{8,10},{9,11},{10,... | collective-permute-start | bytes 294920 | tf_op jit(solution)/shard_map/ppermute | solution.py:287
  15.9 0.4 %shard_map.115 = (f32[2,256,128]{2,1,0:T(8,128)S(1)}, f32[128,128]{1,0:T(8,128)S(1)}) custom-call(s32[1]{0:T(128)S(6)} %copy.12.child, f32[2,256,256]{2,1,0:T(8,128)S(1)} %get-tuple-element.39.right, f32[128,256]{1,0:T(8,128)S(1)} %get-tuple-element.40.coupling, f32[256,128]{1,0:T(8,128)S(1)} %get-tuple-element.48.solve_map), custom_call_target="tpu_custom_call" | custom-call | flops 125829120 | bytes 1114116 | tf_op jit(solution)/shard_map/pallas_call | solution.py:43
  16.6 4.7 %collective-permute-done.2.away = f32[3,64,128]{2,1,0:T(8,128)S(1)} collective-permute-done((f32[3,64,128]{2,1,0:T(8,128)S(1)}, f32[3,64,128]{2,1,0:T(8,128)S(1)}, u32[]{:S(2)}, u32[]{:S(2)}) %collective-permute-start.2) | collective-permute-done | bytes 98336 | tf_op jit(solution)/shard_map/ppermute | solution.py:287
  21.3 0.2 shard_map.120.tails.home
  21.5 0.2 shard_map.124
  21.7 2.5 %collective-permute-start.14 = (f32[320,128]{1,0:T(8,128)S(1)}, f32[320,128]{1,0:T(8,128)S(1)}, u32[]{:S(2)}, u32[]{:S(2)}) collective-permute-start(f32[320,128]{1,0:T(8,128)S(1)} %get-tuple-element.65.refs_6_), channel_id=1, source_target_pairs={{0,24},{8,16},{16,8},{24,0},{1,25},{9,17},{17,9},{25,1},{2,26},{10... | collective-permute-start | bytes 491528 | tf_op jit(solution)/shard_map/ppermute | solution.py:290
  24.3 0.5 %collective-permute-start.12 = (f32[320,128]{1,0:T(8,128)S(1)}, f32[320,128]{1,0:T(8,128)S(1)}, u32[]{:S(2)}, u32[]{:S(2)}) collective-permute-start(f32[320,128]{1,0:T(8,128)S(1)} %get-tuple-element.65.refs_6_), channel_id=1, source_target_pairs={{0,16},{8,24},{16,0},{24,8},{1,17},{9,25},{17,1},{25,9},{2,18},{10... | collective-permute-start | bytes 491528 | tf_op jit(solution)/shard_map/ppermute | solution.py:290
  24.8 0.5 %collective-permute-start.10 = (f32[320,128]{1,0:T(8,128)S(1)}, f32[320,128]{1,0:T(8,128)S(1)}, u32[]{:S(2)}, u32[]{:S(2)}) collective-permute-start(f32[320,128]{1,0:T(8,128)S(1)} %get-tuple-element.65.refs_6_), channel_id=1, source_target_pairs={{0,8},{8,0},{16,24},{24,16},{1,9},{9,1},{17,25},{25,17},{2,10},{10... | collective-permute-start | bytes 491528 | tf_op jit(solution)/shard_map/ppermute | solution.py:290
  25.3 0.5 %collective-permute-start.3 = (f32[4,64,128]{2,1,0:T(8,128)S(1)}, f32[4,64,128]{2,1,0:T(8,128)S(1)}, u32[]{:S(2)}, u32[]{:S(2)}) collective-permute-start(f32[4,64,128]{2,1,0:T(8,128)S(1)} %shard_map.120.tails.home), channel_id=1, source_target_pairs={{0,1},{1,0},{2,3},{3,2},{4,5},{5,4},{6,7},{7,6},{8,9},{9,8},{10,11... | collective-permute-start | bytes 393224 | tf_op jit(solution)/shard_map/ppermute | solution.py:287
  25.8 0.8 %collective-permute-done.6.refs_1_.refs_3_ = f32[256,128]{1,0:T(8,128)S(1)} collective-permute-done((f32[256,128]{1,0:T(8,128)S(1)}, f32[256,128]{1,0:T(8,128)S(1)}, u32[]{:S(2)}, u32[]{:S(2)}) %collective-permute-start.6) | collective-permute-done | bytes 131104 | tf_op jit(solution)/shard_map/ppermute | solution.py:287
  26.8 2.4 %collective-permute-done.14.refs_12_ = f32[320,128]{1,0:T(8,128)S(1)} collective-permute-done((f32[320,128]{1,0:T(8,128)S(1)}, f32[320,128]{1,0:T(8,128)S(1)}, u32[]{:S(2)}, u32[]{:S(2)}) %collective-permute-start.14) | collective-permute-done | bytes 163872 | tf_op jit(solution)/shard_map/ppermute | solution.py:290
  29.2 2.5 %collective-permute-done.12.refs_10_ = f32[320,128]{1,0:T(8,128)S(1)} collective-permute-done((f32[320,128]{1,0:T(8,128)S(1)}, f32[320,128]{1,0:T(8,128)S(1)}, u32[]{:S(2)}, u32[]{:S(2)}) %collective-permute-start.12) | collective-permute-done | bytes 163872 | tf_op jit(solution)/shard_map/ppermute | solution.py:290
  31.7 0.5 %collective-permute-start.11 = (f32[320,128]{1,0:T(8,128)S(1)}, f32[320,128]{1,0:T(8,128)S(1)}, u32[]{:S(2)}, u32[]{:S(2)}) collective-permute-start(f32[320,128]{1,0:T(8,128)S(1)} %collective-permute-done.10.refs_8_), channel_id=1, source_target_pairs={{0,1},{1,0},{2,3},{3,2},{4,5},{5,4},{6,7},{7,6},{8,9},{9,8},{10,11... | collective-permute-start | bytes 491528 | tf_op jit(solution)/shard_map/ppermute | solution.py:287
  32.2 1.3 %collective-permute-done.8.refs_2_.refs_5_ = f32[256,128]{1,0:T(8,128)S(1)} collective-permute-done((f32[256,128]{1,0:T(8,128)S(1)}, f32[256,128]{1,0:T(8,128)S(1)}, u32[]{:S(2)}, u32[]{:S(2)}) %collective-permute-start.8) | collective-permute-done | bytes 131104 | tf_op jit(solution)/shard_map/ppermute | solution.py:287
  33.6 1.5 %shard_map.126 = (f32[512,128]{1,0:T(8,128)}, f32[3,512,128]{2,1,0:T(8,128)}, f32[512,128]{1,0:T(8,128)}) custom-call(f32[2,256,128]{2,1,0:T(8,128)S(1)} %get-tuple-element.49.refs_0_.solved, bf16[384,640]{1,0:T(8,128)(2,1)S(1)} %shard_map.125.wide_maps, f32[256,128]{1,0:T(8,128)S(1)} %get-tuple-element.60.refs_0_, ...), custom_call_target="tpu_custom_call" | custom-call | flops 251658240 | bytes 4161536 | tf_op jit(solution)/shard_map/pallas_call | solution.py:43
  (29 shorter events, 1.4 us)
Async XLA Ops:
  2.6 1.6 %collective-permute-start = (f32[320,128]{1,0:T(8,128)S(1)}, f32[320,128]{1,0:T(8,128)S(1)}, u32[]{:S(2)}, u32[]{:S(2)}) collective-permute-start(f32[320,128]{1,0:T(8,128)S(1)} %get-tuple-element.44), channel_id=1, source_target_pairs={{0,1},{1,0},{2,3},{3,2},{4,5},{5,4},{6,7},{7,6},{8,9},{9,8},{10,11... | collective-permute-start | bytes 491528 | tf_op jit(solution)/shard_map/ppermute | solution.py:287
  3.1 4.9 %copy-start = (f32[1,1,3,256,256]{4,3,2,1,0:T(8,128)S(1)}, f32[1,1,3,256,256]{4,3,2,1,0:T(8,128)}, u32[]{:S(2)}) copy-start(f32[1,1,3,256,256]{4,3,2,1,0:T(8,128)} %param.13) | copy-start | bytes 2359300
  4.2 3.9 %copy-start.1 = (f32[1,1,3,128,128]{4,3,2,1,0:T(8,128)S(1)}, f32[1,1,3,128,128]{4,3,2,1,0:T(8,128)}, u32[]{:S(2)}) copy-start(f32[1,1,3,128,128]{4,3,2,1,0:T(8,128)} %param.14) | copy-start | bytes 589828
  4.2 3.9 %copy-start.2 = (f32[1,1,3,128,128]{4,3,2,1,0:T(8,128)S(1)}, f32[1,1,3,128,128]{4,3,2,1,0:T(8,128)}, u32[]{:S(2)}) copy-start(f32[1,1,3,128,128]{4,3,2,1,0:T(8,128)} %param.15) | copy-start | bytes 589828
  4.4 7.5 %collective-permute-start.5 = (f32[256,128]{1,0:T(8,128)S(1)}, f32[256,128]{1,0:T(8,128)S(1)}, u32[]{:S(2)}, u32[]{:S(2)}) collective-permute-start(f32[256,128]{1,0:T(8,128)S(1)} %get-tuple-element.61.home), channel_id=1, source_target_pairs={{0,2},{1,3},{2,0},{3,1},{4,6},{5,7},{6,4},{7,5},{8,10},{9,11},{10,... | collective-permute-start | bytes 393224 | tf_op jit(solution)/shard_map/ppermute | solution.py:287
  9.1 5.5 %collective-permute-start.1 = (f32[64,128]{1,0:T(8,128)S(1)}, f32[64,128]{1,0:T(8,128)S(1)}, u32[]{:S(2)}, u32[]{:S(2)}) collective-permute-start(f32[64,128]{1,0:T(8,128)S(1)} %shard_map.118.climb.refs_0_), channel_id=1, source_target_pairs={{0,4},{1,5},{2,6},{3,7},{4,0},{5,1},{6,2},{7,3},{8,12},{9,13},{10,... | collective-permute-start | bytes 98312 | tf_op jit(solution)/shard_map/ppermute | solution.py:287
  12.2 9.3 %collective-permute-start.7 = (f32[256,128]{1,0:T(8,128)S(1)}, f32[256,128]{1,0:T(8,128)S(1)}, u32[]{:S(2)}, u32[]{:S(2)}) collective-permute-start(f32[256,128]{1,0:T(8,128)S(1)} %get-tuple-element.63.home), channel_id=1, source_target_pairs={{0,4},{1,5},{2,6},{3,7},{4,0},{5,1},{6,2},{7,3},{8,12},{9,13},{10,... | collective-permute-start | bytes 393224 | tf_op jit(solution)/shard_map/ppermute | solution.py:287
  14.6 6.6 %collective-permute-start.2 = (f32[3,64,128]{2,1,0:T(8,128)S(1)}, f32[3,64,128]{2,1,0:T(8,128)S(1)}, u32[]{:S(2)}, u32[]{:S(2)}) collective-permute-start(f32[3,64,128]{2,1,0:T(8,128)S(1)} %shard_map.119.home), channel_id=1, source_target_pairs={{0,2},{1,3},{2,0},{3,1},{4,6},{5,7},{6,4},{7,5},{8,10},{9,11},{10,... | collective-permute-start | bytes 294920 | tf_op jit(solution)/shard_map/ppermute | solution.py:287
  15.9 9.4 %collective-permute-start.4 = (f32[256,128]{1,0:T(8,128)S(1)}, f32[256,128]{1,0:T(8,128)S(1)}, u32[]{:S(2)}, u32[]{:S(2)}) collective-permute-start(f32[256,128]{1,0:T(8,128)S(1)} %get-tuple-element.60.refs_0_), channel_id=1, source_target_pairs={{0,1},{1,0},{2,3},{3,2},{4,5},{5,4},{6,7},{7,6},{8,9},{9,8},{10,11... | collective-permute-start | bytes 393224 | tf_op jit(solution)/shard_map/ppermute | solution.py:287
  21.7 7.4 %collective-permute-start.14 = (f32[320,128]{1,0:T(8,128)S(1)}, f32[320,128]{1,0:T(8,128)S(1)}, u32[]{:S(2)}, u32[]{:S(2)}) collective-permute-start(f32[320,128]{1,0:T(8,128)S(1)} %get-tuple-element.65.refs_6_), channel_id=1, source_target_pairs={{0,24},{8,16},{16,8},{24,0},{1,25},{9,17},{17,9},{25,1},{2,26},{10... | collective-permute-start | bytes 491528 | tf_op jit(solution)/shard_map/ppermute | solution.py:290
  24.3 7.4 %collective-permute-start.12 = (f32[320,128]{1,0:T(8,128)S(1)}, f32[320,128]{1,0:T(8,128)S(1)}, u32[]{:S(2)}, u32[]{:S(2)}) collective-permute-start(f32[320,128]{1,0:T(8,128)S(1)} %get-tuple-element.65.refs_6_), channel_id=1, source_target_pairs={{0,16},{8,24},{16,0},{24,8},{1,17},{9,25},{17,1},{25,9},{2,18},{10... | collective-permute-start | bytes 491528 | tf_op jit(solution)/shard_map/ppermute | solution.py:290
  24.8 6.9 %collective-permute-start.10 = (f32[320,128]{1,0:T(8,128)S(1)}, f32[320,128]{1,0:T(8,128)S(1)}, u32[]{:S(2)}, u32[]{:S(2)}) collective-permute-start(f32[320,128]{1,0:T(8,128)S(1)} %get-tuple-element.65.refs_6_), channel_id=1, source_target_pairs={{0,8},{8,0},{16,24},{24,16},{1,9},{9,1},{17,25},{25,17},{2,10},{10... | collective-permute-start | bytes 491528 | tf_op jit(solution)/shard_map/ppermute | solution.py:290
  25.3 1.3 %collective-permute-start.6 = (f32[256,128]{1,0:T(8,128)S(1)}, f32[256,128]{1,0:T(8,128)S(1)}, u32[]{:S(2)}, u32[]{:S(2)}) collective-permute-start(f32[256,128]{1,0:T(8,128)S(1)} %get-tuple-element.62.refs_2_), channel_id=1, source_target_pairs={{0,1},{1,0},{2,3},{3,2},{4,5},{5,4},{6,7},{7,6},{8,9},{9,8},{10,11... | collective-permute-start | bytes 393224 | tf_op jit(solution)/shard_map/ppermute | solution.py:287
  25.3 6.9 %collective-permute-start.3 = (f32[4,64,128]{2,1,0:T(8,128)S(1)}, f32[4,64,128]{2,1,0:T(8,128)S(1)}, u32[]{:S(2)}, u32[]{:S(2)}) collective-permute-start(f32[4,64,128]{2,1,0:T(8,128)S(1)} %shard_map.120.tails.home), channel_id=1, source_target_pairs={{0,1},{1,0},{2,3},{3,2},{4,5},{5,4},{6,7},{7,6},{8,9},{9,8},{10,11... | collective-permute-start | bytes 393224 | tf_op jit(solution)/shard_map/ppermute | solution.py:287
  26.6 6.9 %collective-permute-start.9 = (f32[320,128]{1,0:T(8,128)S(1)}, f32[320,128]{1,0:T(8,128)S(1)}, u32[]{:S(2)}, u32[]{:S(2)}) collective-permute-start(f32[320,128]{1,0:T(8,128)S(1)} %get-tuple-element.65.refs_6_), channel_id=1, source_target_pairs={{0,1},{1,0},{2,3},{3,2},{4,5},{5,4},{6,7},{7,6},{8,9},{9,8},{10,11... | collective-permute-start | bytes 491528 | tf_op jit(solution)/shard_map/ppermute | solution.py:287
  29.2 4.4 %collective-permute-start.15 = (f32[320,128]{1,0:T(8,128)S(1)}, f32[320,128]{1,0:T(8,128)S(1)}, u32[]{:S(2)}, u32[]{:S(2)}) collective-permute-start(f32[320,128]{1,0:T(8,128)S(1)} %collective-permute-done.14.refs_12_), channel_id=1, source_target_pairs={{0,1},{1,0},{2,3},{3,2},{4,5},{5,4},{6,7},{7,6},{8,9},{9,8},{10,11... | collective-permute-start | bytes 491528 | tf_op jit(solution)/shard_map/ppermute | solution.py:287
  31.6 2.0 %collective-permute-start.13 = (f32[320,128]{1,0:T(8,128)S(1)}, f32[320,128]{1,0:T(8,128)S(1)}, u32[]{:S(2)}, u32[]{:S(2)}) collective-permute-start(f32[320,128]{1,0:T(8,128)S(1)} %collective-permute-done.12.refs_10_), channel_id=1, source_target_pairs={{0,1},{1,0},{2,3},{3,2},{4,5},{5,4},{6,7},{7,6},{8,9},{9,8},{10,11... | collective-permute-start | bytes 491528 | tf_op jit(solution)/shard_map/ppermute | solution.py:287
  31.7 1.9 %collective-permute-start.11 = (f32[320,128]{1,0:T(8,128)S(1)}, f32[320,128]{1,0:T(8,128)S(1)}, u32[]{:S(2)}, u32[]{:S(2)}) collective-permute-start(f32[320,128]{1,0:T(8,128)S(1)} %collective-permute-done.10.refs_8_), channel_id=1, source_target_pairs={{0,1},{1,0},{2,3},{3,2},{4,5},{5,4},{6,7},{7,6},{8,9},{9,8},{10,11... | collective-permute-start | bytes 491528 | tf_op jit(solution)/shard_map/ppermute | solution.py:287
  32.1 1.3 %collective-permute-start.8 = (f32[256,128]{1,0:T(8,128)S(1)}, f32[256,128]{1,0:T(8,128)S(1)}, u32[]{:S(2)}, u32[]{:S(2)}) collective-permute-start(f32[256,128]{1,0:T(8,128)S(1)} %get-tuple-element.64.refs_4_), channel_id=1, source_target_pairs={{0,1},{1,0},{2,3},{3,2},{4,5},{5,4},{6,7},{7,6},{8,9},{9,8},{10,11... | collective-permute-start | bytes 393224 | tf_op jit(solution)/shard_map/ppermute | solution.py:287

commit v2 on v1

--- a/solution.py
+++ b/solution.py
@@ -162,9 +162,9 @@
     climb[...] = wide_dot(wide_left(carried[...]), mine_maps[index, :, size:])
 
 
-def relay_kernel(carried, climb, far, out):
-    for i, value in enumerate((carried, climb, far)):
-        out[i] = value[...]
+def relay_kernel(carried, far, out):
+    out[0] = carried[...]
+    out[1] = far[...]
 
 
 def pair_kernel(index, home, away, mine_maps, other_maps, out):
@@ -177,11 +177,12 @@
     size = tails.shape[2]
     count = tails.shape[0]
     out[:count] = tails[...]
-    out[count] = wide_dot(wide_left(home[0]), mine_maps[index, :, :size]) + wide_dot(
-        wide_left(away[0]), other_maps[index, :, :size]
-    )
-    both = wide_dot(wide_left(home[1] + away[1]), mine_maps[index + 1]) + wide_dot(
-        wide_left(home[2] + away[2]), other_maps[index + 1]
+    both = wide_dot(wide_left(home[0]), mine_maps[index]) + wide_dot(
+        wide_left(away[0]), other_maps[index]
+    )
+    out[count] = both[:, :size]
+    both = wide_dot(wide_left(both[:, size:]), mine_maps[index + 1]) + wide_dot(
+        wide_left(home[1] + away[1]), other_maps[index + 1]
     )
     out[count + 1] = both[:, :size]
     out[count + 2] = both[:, size:]
@@ -380,7 +381,7 @@
             far = blk_swap(climb, 2 << tier)
             after = (climb,)
         if tier == height - 1:
-            relay = call(relay_kernel, array(3, k_half, size), (carried, climb, far), k_half * size)
+            relay = call(relay_kernel, array(2, k_half, size), (carried, far), k_half * size)
             relayed = blk_swap(relay, 1 << (tier - 1))
             tails = call(
                 functools.partial(top_kernel, tier - 2),

time: 35.3 us -> 39.1 us (1.11)
  waiting for transfers between devices: 12 us -> 18.5 us
  starting transfers between devices: 14.7 us -> 11.9 us
    ppermute x13, waiting for transfers between devices: 7.1 us -> 14.8 us  [blk_swap(): return lax.ppermute(value, 'blk', [(i, i ^ mask) for i in range(leaves)])]
    ppermute x13, starting transfers between devices: 11.1 us -> 8.34 us  [blk_swap(): return lax.ppermute(value, 'blk', [(i, i ^ mask) for i in range(leaves)])]
    ppermute x3, waiting for transfers between devices: 4.9 us -> 3.7 us  [level_swap(): return lax.ppermute(value, 'level', [(i, i ^ mask) for i in range(fronts)])]
  transfers between devices with their start and end apart: 16 -> 16, of which waited for: 7 -> 8; matrix products, arithmetic and copies ran while one was open for 0% -> 0% of each run, Pallas kernels for 10% -> 8%
where the time goes in v2:
time: 39.1 us; the launch traced here: 39 us
  waiting for transfers between devices  18.5 us (47%)
  starting transfers between devices  11.9 us (30%)
  Pallas kernels  7.16 us (18%)
  between operations  1.44 us (4%)
    ppermute x13, waiting for transfers between devices, blk_swap(): return lax.ppermute(value, 'blk', [(i, i ^ mask) for i in range(leaves)])  14.8 us
    ppermute x13, starting transfers between devices, blk_swap(): return lax.ppermute(value, 'blk', [(i, i ^ mask) for i in range(leaves)])  8.34 us
    pallas_call x15, Pallas kernels, call(): pl.pallas_call(kernel, out_shape=out_shape, in_specs=in_specs or [vmem] *...  7.16 us
    ppermute x3, waiting for transfers between devices, level_swap(): return lax.ppermute(value, 'level', [(i, i ^ mask) for i in range(fronts)])  3.7 us
    ppermute x3, starting transfers between devices, level_swap(): return lax.ppermute(value, 'level', [(i, i ^ mask) for i in range(fronts)])  3.55 us
  transfers between devices with their start and end apart: 16, of which 8 were waited for; matrix products, arithmetic and copies ran while one was open for 0% of the time, Pallas kernels for 8%

profile of v2, /device:TPU:0, one launch (start us, length us, event | category | flops | bytes accessed | tf_op | source)
XLA Modules:
  0.0 39.0 jit_solution(12227082200408425978)
XLA Ops:
  0.6 1.9 %shard_map.112 = (f32[320,128]{1,0:T(8,128)S(1)}, f32[256,128]{1,0:T(8,128)S(1)}, bf16[768,128]{1,0:T(8,128)(2,1)S(1)}, f32[2,256,256]{2,1,0:T(8,128)S(1)}, f32[...) custom-call(f32[512,256]{1,0:T(8,128)} %bitcast.19, ...), custom_call_target="tpu_custom_call" | custom-call | flops 113246208 | bytes 3768320 | tf_op jit(solution)/shard_map/pallas_call | solution.py:43
  2.6 0.6 %collective-permute-start = (f32[320,128]{1,0:T(8,128)S(1)}, f32[320,128]{1,0:T(8,128)S(1)}, u32[]{:S(2)}, u32[]{:S(2)}) collective-permute-start(f32[320,128]{1,0:T(8,128)S(1)} %get-tuple-element.44), channel_id=1, source_target_pairs={{0,1},{1,0},{2,3},{3,2},{4,5},{5,4},{6,7},{7,6},{8,9},{9,8},{10,11... | collective-permute-start | bytes 491528 | tf_op jit(solution)/shard_map/ppermute | solution.py:288
  3.1 0.8 %shard_map.113 = (bf16[1,384,256]{2,1,0:T(8,128)(2,1)S(1)}, bf16[1,384,256]{2,1,0:T(8,128)(2,1)S(1)}, f32[256,256]{1,0:T(8,128)S(1)}, f32[64,128]{1,0:T(8,128)S(1)}) custom-call(f32[256,256]{1,0:T(8,128)S(1)} %get-tuple-element.36.generator, f32[128,128]{1,0:T(8,128)S(1)} %get-tuple-element.37.inverse, f32[128,128]{1,0:T(8,128)S(1)} %get-tuple-element.38.lower, ...), custom_call_target="tpu_custom_call" | custom-call | flops 176160768 | bytes 1933312 | tf_op jit(solution)/shard_map/pallas_call | solution.py:43
  3.9 0.3 collective-permute-done.away
  4.4 3.0 %collective-permute-start.5 = (f32[256,128]{1,0:T(8,128)S(1)}, f32[256,128]{1,0:T(8,128)S(1)}, u32[]{:S(2)}, u32[]{:S(2)}) collective-permute-start(f32[256,128]{1,0:T(8,128)S(1)} %get-tuple-element.61.home), channel_id=1, source_target_pairs={{0,2},{1,3},{2,0},{3,1},{4,6},{5,7},{6,4},{7,5},{8,10},{9,11},{10,... | collective-permute-start | bytes 393224 | tf_op jit(solution)/shard_map/ppermute | solution.py:288
  8.1 0.6 %shard_map.117 = (bf16[2,384,256]{2,1,0:T(8,128)(2,1)S(1)}, bf16[2,384,256]{2,1,0:T(8,128)(2,1)S(1)}) custom-call(f32[3,256,256]{2,1,0:T(8,128)S(1)} %bitcast.13, f32[3,128,128]{2,1,0:T(8,128)S(1)} %bitcast.15, f32[3,128,128]{2,1,0:T(8,128)S(1)} %bitcast.17), custom_call_target="tpu_custom_call" | custom-call | flops 100663296 | bytes 1966080 | tf_op jit(solution)/shard_map/pallas_call | solution.py:43
  9.3 1.9 %collective-permute-done.5.away = f32[256,128]{1,0:T(8,128)S(1)} collective-permute-done((f32[256,128]{1,0:T(8,128)S(1)}, f32[256,128]{1,0:T(8,128)S(1)}, u32[]{:S(2)}, u32[]{:S(2)}) %collective-permute-start.5) | collective-permute-done | bytes 131104 | tf_op jit(solution)/shard_map/ppermute | solution.py:288
  11.4 2.8 %collective-permute-start.7 = (f32[256,128]{1,0:T(8,128)S(1)}, f32[256,128]{1,0:T(8,128)S(1)}, u32[]{:S(2)}, u32[]{:S(2)}) collective-permute-start(f32[256,128]{1,0:T(8,128)S(1)} %get-tuple-element.63.home), channel_id=1, source_target_pairs={{0,4},{1,5},{2,6},{3,7},{4,0},{5,1},{6,2},{7,3},{8,12},{9,13},{10,... | collective-permute-start | bytes 393224 | tf_op jit(solution)/shard_map/ppermute | solution.py:288
  14.4 7.2 %collective-permute-done.1.far = f32[64,128]{1,0:T(8,128)S(1)} collective-permute-done((f32[64,128]{1,0:T(8,128)S(1)}, f32[64,128]{1,0:T(8,128)S(1)}, u32[]{:S(2)}, u32[]{:S(2)}) %collective-permute-start.1) | collective-permute-done | bytes 32800 | tf_op jit(solution)/shard_map/ppermute | solution.py:288
  21.6 0.5 %collective-permute-start.2 = (f32[2,64,128]{2,1,0:T(8,128)S(1)}, f32[2,64,128]{2,1,0:T(8,128)S(1)}, u32[]{:S(2)}, u32[]{:S(2)}) collective-permute-start(f32[2,64,128]{2,1,0:T(8,128)S(1)} %shard_map.119.home), channel_id=1, source_target_pairs={{0,2},{1,3},{2,0},{3,1},{4,6},{5,7},{6,4},{7,5},{8,10},{9,11},{10,... | collective-permute-start | bytes 196616 | tf_op jit(solution)/shard_map/ppermute | solution.py:288
  22.1 0.4 %shard_map.115 = (f32[2,256,128]{2,1,0:T(8,128)S(1)}, f32[128,128]{1,0:T(8,128)S(1)}) custom-call(s32[1]{0:T(128)S(6)} %copy.12.child, f32[2,256,256]{2,1,0:T(8,128)S(1)} %get-tuple-element.39.right, f32[128,256]{1,0:T(8,128)S(1)} %get-tuple-element.40.coupling, f32[256,128]{1,0:T(8,128)S(1)} %get-tuple-element.48.solve_map), custom_call_target="tpu_custom_call" | custom-call | flops 125829120 | bytes 1114116 | tf_op jit(solution)/shard_map/pallas_call | solution.py:43
  22.6 3.3 %collective-permute-done.2.away = f32[2,64,128]{2,1,0:T(8,128)S(1)} collective-permute-done((f32[2,64,128]{2,1,0:T(8,128)S(1)}, f32[2,64,128]{2,1,0:T(8,128)S(1)}, u32[]{:S(2)}, u32[]{:S(2)}) %collective-permute-start.2) | collective-permute-done | bytes 65568 | tf_op jit(solution)/shard_map/ppermute | solution.py:288
  25.9 0.4 shard_map.120.tails.home
  26.2 0.2 shard_map.123.base
  26.7 2.4 %collective-permute-start.14 = (f32[320,128]{1,0:T(8,128)S(1)}, f32[320,128]{1,0:T(8,128)S(1)}, u32[]{:S(2)}, u32[]{:S(2)}) collective-permute-start(f32[320,128]{1,0:T(8,128)S(1)} %get-tuple-element.65.refs_6_), channel_id=1, source_target_pairs={{0,24},{8,16},{16,8},{24,0},{1,25},{9,17},{17,9},{25,1},{2,26},{10... | collective-permute-start | bytes 491528 | tf_op jit(solution)/shard_map/ppermute | solution.py:291
  29.1 0.5 %collective-permute-start.12 = (f32[320,128]{1,0:T(8,128)S(1)}, f32[320,128]{1,0:T(8,128)S(1)}, u32[]{:S(2)}, u32[]{:S(2)}) collective-permute-start(f32[320,128]{1,0:T(8,128)S(1)} %get-tuple-element.65.refs_6_), channel_id=1, source_target_pairs={{0,16},{8,24},{16,0},{24,8},{1,17},{9,25},{17,1},{25,9},{2,18},{10... | collective-permute-start | bytes 491528 | tf_op jit(solution)/shard_map/ppermute | solution.py:291
  29.6 0.7 %collective-permute-start.10 = (f32[320,128]{1,0:T(8,128)S(1)}, f32[320,128]{1,0:T(8,128)S(1)}, u32[]{:S(2)}, u32[]{:S(2)}) collective-permute-start(f32[320,128]{1,0:T(8,128)S(1)} %get-tuple-element.65.refs_6_), channel_id=1, source_target_pairs={{0,8},{8,0},{16,24},{24,16},{1,9},{9,1},{17,25},{25,17},{2,10},{10... | collective-permute-start | bytes 491528 | tf_op jit(solution)/shard_map/ppermute | solution.py:291
  30.3 0.5 %collective-permute-start.6 = (f32[256,128]{1,0:T(8,128)S(1)}, f32[256,128]{1,0:T(8,128)S(1)}, u32[]{:S(2)}, u32[]{:S(2)}) collective-permute-start(f32[256,128]{1,0:T(8,128)S(1)} %get-tuple-element.62.refs_2_), channel_id=1, source_target_pairs={{0,1},{1,0},{2,3},{3,2},{4,5},{5,4},{6,7},{7,6},{8,9},{9,8},{10,11... | collective-permute-start | bytes 393224 | tf_op jit(solution)/shard_map/ppermute | solution.py:288
  30.8 0.8 %collective-permute-done.3.away = f32[4,64,128]{2,1,0:T(8,128)S(1)} collective-permute-done((f32[4,64,128]{2,1,0:T(8,128)S(1)}, f32[4,64,128]{2,1,0:T(8,128)S(1)}, u32[]{:S(2)}, u32[]{:S(2)}) %collective-permute-start.3) | collective-permute-done | bytes 131104 | tf_op jit(solution)/shard_map/ppermute | solution.py:288
  31.7 2.3 %collective-permute-done.14.refs_12_ = f32[320,128]{1,0:T(8,128)S(1)} collective-permute-done((f32[320,128]{1,0:T(8,128)S(1)}, f32[320,128]{1,0:T(8,128)S(1)}, u32[]{:S(2)}, u32[]{:S(2)}) %collective-permute-start.14) | collective-permute-done | bytes 163872 | tf_op jit(solution)/shard_map/ppermute | solution.py:291
  34.1 1.4 %collective-permute-done.12.refs_10_ = f32[320,128]{1,0:T(8,128)S(1)} collective-permute-done((f32[320,128]{1,0:T(8,128)S(1)}, f32[320,128]{1,0:T(8,128)S(1)}, u32[]{:S(2)}, u32[]{:S(2)}) %collective-permute-start.12) | collective-permute-done | bytes 163872 | tf_op jit(solution)/shard_map/ppermute | solution.py:291
  35.5 0.5 %collective-permute-start.11 = (f32[320,128]{1,0:T(8,128)S(1)}, f32[320,128]{1,0:T(8,128)S(1)}, u32[]{:S(2)}, u32[]{:S(2)}) collective-permute-start(f32[320,128]{1,0:T(8,128)S(1)} %collective-permute-done.10.refs_8_), channel_id=1, source_target_pairs={{0,1},{1,0},{2,3},{3,2},{4,5},{5,4},{6,7},{7,6},{8,9},{9,8},{10,11... | collective-permute-start | bytes 491528 | tf_op jit(solution)/shard_map/ppermute | solution.py:288
  36.0 1.3 %collective-permute-done.8.refs_2_.refs_5_ = f32[256,128]{1,0:T(8,128)S(1)} collective-permute-done((f32[256,128]{1,0:T(8,128)S(1)}, f32[256,128]{1,0:T(8,128)S(1)}, u32[]{:S(2)}, u32[]{:S(2)}) %collective-permute-start.8) | collective-permute-done | bytes 131104 | tf_op jit(solution)/shard_map/ppermute | solution.py:288
  37.5 1.5 %shard_map.126 = (f32[512,128]{1,0:T(8,128)}, f32[3,512,128]{2,1,0:T(8,128)}, f32[512,128]{1,0:T(8,128)}) custom-call(f32[2,256,128]{2,1,0:T(8,128)S(1)} %get-tuple-element.49.refs_0_.solved, bf16[384,640]{1,0:T(8,128)(2,1)S(1)} %shard_map.125.wide_maps, f32[256,128]{1,0:T(8,128)S(1)} %get-tuple-element.60.refs_0_, ...), custom_call_target="tpu_custom_call" | custom-call | flops 251658240 | bytes 4161536 | tf_op jit(solution)/shard_map/pallas_call | solution.py:43
  (29 shorter events, 1.8 us)
Async XLA Ops:
  2.6 1.6 %collective-permute-start = (f32[320,128]{1,0:T(8,128)S(1)}, f32[320,128]{1,0:T(8,128)S(1)}, u32[]{:S(2)}, u32[]{:S(2)}) collective-permute-start(f32[320,128]{1,0:T(8,128)S(1)} %get-tuple-element.44), channel_id=1, source_target_pairs={{0,1},{1,0},{2,3},{3,2},{4,5},{5,4},{6,7},{7,6},{8,9},{9,8},{10,11... | collective-permute-start | bytes 491528 | tf_op jit(solution)/shard_map/ppermute | solution.py:288
  3.1 4.9 %copy-start = (f32[1,1,3,256,256]{4,3,2,1,0:T(8,128)S(1)}, f32[1,1,3,256,256]{4,3,2,1,0:T(8,128)}, u32[]{:S(2)}) copy-start(f32[1,1,3,256,256]{4,3,2,1,0:T(8,128)} %param.13) | copy-start | bytes 2359300
  4.2 3.9 %copy-start.1 = (f32[1,1,3,128,128]{4,3,2,1,0:T(8,128)S(1)}, f32[1,1,3,128,128]{4,3,2,1,0:T(8,128)}, u32[]{:S(2)}) copy-start(f32[1,1,3,128,128]{4,3,2,1,0:T(8,128)} %param.14) | copy-start | bytes 589828
  4.2 3.9 %copy-start.2 = (f32[1,1,3,128,128]{4,3,2,1,0:T(8,128)S(1)}, f32[1,1,3,128,128]{4,3,2,1,0:T(8,128)}, u32[]{:S(2)}) copy-start(f32[1,1,3,128,128]{4,3,2,1,0:T(8,128)} %param.15) | copy-start | bytes 589828
  4.4 6.8 %collective-permute-start.5 = (f32[256,128]{1,0:T(8,128)S(1)}, f32[256,128]{1,0:T(8,128)S(1)}, u32[]{:S(2)}, u32[]{:S(2)}) collective-permute-start(f32[256,128]{1,0:T(8,128)S(1)} %get-tuple-element.61.home), channel_id=1, source_target_pairs={{0,2},{1,3},{2,0},{3,1},{4,6},{5,7},{6,4},{7,5},{8,10},{9,11},{10,... | collective-permute-start | bytes 393224 | tf_op jit(solution)/shard_map/ppermute | solution.py:288
  11.4 15.0 %collective-permute-start.7 = (f32[256,128]{1,0:T(8,128)S(1)}, f32[256,128]{1,0:T(8,128)S(1)}, u32[]{:S(2)}, u32[]{:S(2)}) collective-permute-start(f32[256,128]{1,0:T(8,128)S(1)} %get-tuple-element.63.home), channel_id=1, source_target_pairs={{0,4},{1,5},{2,6},{3,7},{4,0},{5,1},{6,2},{7,3},{8,12},{9,13},{10,... | collective-permute-start | bytes 393224 | tf_op jit(solution)/shard_map/ppermute | solution.py:288
  14.2 7.3 %collective-permute-start.1 = (f32[64,128]{1,0:T(8,128)S(1)}, f32[64,128]{1,0:T(8,128)S(1)}, u32[]{:S(2)}, u32[]{:S(2)}) collective-permute-start(f32[64,128]{1,0:T(8,128)S(1)} %shard_map.118.refs_0_), channel_id=1, source_target_pairs={{0,4},{1,5},{2,6},{3,7},{4,0},{5,1},{6,2},{7,3},{8,12},{9,13},{10,... | collective-permute-start | bytes 98312 | tf_op jit(solution)/shard_map/ppermute | solution.py:288
  21.6 4.3 %collective-permute-start.2 = (f32[2,64,128]{2,1,0:T(8,128)S(1)}, f32[2,64,128]{2,1,0:T(8,128)S(1)}, u32[]{:S(2)}, u32[]{:S(2)}) collective-permute-start(f32[2,64,128]{2,1,0:T(8,128)S(1)} %shard_map.119.home), channel_id=1, source_target_pairs={{0,2},{1,3},{2,0},{3,1},{4,6},{5,7},{6,4},{7,5},{8,10},{9,11},{10,... | collective-permute-start | bytes 196616 | tf_op jit(solution)/shard_map/ppermute | solution.py:288
  22.1 8.1 %collective-permute-start.4 = (f32[256,128]{1,0:T(8,128)S(1)}, f32[256,128]{1,0:T(8,128)S(1)}, u32[]{:S(2)}, u32[]{:S(2)}) collective-permute-start(f32[256,128]{1,0:T(8,128)S(1)} %get-tuple-element.60.refs_0_), channel_id=1, source_target_pairs={{0,1},{1,0},{2,3},{3,2},{4,5},{5,4},{6,7},{7,6},{8,9},{9,8},{10,11... | collective-permute-start | bytes 393224 | tf_op jit(solution)/shard_map/ppermute | solution.py:288
  26.7 7.4 %collective-permute-start.14 = (f32[320,128]{1,0:T(8,128)S(1)}, f32[320,128]{1,0:T(8,128)S(1)}, u32[]{:S(2)}, u32[]{:S(2)}) collective-permute-start(f32[320,128]{1,0:T(8,128)S(1)} %get-tuple-element.65.refs_6_), channel_id=1, source_target_pairs={{0,24},{8,16},{16,8},{24,0},{1,25},{9,17},{17,9},{25,1},{2,26},{10... | collective-permute-start | bytes 491528 | tf_op jit(solution)/shard_map/ppermute | solution.py:291
  29.1 6.4 %collective-permute-start.12 = (f32[320,128]{1,0:T(8,128)S(1)}, f32[320,128]{1,0:T(8,128)S(1)}, u32[]{:S(2)}, u32[]{:S(2)}) collective-permute-start(f32[320,128]{1,0:T(8,128)S(1)} %get-tuple-element.65.refs_6_), channel_id=1, source_target_pairs={{0,16},{8,24},{16,0},{24,8},{1,17},{9,25},{17,1},{25,9},{2,18},{10... | collective-permute-start | bytes 491528 | tf_op jit(solution)/shard_map/ppermute | solution.py:291
  29.6 5.9 %collective-permute-start.10 = (f32[320,128]{1,0:T(8,128)S(1)}, f32[320,128]{1,0:T(8,128)S(1)}, u32[]{:S(2)}, u32[]{:S(2)}) collective-permute-start(f32[320,128]{1,0:T(8,128)S(1)} %get-tuple-element.65.refs_6_), channel_id=1, source_target_pairs={{0,8},{8,0},{16,24},{24,16},{1,9},{9,1},{17,25},{25,17},{2,10},{10... | collective-permute-start | bytes 491528 | tf_op jit(solution)/shard_map/ppermute | solution.py:291
  30.2 1.3 %collective-permute-start.3 = (f32[4,64,128]{2,1,0:T(8,128)S(1)}, f32[4,64,128]{2,1,0:T(8,128)S(1)}, u32[]{:S(2)}, u32[]{:S(2)}) collective-permute-start(f32[4,64,128]{2,1,0:T(8,128)S(1)} %shard_map.120.tails.home), channel_id=1, source_target_pairs={{0,1},{1,0},{2,3},{3,2},{4,5},{5,4},{6,7},{7,6},{8,9},{9,8},{10,11... | collective-permute-start | bytes 393224 | tf_op jit(solution)/shard_map/ppermute | solution.py:288
  30.3 5.7 %collective-permute-start.6 = (f32[256,128]{1,0:T(8,128)S(1)}, f32[256,128]{1,0:T(8,128)S(1)}, u32[]{:S(2)}, u32[]{:S(2)}) collective-permute-start(f32[256,128]{1,0:T(8,128)S(1)} %get-tuple-element.62.refs_2_), channel_id=1, source_target_pairs={{0,1},{1,0},{2,3},{3,2},{4,5},{5,4},{6,7},{7,6},{8,9},{9,8},{10,11... | collective-permute-start | bytes 393224 | tf_op jit(solution)/shard_map/ppermute | solution.py:288
  31.6 5.7 %collective-permute-start.9 = (f32[320,128]{1,0:T(8,128)S(1)}, f32[320,128]{1,0:T(8,128)S(1)}, u32[]{:S(2)}, u32[]{:S(2)}) collective-permute-start(f32[320,128]{1,0:T(8,128)S(1)} %get-tuple-element.65.refs_6_), channel_id=1, source_target_pairs={{0,1},{1,0},{2,3},{3,2},{4,5},{5,4},{6,7},{7,6},{8,9},{9,8},{10,11... | collective-permute-start | bytes 491528 | tf_op jit(solution)/shard_map/ppermute | solution.py:288
  34.1 3.4 %collective-permute-start.15 = (f32[320,128]{1,0:T(8,128)S(1)}, f32[320,128]{1,0:T(8,128)S(1)}, u32[]{:S(2)}, u32[]{:S(2)}) collective-permute-start(f32[320,128]{1,0:T(8,128)S(1)} %collective-permute-done.14.refs_12_), channel_id=1, source_target_pairs={{0,1},{1,0},{2,3},{3,2},{4,5},{5,4},{6,7},{7,6},{8,9},{9,8},{10,11... | collective-permute-start | bytes 491528 | tf_op jit(solution)/shard_map/ppermute | solution.py:288
  35.5 2.0 %collective-permute-start.13 = (f32[320,128]{1,0:T(8,128)S(1)}, f32[320,128]{1,0:T(8,128)S(1)}, u32[]{:S(2)}, u32[]{:S(2)}) collective-permute-start(f32[320,128]{1,0:T(8,128)S(1)} %collective-permute-done.12.refs_10_), channel_id=1, source_target_pairs={{0,1},{1,0},{2,3},{3,2},{4,5},{5,4},{6,7},{7,6},{8,9},{9,8},{10,11... | collective-permute-start | bytes 491528 | tf_op jit(solution)/shard_map/ppermute | solution.py:288
  35.5 2.0 %collective-permute-start.11 = (f32[320,128]{1,0:T(8,128)S(1)}, f32[320,128]{1,0:T(8,128)S(1)}, u32[]{:S(2)}, u32[]{:S(2)}) collective-permute-start(f32[320,128]{1,0:T(8,128)S(1)} %collective-permute-done.10.refs_8_), channel_id=1, source_target_pairs={{0,1},{1,0},{2,3},{3,2},{4,5},{5,4},{6,7},{7,6},{8,9},{9,8},{10,11... | collective-permute-start | bytes 491528 | tf_op jit(solution)/shard_map/ppermute | solution.py:288
  36.0 1.3 %collective-permute-start.8 = (f32[256,128]{1,0:T(8,128)S(1)}, f32[256,128]{1,0:T(8,128)S(1)}, u32[]{:S(2)}, u32[]{:S(2)}) collective-permute-start(f32[256,128]{1,0:T(8,128)S(1)} %get-tuple-element.64.refs_4_), channel_id=1, source_target_pairs={{0,1},{1,0},{2,3},{3,2},{4,5},{5,4},{6,7},{7,6},{8,9},{9,8},{10,11... | collective-permute-start | bytes 393224 | tf_op jit(solution)/shard_map/ppermute | solution.py:288

commit v3 on v2

--- a/solution.py
+++ b/solution.py
@@ -121,11 +121,11 @@
     base[...] = wide_dot(wide_left(value), mine_maps[0])
 
 
-def fold_kernel(generator, inverse, lower, mine_maps, other_maps, both):
-    for tier in range(1, generator.shape[0]):
-        mine_maps[tier - 1], other_maps[tier - 1] = fold(
-            tier, generator[tier], inverse[tier], lower[tier], both
-        )
+def fold_kernel(first, generator, inverse, lower, *refs):
+    mine_maps, other_maps, both = refs[-3:]
+    for i in range(mine_maps.shape[0]):
+        tier = first + i
+        mine_maps[i], other_maps[i] = fold(tier, generator[tier], inverse[tier], lower[tier], both)
 
 
 def base_kernel(index, home, mine_maps, base):
@@ -147,7 +147,7 @@
     node[...] = both[:, :size]
 
 
-def carry_kernel(child, home, away, mine_maps, other_maps, tail, carried):
+def carry_kernel(child, home, away, mine_maps, other_maps, next_maps, tail, carried, *climb):
     k_half, size = home.shape
     position = lax.axis_index("blk")
     mine = wide_dot(wide_left(home[...]), mine_maps[0])
@@ -155,6 +155,8 @@
     both = jnp.where(position == child[0], mine, 0.0) + jnp.where(position ^ 1 == child[0], other, 0.0)
     tail[...] = both[:, :size]
     carried[...] = both[:, size:]
+    for out in climb:
+        out[...] = wide_dot(wide_left(both[:, size:]), next_maps[0, :, size:])
 
 
 def climb_kernel(index, carried, mine_maps, climb):
@@ -173,7 +175,7 @@
     )
 
 
-def top_kernel(index, tails, home, away, mine_maps, other_maps, out):
+def top_kernel(index, tails, home, away, mine_maps, other_maps, top_mine, top_other, out):
     size = tails.shape[2]
     count = tails.shape[0]
     out[:count] = tails[...]
@@ -181,8 +183,8 @@
         wide_left(away[0]), other_maps[index]
     )
     out[count] = both[:, :size]
-    both = wide_dot(wide_left(both[:, size:]), mine_maps[index + 1]) + wide_dot(
-        wide_left(home[1] + away[1]), other_maps[index + 1]
+    both = wide_dot(wide_left(both[:, size:]), top_mine[0]) + wide_dot(
+        wide_left(home[1] + away[1]), top_other[0]
     )
     out[count + 1] = both[:, :size]
     out[count + 2] = both[:, size:]
@@ -342,51 +344,60 @@
         merge_flops,
     )
     nodes, away_first = [node], away
+
+    def folds(first, last, *after):
+        return call(
+            functools.partial(fold_kernel, first),
+            (wide(last - first),) * 2,
+            (*node_params, *after),
+            (last - first) * fold_flops,
+            in_specs=[vmem] * 3 + [anywhere] * len(after),
+            scratch_shapes=[both],
+        )
+
     child_leaf, skeleton = lax.optimization_barrier((child_leaf, skeleton))
     for tier in range(1, height):
         away = blk_swap(skeleton, 1 << tier)
         after = ()
         if tier == 1:
-            mine_maps, other_maps = call(
-                fold_kernel,
-                (wide(height - 1),) * 2,
-                tuple(node_params),
-                (height - 1) * fold_flops,
-                scratch_shapes=[both],
-            )
-            tail, carried = call(
+            mine_maps, other_maps = folds(1, height - 1)
+            tail, carried, *climb = call(
                 carry_kernel,
-                (array(k_half, size),) * 2,
-                (child_leaf, home, away_first, first_mine, first_other),
-                6 * k_half * 4 * size * size,
-                in_specs=[smem] + [vmem] * 4,
+                (array(k_half, size),) * (3 if height == 3 else 2),
+                (child_leaf, home, away_first, first_mine, first_other, mine_maps),
+                6 * k_half * 5 * size * size,
+                in_specs=[smem] + [vmem] * 5,
             )
             tails = [tail]
         if tier < height - 2:
-            both = call(
+            pair = call(
                 functools.partial(pair_kernel, tier - 1),
                 array(k_half, 2 * size),
                 (carried, blk_swap(carried, 1 << tier), mine_maps, other_maps),
                 6 * k_half * 4 * size * size,
             )
-            tails.append(both[:, :size])
-            carried = both[:, size:]
+            tails.append(pair[:, :size])
+            carried = pair[:, size:]
         if tier == height - 2:
-            climb = call(
-                functools.partial(climb_kernel, tier - 1),
-                array(k_half, size),
-                (carried, mine_maps),
-                6 * k_half * size * size,
-            )
-            far = blk_swap(climb, 2 << tier)
-            after = (climb,)
+            if not climb:
+                climb = [
+                    call(
+                        functools.partial(climb_kernel, tier - 1),
+                        array(k_half, size),
+                        (carried, mine_maps),
+                        6 * k_half * size * size,
+                    )
+                ]
+            far = blk_swap(climb[0], 2 << tier)
+            after = (climb[0],)
         if tier == height - 1:
+            top_mine, top_other = folds(height - 1, height)
             relay = call(relay_kernel, array(2, k_half, size), (carried, far), k_half * size)
             relayed = blk_swap(relay, 1 << (tier - 1))
             tails = call(
                 functools.partial(top_kernel, tier - 2),
                 array(height + 1, k_half, size),
-                (jnp.stack(tails), relay, relayed, mine_maps, other_maps),
+                (jnp.stack(tails), relay, relayed, mine_maps, other_maps, top_mine, top_other),
                 6 * k_half * 6 * size * size,
             )
             solved, leaf_map = call(
@@ -397,15 +408,18 @@
                 in_specs=[smem] + [vmem] * 3,
             )
             after = (solved,)
+        last = tier == height - 1
+        if last:
+            mine_maps, other_maps = top_mine, top_other
+        index = 0 if last else tier - 1
         base = call(
-            functools.partial(base_kernel, tier - 1),
+            functools.partial(base_kernel, index),
             array(half, 2 * size),
             (skeleton, mine_maps),
             merge_flops,
         )
-        last = tier == height - 1
         node, skeleton = call(
-            functools.partial(last_merge_kernel if last else merge_kernel, tier - 1),
+            functools.partial(last_merge_kernel if last else merge_kernel, index),
             (array(half, size), array(part if last else half, size)),
             (base, away, other_maps) + ((tails,) if last else ()) + after,
             merge_flops,

time: 39.1 us -> 39.1 us (level)
  transfers between devices with their start and end apart: 16 -> 16, of which waited for: 8 -> 8; matrix products, arithmetic and copies ran while one was open for 0% -> 0% of each run, Pallas kernels for 8% -> 9%
where the time goes in v3:
time: 39.1 us; the launch traced here: 39 us
  waiting for transfers between devices  18.4 us (47%)
  starting transfers between devices  11.9 us (30%)
  Pallas kernels  7.29 us (19%)
  between operations  1.44 us (4%)
    ppermute x13, waiting for transfers between devices, blk_swap(): return lax.ppermute(value, 'blk', [(i, i ^ mask) for i in range(leaves)])  14.6 us
    ppermute x13, starting transfers between devices, blk_swap(): return lax.ppermute(value, 'blk', [(i, i ^ mask) for i in range(leaves)])  8.34 us
    pallas_call x15, Pallas kernels, call(): pl.pallas_call(kernel, out_shape=out_shape, in_specs=in_specs or [vmem] *...  7.29 us
    ppermute x3, waiting for transfers between devices, level_swap(): return lax.ppermute(value, 'level', [(i, i ^ mask) for i in range(fronts)])  3.71 us
    ppermute x3, starting transfers between devices, level_swap(): return lax.ppermute(value, 'level', [(i, i ^ mask) for i in range(fronts)])  3.55 us
  transfers between devices with their start and end apart: 16, of which 8 were waited for; matrix products, arithmetic and copies ran while one was open for 0% of the time, Pallas kernels for 9%

profile of v3, /device:TPU:0, one launch (start us, length us, event | category | flops | bytes accessed | tf_op | source)
XLA Modules:
  0.0 39.0 jit_solution(18269983453108657061)
XLA Ops:
  0.6 1.9 %shard_map.112 = (f32[320,128]{1,0:T(8,128)S(1)}, f32[256,128]{1,0:T(8,128)S(1)}, bf16[768,128]{1,0:T(8,128)(2,1)S(1)}, f32[2,256,256]{2,1,0:T(8,128)S(1)}, f32[...) custom-call(f32[512,256]{1,0:T(8,128)} %bitcast.22, ...), custom_call_target="tpu_custom_call" | custom-call | flops 113246208 | bytes 3768320 | tf_op jit(solution)/shard_map/pallas_call | solution.py:43
  2.6 0.6 %collective-permute-start = (f32[320,128]{1,0:T(8,128)S(1)}, f32[320,128]{1,0:T(8,128)S(1)}, u32[]{:S(2)}, u32[]{:S(2)}) collective-permute-start(f32[320,128]{1,0:T(8,128)S(1)} %get-tuple-element.47), channel_id=1, source_target_pairs={{0,1},{1,0},{2,3},{3,2},{4,5},{5,4},{6,7},{7,6},{8,9},{9,8},{10,11... | collective-permute-start | bytes 491528 | tf_op jit(solution)/shard_map/ppermute | solution.py:290
  3.1 0.8 %shard_map.113 = (bf16[1,384,256]{2,1,0:T(8,128)(2,1)S(1)}, bf16[1,384,256]{2,1,0:T(8,128)(2,1)S(1)}, f32[256,256]{1,0:T(8,128)S(1)}, f32[64,128]{1,0:T(8,128)S(1)}) custom-call(f32[256,256]{1,0:T(8,128)S(1)} %get-tuple-element.39.generator, f32[128,128]{1,0:T(8,128)S(1)} %get-tuple-element.40.inverse, f32[128,128]{1,0:T(8,128)S(1)} %get-tuple-element.41.lower, ...), custom_call_target="tpu_custom_call" | custom-call | flops 176160768 | bytes 1933312 | tf_op jit(solution)/shard_map/pallas_call | solution.py:43
  4.4 3.0 %collective-permute-start.5 = (f32[256,128]{1,0:T(8,128)S(1)}, f32[256,128]{1,0:T(8,128)S(1)}, u32[]{:S(2)}, u32[]{:S(2)}) collective-permute-start(f32[256,128]{1,0:T(8,128)S(1)} %get-tuple-element.67.home), channel_id=1, source_target_pairs={{0,2},{1,3},{2,0},{3,1},{4,6},{5,7},{6,4},{7,5},{8,10},{9,11},{10,... | collective-permute-start | bytes 393224 | tf_op jit(solution)/shard_map/ppermute | solution.py:290
  8.1 0.4 shard_map.116
  8.5 0.3 shard_map.117
  9.0 2.2 %collective-permute-done.5.away = f32[256,128]{1,0:T(8,128)S(1)} collective-permute-done((f32[256,128]{1,0:T(8,128)S(1)}, f32[256,128]{1,0:T(8,128)S(1)}, u32[]{:S(2)}, u32[]{:S(2)}) %collective-permute-start.5) | collective-permute-done | bytes 131104 | tf_op jit(solution)/shard_map/ppermute | solution.py:290
  11.4 2.8 %collective-permute-start.7 = (f32[256,128]{1,0:T(8,128)S(1)}, f32[256,128]{1,0:T(8,128)S(1)}, u32[]{:S(2)}, u32[]{:S(2)}) collective-permute-start(f32[256,128]{1,0:T(8,128)S(1)} %get-tuple-element.69.home), channel_id=1, source_target_pairs={{0,4},{1,5},{2,6},{3,7},{4,0},{5,1},{6,2},{7,3},{8,12},{9,13},{10,... | collective-permute-start | bytes 393224 | tf_op jit(solution)/shard_map/ppermute | solution.py:290
  14.4 7.2 %collective-permute-done.1.far = f32[64,128]{1,0:T(8,128)S(1)} collective-permute-done((f32[64,128]{1,0:T(8,128)S(1)}, f32[64,128]{1,0:T(8,128)S(1)}, u32[]{:S(2)}, u32[]{:S(2)}) %collective-permute-start.1) | collective-permute-done | bytes 32800 | tf_op jit(solution)/shard_map/ppermute | solution.py:290
  21.6 0.5 %collective-permute-start.2 = (f32[2,64,128]{2,1,0:T(8,128)S(1)}, f32[2,64,128]{2,1,0:T(8,128)S(1)}, u32[]{:S(2)}, u32[]{:S(2)}) collective-permute-start(f32[2,64,128]{2,1,0:T(8,128)S(1)} %shard_map.118.home), channel_id=1, source_target_pairs={{0,2},{1,3},{2,0},{3,1},{4,6},{5,7},{6,4},{7,5},{8,10},{9,11},{10,... | collective-permute-start | bytes 196616 | tf_op jit(solution)/shard_map/ppermute | solution.py:290
  22.1 0.4 shard_map.119
  22.5 0.4 %shard_map.115 = (f32[2,256,128]{2,1,0:T(8,128)S(1)}, f32[128,128]{1,0:T(8,128)S(1)}) custom-call(s32[1]{0:T(128)S(6)} %copy.12.child, f32[2,256,256]{2,1,0:T(8,128)S(1)} %get-tuple-element.42.right, f32[128,256]{1,0:T(8,128)S(1)} %get-tuple-element.43.coupling, f32[256,128]{1,0:T(8,128)S(1)} %get-tuple-element.51.solve_map), custom_call_target="tpu_custom_call" | custom-call | flops 125829120 | bytes 1114116 | tf_op jit(solution)/shard_map/pallas_call | solution.py:43
  22.9 2.9 %collective-permute-done.2.away = f32[2,64,128]{2,1,0:T(8,128)S(1)} collective-permute-done((f32[2,64,128]{2,1,0:T(8,128)S(1)}, f32[2,64,128]{2,1,0:T(8,128)S(1)}, u32[]{:S(2)}, u32[]{:S(2)}) %collective-permute-start.2) | collective-permute-done | bytes 65568 | tf_op jit(solution)/shard_map/ppermute | solution.py:290
  25.9 0.4 shard_map.120.tails.home
  26.7 2.4 %collective-permute-start.14 = (f32[320,128]{1,0:T(8,128)S(1)}, f32[320,128]{1,0:T(8,128)S(1)}, u32[]{:S(2)}, u32[]{:S(2)}) collective-permute-start(f32[320,128]{1,0:T(8,128)S(1)} %get-tuple-element.71.refs_6_), channel_id=1, source_target_pairs={{0,24},{8,16},{16,8},{24,0},{1,25},{9,17},{17,9},{25,1},{2,26},{10... | collective-permute-start | bytes 491528 | tf_op jit(solution)/shard_map/ppermute | solution.py:293
  29.1 0.5 %collective-permute-start.12 = (f32[320,128]{1,0:T(8,128)S(1)}, f32[320,128]{1,0:T(8,128)S(1)}, u32[]{:S(2)}, u32[]{:S(2)}) collective-permute-start(f32[320,128]{1,0:T(8,128)S(1)} %get-tuple-element.71.refs_6_), channel_id=1, source_target_pairs={{0,16},{8,24},{16,0},{24,8},{1,17},{9,25},{17,1},{25,9},{2,18},{10... | collective-permute-start | bytes 491528 | tf_op jit(solution)/shard_map/ppermute | solution.py:293
  29.6 0.7 %collective-permute-start.10 = (f32[320,128]{1,0:T(8,128)S(1)}, f32[320,128]{1,0:T(8,128)S(1)}, u32[]{:S(2)}, u32[]{:S(2)}) collective-permute-start(f32[320,128]{1,0:T(8,128)S(1)} %get-tuple-element.71.refs_6_), channel_id=1, source_target_pairs={{0,8},{8,0},{16,24},{24,16},{1,9},{9,1},{17,25},{25,17},{2,10},{10... | collective-permute-start | bytes 491528 | tf_op jit(solution)/shard_map/ppermute | solution.py:293
  30.3 0.5 %collective-permute-start.6 = (f32[256,128]{1,0:T(8,128)S(1)}, f32[256,128]{1,0:T(8,128)S(1)}, u32[]{:S(2)}, u32[]{:S(2)}) collective-permute-start(f32[256,128]{1,0:T(8,128)S(1)} %get-tuple-element.68.refs_2_), channel_id=1, source_target_pairs={{0,1},{1,0},{2,3},{3,2},{4,5},{5,4},{6,7},{7,6},{8,9},{9,8},{10,11... | collective-permute-start | bytes 393224 | tf_op jit(solution)/shard_map/ppermute | solution.py:290
  30.8 0.8 %collective-permute-done.3.away = f32[4,64,128]{2,1,0:T(8,128)S(1)} collective-permute-done((f32[4,64,128]{2,1,0:T(8,128)S(1)}, f32[4,64,128]{2,1,0:T(8,128)S(1)}, u32[]{:S(2)}, u32[]{:S(2)}) %collective-permute-start.3) | collective-permute-done | bytes 131104 | tf_op jit(solution)/shard_map/ppermute | solution.py:290
  31.7 2.3 %collective-permute-done.14.refs_12_ = f32[320,128]{1,0:T(8,128)S(1)} collective-permute-done((f32[320,128]{1,0:T(8,128)S(1)}, f32[320,128]{1,0:T(8,128)S(1)}, u32[]{:S(2)}, u32[]{:S(2)}) %collective-permute-start.14) | collective-permute-done | bytes 163872 | tf_op jit(solution)/shard_map/ppermute | solution.py:293
  34.1 1.4 %collective-permute-done.12.refs_10_ = f32[320,128]{1,0:T(8,128)S(1)} collective-permute-done((f32[320,128]{1,0:T(8,128)S(1)}, f32[320,128]{1,0:T(8,128)S(1)}, u32[]{:S(2)}, u32[]{:S(2)}) %collective-permute-start.12) | collective-permute-done | bytes 163872 | tf_op jit(solution)/shard_map/ppermute | solution.py:293
  35.5 0.5 %collective-permute-start.11 = (f32[320,128]{1,0:T(8,128)S(1)}, f32[320,128]{1,0:T(8,128)S(1)}, u32[]{:S(2)}, u32[]{:S(2)}) collective-permute-start(f32[320,128]{1,0:T(8,128)S(1)} %collective-permute-done.10.refs_8_), channel_id=1, source_target_pairs={{0,1},{1,0},{2,3},{3,2},{4,5},{5,4},{6,7},{7,6},{8,9},{9,8},{10,11... | collective-permute-start | bytes 491528 | tf_op jit(solution)/shard_map/ppermute | solution.py:290
  36.0 1.3 %collective-permute-done.8.refs_2_.refs_5_ = f32[256,128]{1,0:T(8,128)S(1)} collective-permute-done((f32[256,128]{1,0:T(8,128)S(1)}, f32[256,128]{1,0:T(8,128)S(1)}, u32[]{:S(2)}, u32[]{:S(2)}) %collective-permute-start.8) | collective-permute-done | bytes 131104 | tf_op jit(solution)/shard_map/ppermute | solution.py:290
  37.5 1.5 %shard_map.126 = (f32[512,128]{1,0:T(8,128)}, f32[3,512,128]{2,1,0:T(8,128)}, f32[512,128]{1,0:T(8,128)}) custom-call(f32[2,256,128]{2,1,0:T(8,128)S(1)} %get-tuple-element.52.refs_0_.solved, bf16[384,640]{1,0:T(8,128)(2,1)S(1)} %shard_map.125.wide_maps, f32[256,128]{1,0:T(8,128)S(1)} %get-tuple-element.66.refs_0_, ...), custom_call_target="tpu_custom_call" | custom-call | flops 251658240 | bytes 4161536 | tf_op jit(solution)/shard_map/pallas_call | solution.py:43
  (29 shorter events, 1.9 us)
Async XLA Ops:
  2.6 1.6 %collective-permute-start = (f32[320,128]{1,0:T(8,128)S(1)}, f32[320,128]{1,0:T(8,128)S(1)}, u32[]{:S(2)}, u32[]{:S(2)}) collective-permute-start(f32[320,128]{1,0:T(8,128)S(1)} %get-tuple-element.47), channel_id=1, source_target_pairs={{0,1},{1,0},{2,3},{3,2},{4,5},{5,4},{6,7},{7,6},{8,9},{9,8},{10,11... | collective-permute-start | bytes 491528 | tf_op jit(solution)/shard_map/ppermute | solution.py:290
  3.1 4.9 %copy-start = (f32[1,1,3,256,256]{4,3,2,1,0:T(8,128)S(1)}, f32[1,1,3,256,256]{4,3,2,1,0:T(8,128)}, u32[]{:S(2)}) copy-start(f32[1,1,3,256,256]{4,3,2,1,0:T(8,128)} %param.13) | copy-start | bytes 2359300
  4.2 3.9 %copy-start.1 = (f32[1,1,3,128,128]{4,3,2,1,0:T(8,128)S(1)}, f32[1,1,3,128,128]{4,3,2,1,0:T(8,128)}, u32[]{:S(2)}) copy-start(f32[1,1,3,128,128]{4,3,2,1,0:T(8,128)} %param.14) | copy-start | bytes 589828
  4.2 3.9 %copy-start.2 = (f32[1,1,3,128,128]{4,3,2,1,0:T(8,128)S(1)}, f32[1,1,3,128,128]{4,3,2,1,0:T(8,128)}, u32[]{:S(2)}) copy-start(f32[1,1,3,128,128]{4,3,2,1,0:T(8,128)} %param.15) | copy-start | bytes 589828
  4.4 6.8 %collective-permute-start.5 = (f32[256,128]{1,0:T(8,128)S(1)}, f32[256,128]{1,0:T(8,128)S(1)}, u32[]{:S(2)}, u32[]{:S(2)}) collective-permute-start(f32[256,128]{1,0:T(8,128)S(1)} %get-tuple-element.67.home), channel_id=1, source_target_pairs={{0,2},{1,3},{2,0},{3,1},{4,6},{5,7},{6,4},{7,5},{8,10},{9,11},{10,... | collective-permute-start | bytes 393224 | tf_op jit(solution)/shard_map/ppermute | solution.py:290
  11.4 15.0 %collective-permute-start.7 = (f32[256,128]{1,0:T(8,128)S(1)}, f32[256,128]{1,0:T(8,128)S(1)}, u32[]{:S(2)}, u32[]{:S(2)}) collective-permute-start(f32[256,128]{1,0:T(8,128)S(1)} %get-tuple-element.69.home), channel_id=1, source_target_pairs={{0,4},{1,5},{2,6},{3,7},{4,0},{5,1},{6,2},{7,3},{8,12},{9,13},{10,... | collective-permute-start | bytes 393224 | tf_op jit(solution)/shard_map/ppermute | solution.py:290
  14.2 7.3 %collective-permute-start.1 = (f32[64,128]{1,0:T(8,128)S(1)}, f32[64,128]{1,0:T(8,128)S(1)}, u32[]{:S(2)}, u32[]{:S(2)}) collective-permute-start(f32[64,128]{1,0:T(8,128)S(1)} %get-tuple-element.62.refs_0_), channel_id=1, source_target_pairs={{0,4},{1,5},{2,6},{3,7},{4,0},{5,1},{6,2},{7,3},{8,12},{9,13},{10,... | collective-permute-start | bytes 98312 | tf_op jit(solution)/shard_map/ppermute | solution.py:290
  21.6 4.3 %collective-permute-start.2 = (f32[2,64,128]{2,1,0:T(8,128)S(1)}, f32[2,64,128]{2,1,0:T(8,128)S(1)}, u32[]{:S(2)}, u32[]{:S(2)}) collective-permute-start(f32[2,64,128]{2,1,0:T(8,128)S(1)} %shard_map.118.home), channel_id=1, source_target_pairs={{0,2},{1,3},{2,0},{3,1},{4,6},{5,7},{6,4},{7,5},{8,10},{9,11},{10,... | collective-permute-start | bytes 196616 | tf_op jit(solution)/shard_map/ppermute | solution.py:290
  22.1 8.1 %collective-permute-start.4 = (f32[256,128]{1,0:T(8,128)S(1)}, f32[256,128]{1,0:T(8,128)S(1)}, u32[]{:S(2)}, u32[]{:S(2)}) collective-permute-start(f32[256,128]{1,0:T(8,128)S(1)} %get-tuple-element.66.refs_0_), channel_id=1, source_target_pairs={{0,1},{1,0},{2,3},{3,2},{4,5},{5,4},{6,7},{7,6},{8,9},{9,8},{10,11... | collective-permute-start | bytes 393224 | tf_op jit(solution)/shard_map/ppermute | solution.py:290
  26.7 7.4 %collective-permute-start.14 = (f32[320,128]{1,0:T(8,128)S(1)}, f32[320,128]{1,0:T(8,128)S(1)}, u32[]{:S(2)}, u32[]{:S(2)}) collective-permute-start(f32[320,128]{1,0:T(8,128)S(1)} %get-tuple-element.71.refs_6_), channel_id=1, source_target_pairs={{0,24},{8,16},{16,8},{24,0},{1,25},{9,17},{17,9},{25,1},{2,26},{10... | collective-permute-start | bytes 491528 | tf_op jit(solution)/shard_map/ppermute | solution.py:293
  29.1 6.4 %collective-permute-start.12 = (f32[320,128]{1,0:T(8,128)S(1)}, f32[320,128]{1,0:T(8,128)S(1)}, u32[]{:S(2)}, u32[]{:S(2)}) collective-permute-start(f32[320,128]{1,0:T(8,128)S(1)} %get-tuple-element.71.refs_6_), channel_id=1, source_target_pairs={{0,16},{8,24},{16,0},{24,8},{1,17},{9,25},{17,1},{25,9},{2,18},{10... | collective-permute-start | bytes 491528 | tf_op jit(solution)/shard_map/ppermute | solution.py:293
  29.6 5.9 %collective-permute-start.10 = (f32[320,128]{1,0:T(8,128)S(1)}, f32[320,128]{1,0:T(8,128)S(1)}, u32[]{:S(2)}, u32[]{:S(2)}) collective-permute-start(f32[320,128]{1,0:T(8,128)S(1)} %get-tuple-element.71.refs_6_), channel_id=1, source_target_pairs={{0,8},{8,0},{16,24},{24,16},{1,9},{9,1},{17,25},{25,17},{2,10},{10... | collective-permute-start | bytes 491528 | tf_op jit(solution)/shard_map/ppermute | solution.py:293
  30.2 1.3 %collective-permute-start.3 = (f32[4,64,128]{2,1,0:T(8,128)S(1)}, f32[4,64,128]{2,1,0:T(8,128)S(1)}, u32[]{:S(2)}, u32[]{:S(2)}) collective-permute-start(f32[4,64,128]{2,1,0:T(8,128)S(1)} %shard_map.120.tails.home), channel_id=1, source_target_pairs={{0,1},{1,0},{2,3},{3,2},{4,5},{5,4},{6,7},{7,6},{8,9},{9,8},{10,11... | collective-permute-start | bytes 393224 | tf_op jit(solution)/shard_map/ppermute | solution.py:290
  30.3 5.7 %collective-permute-start.6 = (f32[256,128]{1,0:T(8,128)S(1)}, f32[256,128]{1,0:T(8,128)S(1)}, u32[]{:S(2)}, u32[]{:S(2)}) collective-permute-start(f32[256,128]{1,0:T(8,128)S(1)} %get-tuple-element.68.refs_2_), channel_id=1, source_target_pairs={{0,1},{1,0},{2,3},{3,2},{4,5},{5,4},{6,7},{7,6},{8,9},{9,8},{10,11... | collective-permute-start | bytes 393224 | tf_op jit(solution)/shard_map/ppermute | solution.py:290
  31.6 5.7 %collective-permute-start.9 = (f32[320,128]{1,0:T(8,128)S(1)}, f32[320,128]{1,0:T(8,128)S(1)}, u32[]{:S(2)}, u32[]{:S(2)}) collective-permute-start(f32[320,128]{1,0:T(8,128)S(1)} %get-tuple-element.71.refs_6_), channel_id=1, source_target_pairs={{0,1},{1,0},{2,3},{3,2},{4,5},{5,4},{6,7},{7,6},{8,9},{9,8},{10,11... | collective-permute-start | bytes 491528 | tf_op jit(solution)/shard_map/ppermute | solution.py:290
  34.1 3.4 %collective-permute-start.15 = (f32[320,128]{1,0:T(8,128)S(1)}, f32[320,128]{1,0:T(8,128)S(1)}, u32[]{:S(2)}, u32[]{:S(2)}) collective-permute-start(f32[320,128]{1,0:T(8,128)S(1)} %collective-permute-done.14.refs_12_), channel_id=1, source_target_pairs={{0,1},{1,0},{2,3},{3,2},{4,5},{5,4},{6,7},{7,6},{8,9},{9,8},{10,11... | collective-permute-start | bytes 491528 | tf_op jit(solution)/shard_map/ppermute | solution.py:290
  35.5 2.0 %collective-permute-start.13 = (f32[320,128]{1,0:T(8,128)S(1)}, f32[320,128]{1,0:T(8,128)S(1)}, u32[]{:S(2)}, u32[]{:S(2)}) collective-permute-start(f32[320,128]{1,0:T(8,128)S(1)} %collective-permute-done.12.refs_10_), channel_id=1, source_target_pairs={{0,1},{1,0},{2,3},{3,2},{4,5},{5,4},{6,7},{7,6},{8,9},{9,8},{10,11... | collective-permute-start | bytes 491528 | tf_op jit(solution)/shard_map/ppermute | solution.py:290
  35.5 2.0 %collective-permute-start.11 = (f32[320,128]{1,0:T(8,128)S(1)}, f32[320,128]{1,0:T(8,128)S(1)}, u32[]{:S(2)}, u32[]{:S(2)}) collective-permute-start(f32[320,128]{1,0:T(8,128)S(1)} %collective-permute-done.10.refs_8_), channel_id=1, source_target_pairs={{0,1},{1,0},{2,3},{3,2},{4,5},{5,4},{6,7},{7,6},{8,9},{9,8},{10,11... | collective-permute-start | bytes 491528 | tf_op jit(solution)/shard_map/ppermute | solution.py:290
  36.0 1.3 %collective-permute-start.8 = (f32[256,128]{1,0:T(8,128)S(1)}, f32[256,128]{1,0:T(8,128)S(1)}, u32[]{:S(2)}, u32[]{:S(2)}) collective-permute-start(f32[256,128]{1,0:T(8,128)S(1)} %get-tuple-element.70.refs_4_), channel_id=1, source_target_pairs={{0,1},{1,0},{2,3},{3,2},{4,5},{5,4},{6,7},{7,6},{8,9},{9,8},{10,11... | collective-permute-start | bytes 393224 | tf_op jit(solution)/shard_map/ppermute | solution.py:290

commit v4 on v3

--- a/solution.py
+++ b/solution.py
@@ -93,12 +93,26 @@
         copy.wait()
 
 
-def leaf_solve_kernel(child, right, coupling, solve_map, solved, leaf_map):
+def leaf_solve(child, right, coupling, solve_map, solved, leaf_map):
     parts = wide_right(solve_map[...])
     for part in range(2):
         solved[part] = wide_dot(wide_left(right[1 - part]), parts)
     on_target = lax.axis_index("blk") == child[0]
     leaf_map[...] = jnp.where(on_target, wide_dot(wide_left(coupling[...]), parts), 0.0)
+
+
+def leaf_solve_kernel(bit, solved_early, map_early, *refs):
+    solved, leaf_map = refs[-2:]
+    early = (lax.axis_index("blk") >> bit) & 1
+
+    @pl.when(early == 1)
+    def _():
+        solved[...] = solved_early[...]
+        leaf_map[...] = map_early[...]
+
+    @pl.when(early == 0)
+    def _():
+        leaf_solve(*refs)
 
 
 def fold(tier, generator, inverse, lower, both):
@@ -130,6 +144,15 @@
 
 def base_kernel(index, home, mine_maps, base):
     base[...] = wide_dot(wide_left(home[...]), mine_maps[index])
+
+
+def late_merge_kernel(index, bit, base, away, other_maps, child, right, coupling, solve_map, *refs):
+    node, skeleton, solved, leaf_map = refs[-4:]
+    merge_kernel(index, base, away, other_maps, node, skeleton)
+
+    @pl.when((lax.axis_index("blk") >> bit) & 1 == 1)
+    def _():
+        leaf_solve(child, right, coupling, solve_map, solved, leaf_map)
 
 
 def merge_kernel(index, base, away, other_maps, *refs):
@@ -294,7 +317,7 @@
 
     k_half = k_rows // 2
     node_params = (node_gen[0, 0], node_inverse[0, 0], node_lower[0, 0])
-    away, leaf_solve, leaf_skeleton, right_here, coupling_here, *first_params = call(
+    away, leaf_solve_map, leaf_skeleton, right_here, coupling_here, *first_params = call(
         leaf_kernel,
         (
             array(part, size),
@@ -401,11 +424,11 @@
                 6 * k_half * 6 * size * size,
             )
             solved, leaf_map = call(
-                leaf_solve_kernel,
+                functools.partial(leaf_solve_kernel, height - 2),
                 (array(2, half, size), array(k_rows, size)),
-                (child_leaf, right_here, coupling_here, leaf_solve),
+                (*early, *leaf_args),
                 6 * (rows + k_rows) * leaf_size * size,
-                in_specs=[smem] + [vmem] * 3,
+                in_specs=[vmem] * 2 + [smem] + [vmem] * 3,
             )
             after = (solved,)
         last = tier == height - 1
@@ -418,12 +441,18 @@
             (skeleton, mine_maps),
             merge_flops,
         )
-        node, skeleton = call(
-            functools.partial(last_merge_kernel if last else merge_kernel, index),
-            (array(half, size), array(part if last else half, size)),
-            (base, away, other_maps) + ((tails,) if last else ()) + after,
-            merge_flops,
-            in_specs=[vmem] * (4 if last else 3) + [anywhere] * len(after),
+        leaf_args = (child_leaf, right_here, coupling_here, leaf_solve_map)
+        kernel = functools.partial(last_merge_kernel if last else merge_kernel, index)
+        args, specs = (base, away, other_maps), [vmem] * 3
+        shapes = (array(half, size), array(part if last else half, size))
+        if last:
+            args, specs = args + (tails,), specs + [vmem]
+        if tier == height - 2:
+            kernel = functools.partial(late_merge_kernel, index, height - 2)
+            args, specs = args + leaf_args, specs + [smem] + [vmem] * 3
+            shapes += (array(2, half, size), array(k_rows, size))
+        node, skeleton, *early = call(
+            kernel, shapes, args + after, merge_flops, in_specs=specs + [anywhere] * len(after)
         )
         nodes.append(node)
     received = [level_swap(skeleton, mask) for mask in range(1, fronts)]

time: 39.1 us -> 39.6 us (1.013)
  waiting for transfers between devices: 18.4 us -> 18.8 us
    ppermute x13, waiting for transfers between devices: 14.6 us -> 15.1 us  [blk_swap(): return lax.ppermute(value, 'blk', [(i, i ^ mask) for i in range(leaves)])]
where the time goes in v4:
time: 39.6 us; the launch traced here: 39.4 us
  waiting for transfers between devices  18.8 us (47%)
  starting transfers between devices  11.9 us (30%)
  Pallas kernels  7.3 us (18%)
  between operations  1.44 us (4%)
    ppermute x13, waiting for transfers between devices, blk_swap(): return lax.ppermute(value, 'blk', [(i, i ^ mask) for i in range(leaves)])  15.1 us
    ppermute x13, starting transfers between devices, blk_swap(): return lax.ppermute(value, 'blk', [(i, i ^ mask) for i in range(leaves)])  8.34 us
    pallas_call x15, Pallas kernels, call(): pl.pallas_call(kernel, out_shape=out_shape, in_specs=in_specs or [vmem] *...  7.3 us
    ppermute x3, waiting for transfers between devices, level_swap(): return lax.ppermute(value, 'level', [(i, i ^ mask) for i in range(fronts)])  3.71 us
    ppermute x3, starting transfers between devices, level_swap(): return lax.ppermute(value, 'level', [(i, i ^ mask) for i in range(fronts)])  3.55 us
  transfers between devices with their start and end apart: 16, of which 8 were waited for; matrix products, arithmetic and copies ran while one was open for 0% of the time, Pallas kernels for 9%

profile of v4, /device:TPU:0, one launch (start us, length us, event | category | flops | bytes accessed | tf_op | source)
XLA Modules:
  0.0 39.4 jit_solution(7309926357623256671)
XLA Ops:
  0.6 1.9 %shard_map.112 = (f32[320,128]{1,0:T(8,128)S(1)}, f32[256,128]{1,0:T(8,128)S(1)}, bf16[768,128]{1,0:T(8,128)(2,1)S(1)}, f32[2,256,256]{2,1,0:T(8,128)S(1)}, f32[...) custom-call(f32[512,256]{1,0:T(8,128)} %bitcast.22, ...), custom_call_target="tpu_custom_call" | custom-call | flops 113246208 | bytes 3768320 | tf_op jit(solution)/shard_map/pallas_call | solution.py:43
  2.6 0.6 %collective-permute-start = (f32[320,128]{1,0:T(8,128)S(1)}, f32[320,128]{1,0:T(8,128)S(1)}, u32[]{:S(2)}, u32[]{:S(2)}) collective-permute-start(f32[320,128]{1,0:T(8,128)S(1)} %get-tuple-element.49), channel_id=1, source_target_pairs={{0,1},{1,0},{2,3},{3,2},{4,5},{5,4},{6,7},{7,6},{8,9},{9,8},{10,11... | collective-permute-start | bytes 491528 | tf_op jit(solution)/shard_map/ppermute | solution.py:313
  3.1 0.8 %shard_map.113 = (bf16[1,384,256]{2,1,0:T(8,128)(2,1)S(1)}, bf16[1,384,256]{2,1,0:T(8,128)(2,1)S(1)}, f32[256,256]{1,0:T(8,128)S(1)}, f32[64,128]{1,0:T(8,128)S(1)}) custom-call(f32[256,256]{1,0:T(8,128)S(1)} %get-tuple-element.41.generator, f32[128,128]{1,0:T(8,128)S(1)} %get-tuple-element.42.inverse, f32[128,128]{1,0:T(8,128)S(1)} %get-tuple-element.43.lower, ...), custom_call_target="tpu_custom_call" | custom-call | flops 176160768 | bytes 1933312 | tf_op jit(solution)/shard_map/pallas_call | solution.py:43
  4.4 3.0 %collective-permute-start.1 = (f32[256,128]{1,0:T(8,128)S(1)}, f32[256,128]{1,0:T(8,128)S(1)}, u32[]{:S(2)}, u32[]{:S(2)}) collective-permute-start(f32[256,128]{1,0:T(8,128)S(1)} %get-tuple-element.52.home), channel_id=1, source_target_pairs={{0,2},{1,3},{2,0},{3,1},{4,6},{5,7},{6,4},{7,5},{8,10},{9,11},{10,... | collective-permute-start | bytes 393224 | tf_op jit(solution)/shard_map/ppermute | solution.py:313
  8.1 0.4 shard_map.115
  8.5 0.3 shard_map.117
  9.0 2.2 %collective-permute-done.1.away = f32[256,128]{1,0:T(8,128)S(1)} collective-permute-done((f32[256,128]{1,0:T(8,128)S(1)}, f32[256,128]{1,0:T(8,128)S(1)}, u32[]{:S(2)}, u32[]{:S(2)}) %collective-permute-start.1) | collective-permute-done | bytes 131104 | tf_op jit(solution)/shard_map/ppermute | solution.py:313
  11.4 2.8 %collective-permute-start.7 = (f32[256,128]{1,0:T(8,128)S(1)}, f32[256,128]{1,0:T(8,128)S(1)}, u32[]{:S(2)}, u32[]{:S(2)}) collective-permute-start(f32[256,128]{1,0:T(8,128)S(1)} %get-tuple-element.73.home), channel_id=1, source_target_pairs={{0,4},{1,5},{2,6},{3,7},{4,0},{5,1},{6,2},{7,3},{8,12},{9,13},{10,... | collective-permute-start | bytes 393224 | tf_op jit(solution)/shard_map/ppermute | solution.py:313
  14.4 7.2 %collective-permute-done.2.far = f32[64,128]{1,0:T(8,128)S(1)} collective-permute-done((f32[64,128]{1,0:T(8,128)S(1)}, f32[64,128]{1,0:T(8,128)S(1)}, u32[]{:S(2)}, u32[]{:S(2)}) %collective-permute-start.2) | collective-permute-done | bytes 32800 | tf_op jit(solution)/shard_map/ppermute | solution.py:313
  21.6 0.5 %collective-permute-start.3 = (f32[2,64,128]{2,1,0:T(8,128)S(1)}, f32[2,64,128]{2,1,0:T(8,128)S(1)}, u32[]{:S(2)}, u32[]{:S(2)}) collective-permute-start(f32[2,64,128]{2,1,0:T(8,128)S(1)} %shard_map.120.home), channel_id=1, source_target_pairs={{0,2},{1,3},{2,0},{3,1},{4,6},{5,7},{6,4},{7,5},{8,10},{9,11},{10,... | collective-permute-start | bytes 196616 | tf_op jit(solution)/shard_map/ppermute | solution.py:313
  22.1 0.4 shard_map.121
  22.5 3.3 %collective-permute-done.3.away = f32[2,64,128]{2,1,0:T(8,128)S(1)} collective-permute-done((f32[2,64,128]{2,1,0:T(8,128)S(1)}, f32[2,64,128]{2,1,0:T(8,128)S(1)}, u32[]{:S(2)}, u32[]{:S(2)}) %collective-permute-start.3) | collective-permute-done | bytes 65568 | tf_op jit(solution)/shard_map/ppermute | solution.py:313
  25.9 0.4 shard_map.122.tails.home
  26.5 0.4 %shard_map.119 = (f32[2,256,128]{2,1,0:T(8,128)S(1)}, f32[128,128]{1,0:T(8,128)S(1)}) custom-call(f32[2,256,128]{2,1,0:T(8,128)S(1)} %get-tuple-element.63.solved_early, f32[128,128]{1,0:T(8,128)S(1)} %get-tuple-element.64.map_early, s32[1]{0:T(128)S(6)} %copy.12.child.refs_0_, f32[2,256,256]{2,1,0:T(8,128)S(1)} %get-tuple-element.44.right.refs_1_, ...), custom_call_target="tpu_custom_call" | custom-call | flops 125829120 | bytes 1441796 | tf_op jit(solution)/shard_map/pallas_call | solution.py:43
  27.1 2.4 %collective-permute-start.14 = (f32[320,128]{1,0:T(8,128)S(1)}, f32[320,128]{1,0:T(8,128)S(1)}, u32[]{:S(2)}, u32[]{:S(2)}) collective-permute-start(f32[320,128]{1,0:T(8,128)S(1)} %get-tuple-element.75.refs_6_), channel_id=1, source_target_pairs={{0,24},{8,16},{16,8},{24,0},{1,25},{9,17},{17,9},{25,1},{2,26},{10... | collective-permute-start | bytes 491528 | tf_op jit(solution)/shard_map/ppermute | solution.py:316
  29.5 0.5 %collective-permute-start.12 = (f32[320,128]{1,0:T(8,128)S(1)}, f32[320,128]{1,0:T(8,128)S(1)}, u32[]{:S(2)}, u32[]{:S(2)}) collective-permute-start(f32[320,128]{1,0:T(8,128)S(1)} %get-tuple-element.75.refs_6_), channel_id=1, source_target_pairs={{0,16},{8,24},{16,0},{24,8},{1,17},{9,25},{17,1},{25,9},{2,18},{10... | collective-permute-start | bytes 491528 | tf_op jit(solution)/shard_map/ppermute | solution.py:316
  30.1 0.6 %collective-permute-start.10 = (f32[320,128]{1,0:T(8,128)S(1)}, f32[320,128]{1,0:T(8,128)S(1)}, u32[]{:S(2)}, u32[]{:S(2)}) collective-permute-start(f32[320,128]{1,0:T(8,128)S(1)} %get-tuple-element.75.refs_6_), channel_id=1, source_target_pairs={{0,8},{8,0},{16,24},{24,16},{1,9},{9,1},{17,25},{25,17},{2,10},{10... | collective-permute-start | bytes 491528 | tf_op jit(solution)/shard_map/ppermute | solution.py:316
  30.7 0.5 %collective-permute-start.6 = (f32[256,128]{1,0:T(8,128)S(1)}, f32[256,128]{1,0:T(8,128)S(1)}, u32[]{:S(2)}, u32[]{:S(2)}) collective-permute-start(f32[256,128]{1,0:T(8,128)S(1)} %get-tuple-element.72.refs_2_), channel_id=1, source_target_pairs={{0,1},{1,0},{2,3},{3,2},{4,5},{5,4},{6,7},{7,6},{8,9},{9,8},{10,11... | collective-permute-start | bytes 393224 | tf_op jit(solution)/shard_map/ppermute | solution.py:313
  31.2 0.8 %collective-permute-done.4.away = f32[4,64,128]{2,1,0:T(8,128)S(1)} collective-permute-done((f32[4,64,128]{2,1,0:T(8,128)S(1)}, f32[4,64,128]{2,1,0:T(8,128)S(1)}, u32[]{:S(2)}, u32[]{:S(2)}) %collective-permute-start.4) | collective-permute-done | bytes 131104 | tf_op jit(solution)/shard_map/ppermute | solution.py:313
  32.2 2.3 %collective-permute-done.14.refs_12_ = f32[320,128]{1,0:T(8,128)S(1)} collective-permute-done((f32[320,128]{1,0:T(8,128)S(1)}, f32[320,128]{1,0:T(8,128)S(1)}, u32[]{:S(2)}, u32[]{:S(2)}) %collective-permute-start.14) | collective-permute-done | bytes 163872 | tf_op jit(solution)/shard_map/ppermute | solution.py:316
  34.4 1.5 %collective-permute-done.12.refs_10_ = f32[320,128]{1,0:T(8,128)S(1)} collective-permute-done((f32[320,128]{1,0:T(8,128)S(1)}, f32[320,128]{1,0:T(8,128)S(1)}, u32[]{:S(2)}, u32[]{:S(2)}) %collective-permute-start.12) | collective-permute-done | bytes 163872 | tf_op jit(solution)/shard_map/ppermute | solution.py:316
  35.9 0.5 %collective-permute-start.11 = (f32[320,128]{1,0:T(8,128)S(1)}, f32[320,128]{1,0:T(8,128)S(1)}, u32[]{:S(2)}, u32[]{:S(2)}) collective-permute-start(f32[320,128]{1,0:T(8,128)S(1)} %collective-permute-done.10.refs_8_), channel_id=1, source_target_pairs={{0,1},{1,0},{2,3},{3,2},{4,5},{5,4},{6,7},{7,6},{8,9},{9,8},{10,11... | collective-permute-start | bytes 491528 | tf_op jit(solution)/shard_map/ppermute | solution.py:313
  36.5 1.3 %collective-permute-done.8.refs_2_.refs_5_ = f32[256,128]{1,0:T(8,128)S(1)} collective-permute-done((f32[256,128]{1,0:T(8,128)S(1)}, f32[256,128]{1,0:T(8,128)S(1)}, u32[]{:S(2)}, u32[]{:S(2)}) %collective-permute-start.8) | collective-permute-done | bytes 131104 | tf_op jit(solution)/shard_map/ppermute | solution.py:313
  37.9 1.5 %shard_map.126 = (f32[512,128]{1,0:T(8,128)}, f32[3,512,128]{2,1,0:T(8,128)}, f32[512,128]{1,0:T(8,128)}) custom-call(f32[2,256,128]{2,1,0:T(8,128)S(1)} %get-tuple-element.65.refs_0_.solved, bf16[384,640]{1,0:T(8,128)(2,1)S(1)} %shard_map.125.wide_maps, f32[256,128]{1,0:T(8,128)S(1)} %get-tuple-element.71.refs_0_, ...), custom_call_target="tpu_custom_call" | custom-call | flops 251658240 | bytes 4161536 | tf_op jit(solution)/shard_map/pallas_call | solution.py:43
  (29 shorter events, 1.9 us)
Async XLA Ops:
  2.6 1.6 %collective-permute-start = (f32[320,128]{1,0:T(8,128)S(1)}, f32[320,128]{1,0:T(8,128)S(1)}, u32[]{:S(2)}, u32[]{:S(2)}) collective-permute-start(f32[320,128]{1,0:T(8,128)S(1)} %get-tuple-element.49), channel_id=1, source_target_pairs={{0,1},{1,0},{2,3},{3,2},{4,5},{5,4},{6,7},{7,6},{8,9},{9,8},{10,11... | collective-permute-start | bytes 491528 | tf_op jit(solution)/shard_map/ppermute | solution.py:313
  3.1 4.9 %copy-start = (f32[1,1,3,256,256]{4,3,2,1,0:T(8,128)S(1)}, f32[1,1,3,256,256]{4,3,2,1,0:T(8,128)}, u32[]{:S(2)}) copy-start(f32[1,1,3,256,256]{4,3,2,1,0:T(8,128)} %param.13) | copy-start | bytes 2359300
  4.2 3.9 %copy-start.1 = (f32[1,1,3,128,128]{4,3,2,1,0:T(8,128)S(1)}, f32[1,1,3,128,128]{4,3,2,1,0:T(8,128)}, u32[]{:S(2)}) copy-start(f32[1,1,3,128,128]{4,3,2,1,0:T(8,128)} %param.14) | copy-start | bytes 589828
  4.2 3.9 %copy-start.2 = (f32[1,1,3,128,128]{4,3,2,1,0:T(8,128)S(1)}, f32[1,1,3,128,128]{4,3,2,1,0:T(8,128)}, u32[]{:S(2)}) copy-start(f32[1,1,3,128,128]{4,3,2,1,0:T(8,128)} %param.15) | copy-start | bytes 589828
  4.4 6.8 %collective-permute-start.1 = (f32[256,128]{1,0:T(8,128)S(1)}, f32[256,128]{1,0:T(8,128)S(1)}, u32[]{:S(2)}, u32[]{:S(2)}) collective-permute-start(f32[256,128]{1,0:T(8,128)S(1)} %get-tuple-element.52.home), channel_id=1, source_target_pairs={{0,2},{1,3},{2,0},{3,1},{4,6},{5,7},{6,4},{7,5},{8,10},{9,11},{10,... | collective-permute-start | bytes 393224 | tf_op jit(solution)/shard_map/ppermute | solution.py:313
  11.4 15.5 %collective-permute-start.7 = (f32[256,128]{1,0:T(8,128)S(1)}, f32[256,128]{1,0:T(8,128)S(1)}, u32[]{:S(2)}, u32[]{:S(2)}) collective-permute-start(f32[256,128]{1,0:T(8,128)S(1)} %get-tuple-element.73.home), channel_id=1, source_target_pairs={{0,4},{1,5},{2,6},{3,7},{4,0},{5,1},{6,2},{7,3},{8,12},{9,13},{10,... | collective-permute-start | bytes 393224 | tf_op jit(solution)/shard_map/ppermute | solution.py:313
  14.2 7.3 %collective-permute-start.2 = (f32[64,128]{1,0:T(8,128)S(1)}, f32[64,128]{1,0:T(8,128)S(1)}, u32[]{:S(2)}, u32[]{:S(2)}) collective-permute-start(f32[64,128]{1,0:T(8,128)S(1)} %get-tuple-element.62.refs_0_), channel_id=1, source_target_pairs={{0,4},{1,5},{2,6},{3,7},{4,0},{5,1},{6,2},{7,3},{8,12},{9,13},{10,... | collective-permute-start | bytes 98312 | tf_op jit(solution)/shard_map/ppermute | solution.py:313
  21.6 4.3 %collective-permute-start.3 = (f32[2,64,128]{2,1,0:T(8,128)S(1)}, f32[2,64,128]{2,1,0:T(8,128)S(1)}, u32[]{:S(2)}, u32[]{:S(2)}) collective-permute-start(f32[2,64,128]{2,1,0:T(8,128)S(1)} %shard_map.120.home), channel_id=1, source_target_pairs={{0,2},{1,3},{2,0},{3,1},{4,6},{5,7},{6,4},{7,5},{8,10},{9,11},{10,... | collective-permute-start | bytes 196616 | tf_op jit(solution)/shard_map/ppermute | solution.py:313
  22.1 8.5 %collective-permute-start.5 = (f32[256,128]{1,0:T(8,128)S(1)}, f32[256,128]{1,0:T(8,128)S(1)}, u32[]{:S(2)}, u32[]{:S(2)}) collective-permute-start(f32[256,128]{1,0:T(8,128)S(1)} %get-tuple-element.71.refs_0_), channel_id=1, source_target_pairs={{0,1},{1,0},{2,3},{3,2},{4,5},{5,4},{6,7},{7,6},{8,9},{9,8},{10,11... | collective-permute-start | bytes 393224 | tf_op jit(solution)/shard_map/ppermute | solution.py:313
  27.1 7.3 %collective-permute-start.14 = (f32[320,128]{1,0:T(8,128)S(1)}, f32[320,128]{1,0:T(8,128)S(1)}, u32[]{:S(2)}, u32[]{:S(2)}) collective-permute-start(f32[320,128]{1,0:T(8,128)S(1)} %get-tuple-element.75.refs_6_), channel_id=1, source_target_pairs={{0,24},{8,16},{16,8},{24,0},{1,25},{9,17},{17,9},{25,1},{2,26},{10... | collective-permute-start | bytes 491528 | tf_op jit(solution)/shard_map/ppermute | solution.py:316
  29.5 6.3 %collective-permute-start.12 = (f32[320,128]{1,0:T(8,128)S(1)}, f32[320,128]{1,0:T(8,128)S(1)}, u32[]{:S(2)}, u32[]{:S(2)}) collective-permute-start(f32[320,128]{1,0:T(8,128)S(1)} %get-tuple-element.75.refs_6_), channel_id=1, source_target_pairs={{0,16},{8,24},{16,0},{24,8},{1,17},{9,25},{17,1},{25,9},{2,18},{10... | collective-permute-start | bytes 491528 | tf_op jit(solution)/shard_map/ppermute | solution.py:316
  30.1 5.8 %collective-permute-start.10 = (f32[320,128]{1,0:T(8,128)S(1)}, f32[320,128]{1,0:T(8,128)S(1)}, u32[]{:S(2)}, u32[]{:S(2)}) collective-permute-start(f32[320,128]{1,0:T(8,128)S(1)} %get-tuple-element.75.refs_6_), channel_id=1, source_target_pairs={{0,8},{8,0},{16,24},{24,16},{1,9},{9,1},{17,25},{25,17},{2,10},{10... | collective-permute-start | bytes 491528 | tf_op jit(solution)/shard_map/ppermute | solution.py:316
  30.7 1.3 %collective-permute-start.4 = (f32[4,64,128]{2,1,0:T(8,128)S(1)}, f32[4,64,128]{2,1,0:T(8,128)S(1)}, u32[]{:S(2)}, u32[]{:S(2)}) collective-permute-start(f32[4,64,128]{2,1,0:T(8,128)S(1)} %shard_map.122.tails.home), channel_id=1, source_target_pairs={{0,1},{1,0},{2,3},{3,2},{4,5},{5,4},{6,7},{7,6},{8,9},{9,8},{10,11... | collective-permute-start | bytes 393224 | tf_op jit(solution)/shard_map/ppermute | solution.py:313
  30.7 5.7 %collective-permute-start.6 = (f32[256,128]{1,0:T(8,128)S(1)}, f32[256,128]{1,0:T(8,128)S(1)}, u32[]{:S(2)}, u32[]{:S(2)}) collective-permute-start(f32[256,128]{1,0:T(8,128)S(1)} %get-tuple-element.72.refs_2_), channel_id=1, source_target_pairs={{0,1},{1,0},{2,3},{3,2},{4,5},{5,4},{6,7},{7,6},{8,9},{9,8},{10,11... | collective-permute-start | bytes 393224 | tf_op jit(solution)/shard_map/ppermute | solution.py:313
  32.0 5.7 %collective-permute-start.9 = (f32[320,128]{1,0:T(8,128)S(1)}, f32[320,128]{1,0:T(8,128)S(1)}, u32[]{:S(2)}, u32[]{:S(2)}) collective-permute-start(f32[320,128]{1,0:T(8,128)S(1)} %get-tuple-element.75.refs_6_), channel_id=1, source_target_pairs={{0,1},{1,0},{2,3},{3,2},{4,5},{5,4},{6,7},{7,6},{8,9},{9,8},{10,11... | collective-permute-start | bytes 491528 | tf_op jit(solution)/shard_map/ppermute | solution.py:313
  34.4 3.4 %collective-permute-start.15 = (f32[320,128]{1,0:T(8,128)S(1)}, f32[320,128]{1,0:T(8,128)S(1)}, u32[]{:S(2)}, u32[]{:S(2)}) collective-permute-start(f32[320,128]{1,0:T(8,128)S(1)} %collective-permute-done.14.refs_12_), channel_id=1, source_target_pairs={{0,1},{1,0},{2,3},{3,2},{4,5},{5,4},{6,7},{7,6},{8,9},{9,8},{10,11... | collective-permute-start | bytes 491528 | tf_op jit(solution)/shard_map/ppermute | solution.py:313
  35.9 2.0 %collective-permute-start.13 = (f32[320,128]{1,0:T(8,128)S(1)}, f32[320,128]{1,0:T(8,128)S(1)}, u32[]{:S(2)}, u32[]{:S(2)}) collective-permute-start(f32[320,128]{1,0:T(8,128)S(1)} %collective-permute-done.12.refs_10_), channel_id=1, source_target_pairs={{0,1},{1,0},{2,3},{3,2},{4,5},{5,4},{6,7},{7,6},{8,9},{9,8},{10,11... | collective-permute-start | bytes 491528 | tf_op jit(solution)/shard_map/ppermute | solution.py:313
  35.9 2.0 %collective-permute-start.11 = (f32[320,128]{1,0:T(8,128)S(1)}, f32[320,128]{1,0:T(8,128)S(1)}, u32[]{:S(2)}, u32[]{:S(2)}) collective-permute-start(f32[320,128]{1,0:T(8,128)S(1)} %collective-permute-done.10.refs_8_), channel_id=1, source_target_pairs={{0,1},{1,0},{2,3},{3,2},{4,5},{5,4},{6,7},{7,6},{8,9},{9,8},{10,11... | collective-permute-start | bytes 491528 | tf_op jit(solution)/shard_map/ppermute | solution.py:313
  36.4 1.3 %collective-permute-start.8 = (f32[256,128]{1,0:T(8,128)S(1)}, f32[256,128]{1,0:T(8,128)S(1)}, u32[]{:S(2)}, u32[]{:S(2)}) collective-permute-start(f32[256,128]{1,0:T(8,128)S(1)} %get-tuple-element.74.refs_4_), channel_id=1, source_target_pairs={{0,1},{1,0},{2,3},{3,2},{4,5},{5,4},{6,7},{7,6},{8,9},{9,8},{10,11... | collective-permute-start | bytes 393224 | tf_op jit(solution)/shard_map/ppermute | solution.py:313

commit v5 on v4

--- a/solution.py
+++ b/solution.py
@@ -36,7 +36,7 @@
     return wide_dot(wide_left(left), wide_right(right))
 
 
-def call(kernel, out_shape, args, flops, in_specs=None, out_specs=None, scratch_shapes=()):
+def call(kernel, out_shape, args, flops, in_specs=None, out_specs=None, scratch_shapes=(), aliases={}):
     size = lambda s: s.size * s.dtype.itemsize
     vmem = pl.BlockSpec(memory_space=pltpu.VMEM)
     moved = sum(size(a) for a in args) + sum(size(o) for o in jax.tree.leaves(out_shape))
@@ -46,6 +46,7 @@
         in_specs=in_specs or [vmem] * len(args),
         out_specs=out_specs or jax.tree.map(lambda _: vmem, out_shape),
         scratch_shapes=scratch_shapes,
+        input_output_aliases=aliases,
         compiler_params=pltpu.CompilerParams(vmem_limit_bytes=VMEM_LIMIT),
         cost_estimate=pl.CostEstimate(flops=flops, bytes_accessed=moved, transcendentals=0),
     )(*args)
@@ -234,23 +235,57 @@
     wide_maps[...] = wide_right(maps[...])
 
 
-def final_kernel(fronts, height, solved, wide_maps, *refs):
+def affected(child, height):
+    position = lax.axis_index("blk")
+    below = lax.axis_index("level") > 0
+    shared = [position >> t == child[0] >> t for t in range(height)]
+    return [jnp.logical_and(below, same) for same in shared] + [below, below]
+
+
+def targets(leaf_out, node_out, root_out, rows):
+    nodes = [node_out.at[tier, rows] for tier in range(node_out.shape[0])]
+    return [leaf_out.at[rows]] + nodes + [root_out.at[rows]]
+
+
+def part_rows(part, half):
+    core = lax.axis_index("blk") & 1
+    return pl.ds(pl.multiple_of((core if part == 0 else 1 - core) * half, 8), half)
+
+
+def early_kernel(height, child, solved, *refs):
+    nodes, roots, refs = refs[: 2 * height], refs[2 * height : 2 * height + 2], refs[-4:]
+    leaf_out, node_out, root_out, sems = refs
+    half, _ = solved.shape[1:]
+    late = affected(child, height)
+    copies = []
+    for part in range(2):
+        outs = targets(leaf_out, node_out, root_out, part_rows(part, half))
+        bases = [solved.at[part]] + [nodes[2 * tier + part] for tier in range(height)]
+        bases += [roots[part].at[pl.ds(0, half)]]
+        copies += [
+            (late[i], pltpu.make_async_copy(base, out, sems.at[part, i]))
+            for i, (base, out) in enumerate(zip(bases, outs))
+        ]
+    for act in ("start", "wait"):
+        for skip, copy in copies:
+            pl.when(jnp.logical_not(skip))(getattr(copy, act))
+
+
+def final_kernel(fronts, height, child, solved, wide_maps, *refs):
     nodes, refs = refs[: 2 * height], refs[2 * height :]
-    roots, refs = refs[: 2 * fronts], refs[2 * fronts :]
+    roots, refs = refs[: 2 * fronts], refs[2 * fronts + 3 :]
     leaf_out, node_out, root_out, root_maps, incoming, result, sems = refs
     core, level = lax.axis_index("blk") & 1, lax.axis_index("level")
     half, size = solved.shape[1:]
     k_half = root_maps.shape[1] // 2
+    count = height + 2
+    late = affected(child, height)
     for front in range(1, fronts):
         root_maps[front, span(core, k_half), :] = roots[2 * front][half:, :]
         root_maps[front, span(1 - core, k_half), :] = roots[2 * front + 1][half:, :]
 
     def both_rows(mask):
         return jnp.concatenate([roots[2 * mask][:half, :], roots[2 * mask + 1][:half, :]], axis=0)
-
-    @pl.when(level == 0)
-    def _():
-        incoming[...] = jnp.zeros_like(incoming)
 
     for here in range(1, fronts):
 
@@ -259,29 +294,42 @@
             value = both_rows(here)
             for front in range(1, here):
                 value = both_rows(here ^ front) + product(value, root_maps[here ^ front])
-            incoming[...] = value
-
+            incoming[...] = wide_left(value)
+
+    step = half // 2
     copies = []
-    step = half // 2
     for chunk in range(4):
-        part, first = chunk // 2, chunk % 2 * step
-        inner = slice(first, first + step)
-        rows = pl.ds(pl.multiple_of((core if part == 0 else 1 - core) * half + first, 8), step)
-        change = wide_dot(wide_left(incoming[chunk * step : (chunk + 1) * step, :]), wide_maps[...])
-        bases = (
-            [solved[part, inner, :]]
-            + [nodes[2 * tier + part][inner, :] for tier in range(height)]
-            + [roots[part][inner, :]]
+        first = (core if chunk < 2 else 1 - core) * half + chunk % 2 * step
+        outs = targets(leaf_out, node_out, root_out, pl.ds(pl.multiple_of(first, 8), step))
+        copies.append(
+            [
+                pltpu.make_async_copy(result.at[chunk, i], out, sems.at[chunk, i])
+                for i, out in enumerate(outs)
+            ]
         )
-        targets = (
-            [leaf_out.at[rows]] + [node_out.at[tier, rows] for tier in range(height)] + [root_out.at[rows]]
-        )
-        for i, (base, target) in enumerate(zip(bases, targets)):
-            result[chunk, i] = base + change[:, i * size : (i + 1) * size]
-            copies.append(pltpu.make_async_copy(result.at[chunk, i], target, sems.at[chunk, i]))
-            copies[-1].start()
-    for copy in copies:
-        copy.wait()
+
+    def update(first, last):
+        for chunk in range(4):
+            part, inner = chunk // 2, slice(chunk % 2 * step, (chunk % 2 + 1) * step)
+            change = wide_dot(
+                incoming[chunk * step : (chunk + 1) * step, :], wide_maps[:, first * size : last * size]
+            )
+            for i in range(first, last):
+                if i == 0:
+                    base = solved[part, inner, :]
+                elif i <= height:
+                    base = nodes[2 * (i - 1) + part][inner, :]
+                else:
+                    base = roots[part][inner, :]
+                result[chunk, i] = base + change[:, (i - first) * size : (i + 1 - first) * size]
+                copies[chunk][i].start()
+
+    pl.when(late[height])(functools.partial(update, height, count))
+    for i in reversed(range(height)):
+        pl.when(late[i])(functools.partial(update, i, i + 1))
+    for i, flag in enumerate(late):
+        for chunk in range(4):
+            pl.when(flag)(copies[chunk][i].wait)
 
 
 def shards(
@@ -462,24 +510,35 @@
     pairs = []
     for value in nodes:
         pairs += [value, blk_swap(value, 1)]
-    after = (*pairs[1::2], roots[1])
+    shapes = (array(rows, size), array(height, rows, size), array(rows, size))
+    early = call(
+        functools.partial(early_kernel, height),
+        shapes,
+        (child_leaf, solved, *pairs, *roots[:2]),
+        rows * size,
+        in_specs=[smem] + [vmem] * (len(pairs) + 3),
+        out_specs=(hbm,) * 3,
+        scratch_shapes=[pltpu.SemaphoreType.DMA((2, height + 2))],
+    )
     wide_maps = call(
         maps_kernel,
         jax.ShapeDtypeStruct((3 * k_rows, size * (height + 2)), bf16),
-        (leaf_map, tails, blk_swap(tails, 1), *after),
+        (leaf_map, tails, blk_swap(tails, 1)),
         k_rows * size * (height + 2) * 4,
-        in_specs=[vmem] * 3 + [anywhere] * len(after),
         scratch_shapes=[pltpu.VMEM((k_rows, size * (height + 2)), f32)],
     )
+    args = (child_leaf, solved, wide_maps, *pairs, *roots)
     leaf_out, node_out, root_out = call(
         functools.partial(final_kernel, fronts, height),
-        (array(rows, size), array(height, rows, size), array(rows, size)),
-        (solved, wide_maps, *pairs, *roots),
+        shapes,
+        (*args, *early),
         6 * rows * size * size * (height + 2),
+        in_specs=[smem] + [vmem] * (len(args) - 1) + [hbm] * 3,
         out_specs=(hbm,) * 3,
+        aliases={len(args) + i: i for i in range(3)},
         scratch_shapes=[
             pltpu.VMEM((fronts, k_rows, size), f32),
-            pltpu.VMEM((rows, size), f32),
+            pltpu.VMEM((rows, 3 * size), bf16),
             pltpu.VMEM((4, height + 2, rows // 4, size), f32),
             pltpu.SemaphoreType.DMA((4, height + 2)),
         ],

time: 39.6 us -> 40.1 us (1.013)
  the two profiles are of different devices: /device:TPU:0 before, /device:TPU:21 now
where the time goes in v5:
time: 40.1 us; the launch traced here: 39.9 us
  starting transfers between devices  20.4 us (51%)
  waiting for transfers between devices  9.68 us (24%)
  Pallas kernels  8.42 us (21%)
  between operations  1.45 us (4%)
    ppermute x13, starting transfers between devices, blk_swap(): return lax.ppermute(value, 'blk', [(i, i ^ mask) for i in range(leaves)])  17.7 us
    pallas_call x16, Pallas kernels, call(): pl.pallas_call(kernel, out_shape=out_shape, in_specs=in_specs or [vmem] *...  8.42 us
    ppermute x13, waiting for transfers between devices, blk_swap(): return lax.ppermute(value, 'blk', [(i, i ^ mask) for i in range(leaves)])  8.21 us
    ppermute x3, starting transfers between devices, level_swap(): return lax.ppermute(value, 'level', [(i, i ^ mask) for i in range(fronts)])  2.71 us
    ppermute x3, waiting for transfers between devices, level_swap(): return lax.ppermute(value, 'level', [(i, i ^ mask) for i in range(fronts)])  1.47 us
  transfers between devices with their start and end apart: 16, of which 7 were waited for; matrix products, arithmetic and copies ran while one was open for 0% of the time, Pallas kernels for 11%

profile of v5, /device:TPU:21, one launch (start us, length us, event | category | flops | bytes accessed | tf_op | source)
XLA Modules:
  0.0 39.9 jit_solution(10112001429637531430)
XLA Ops:
  0.6 1.9 %shard_map.112 = (f32[320,128]{1,0:T(8,128)S(1)}, f32[256,128]{1,0:T(8,128)S(1)}, bf16[768,128]{1,0:T(8,128)(2,1)S(1)}, f32[2,256,256]{2,1,0:T(8,128)S(1)}, f32[...) custom-call(f32[512,256]{1,0:T(8,128)} %bitcast.23, ...), custom_call_target="tpu_custom_call" | custom-call | flops 113246208 | bytes 3768320 | tf_op jit(solution)/shard_map/pallas_call | solution.py:43
  2.6 0.7 %collective-permute-start = (f32[320,128]{1,0:T(8,128)S(1)}, f32[320,128]{1,0:T(8,128)S(1)}, u32[]{:S(2)}, u32[]{:S(2)}) collective-permute-start(f32[320,128]{1,0:T(8,128)S(1)} %get-tuple-element.52), channel_id=1, source_target_pairs={{0,1},{1,0},{2,3},{3,2},{4,5},{5,4},{6,7},{7,6},{8,9},{9,8},{10,11... | collective-permute-start | bytes 491528 | tf_op jit(solution)/shard_map/ppermute | solution.py:361
  3.3 0.8 %shard_map.113 = (bf16[1,384,256]{2,1,0:T(8,128)(2,1)S(1)}, bf16[1,384,256]{2,1,0:T(8,128)(2,1)S(1)}, f32[256,256]{1,0:T(8,128)S(1)}, f32[64,128]{1,0:T(8,128)S(1)}) custom-call(f32[256,256]{1,0:T(8,128)S(1)} %get-tuple-element.44.generator, f32[128,128]{1,0:T(8,128)S(1)} %get-tuple-element.45.inverse, f32[128,128]{1,0:T(8,128)S(1)} %get-tuple-element.46.lower, ...), custom_call_target="tpu_custom_call" | custom-call | flops 176160768 | bytes 1933312 | tf_op jit(solution)/shard_map/pallas_call | solution.py:43
  4.6 1.4 %collective-permute-start.1 = (f32[256,128]{1,0:T(8,128)S(1)}, f32[256,128]{1,0:T(8,128)S(1)}, u32[]{:S(2)}, u32[]{:S(2)}) collective-permute-start(f32[256,128]{1,0:T(8,128)S(1)} %get-tuple-element.56.home), channel_id=1, source_target_pairs={{0,2},{1,3},{2,0},{3,1},{4,6},{5,7},{6,4},{7,5},{8,10},{9,11},{10,... | collective-permute-start | bytes 393224 | tf_op jit(solution)/shard_map/ppermute | solution.py:361
  6.6 0.4 shard_map.115
  7.6 1.8 %collective-permute-done.1.away = f32[256,128]{1,0:T(8,128)S(1)} collective-permute-done((f32[256,128]{1,0:T(8,128)S(1)}, f32[256,128]{1,0:T(8,128)S(1)}, u32[]{:S(2)}, u32[]{:S(2)}) %collective-permute-start.1) | collective-permute-done | bytes 131104 | tf_op jit(solution)/shard_map/ppermute | solution.py:361
  9.7 2.3 %collective-permute-start.2 = (f32[64,128]{1,0:T(8,128)S(1)}, f32[64,128]{1,0:T(8,128)S(1)}, u32[]{:S(2)}, u32[]{:S(2)}) collective-permute-start(f32[64,128]{1,0:T(8,128)S(1)} %get-tuple-element.65.refs_0_), channel_id=1, source_target_pairs={{0,4},{1,5},{2,6},{3,7},{4,0},{5,1},{6,2},{7,3},{8,12},{9,13},{10,... | collective-permute-start | bytes 98312 | tf_op jit(solution)/shard_map/ppermute | solution.py:361
  12.0 3.4 %collective-permute-done.2.far = f32[64,128]{1,0:T(8,128)S(1)} collective-permute-done((f32[64,128]{1,0:T(8,128)S(1)}, f32[64,128]{1,0:T(8,128)S(1)}, u32[]{:S(2)}, u32[]{:S(2)}) %collective-permute-start.2) | collective-permute-done | bytes 32800 | tf_op jit(solution)/shard_map/ppermute | solution.py:361
  15.4 5.9 %collective-permute-start.3 = (f32[2,64,128]{2,1,0:T(8,128)S(1)}, f32[2,64,128]{2,1,0:T(8,128)S(1)}, u32[]{:S(2)}, u32[]{:S(2)}) collective-permute-start(f32[2,64,128]{2,1,0:T(8,128)S(1)} %shard_map.120.home), channel_id=1, source_target_pairs={{0,2},{1,3},{2,0},{3,1},{4,6},{5,7},{6,4},{7,5},{8,10},{9,11},{10,... | collective-permute-start | bytes 196616 | tf_op jit(solution)/shard_map/ppermute | solution.py:361
  21.4 0.8 %collective-permute-start.5 = (f32[256,128]{1,0:T(8,128)S(1)}, f32[256,128]{1,0:T(8,128)S(1)}, u32[]{:S(2)}, u32[]{:S(2)}) collective-permute-start(f32[256,128]{1,0:T(8,128)S(1)} %get-tuple-element.74.refs_0_), channel_id=1, source_target_pairs={{0,1},{1,0},{2,3},{3,2},{4,5},{5,4},{6,7},{7,6},{8,9},{9,8},{10,11... | collective-permute-start | bytes 393224 | tf_op jit(solution)/shard_map/ppermute | solution.py:361
  22.1 0.4 shard_map.121
  22.5 0.8 %collective-permute-done.3.away = f32[2,64,128]{2,1,0:T(8,128)S(1)} collective-permute-done((f32[2,64,128]{2,1,0:T(8,128)S(1)}, f32[2,64,128]{2,1,0:T(8,128)S(1)}, u32[]{:S(2)}, u32[]{:S(2)}) %collective-permute-start.3) | collective-permute-done | bytes 65568 | tf_op jit(solution)/shard_map/ppermute | solution.py:361
  23.9 0.4 %shard_map.119 = (f32[2,256,128]{2,1,0:T(8,128)S(1)}, f32[128,128]{1,0:T(8,128)S(1)}) custom-call(f32[2,256,128]{2,1,0:T(8,128)S(1)} %get-tuple-element.66.solved_early, f32[128,128]{1,0:T(8,128)S(1)} %get-tuple-element.67.map_early, s32[1]{0:T(128)S(6)} %copy.18.child.refs_0_, f32[2,256,256]{2,1,0:T(8,128)S(1)} %get-tuple-element.47.right.refs_1_, ...), custom_call_target="tpu_custom_call" | custom-call | flops 125829120 | bytes 1441796 | tf_op jit(solution)/shard_map/pallas_call | solution.py:43
  24.6 1.2 %collective-permute-start.14 = (f32[320,128]{1,0:T(8,128)S(1)}, f32[320,128]{1,0:T(8,128)S(1)}, u32[]{:S(2)}, u32[]{:S(2)}) collective-permute-start(f32[320,128]{1,0:T(8,128)S(1)} %get-tuple-element.78.refs_6_), channel_id=1, source_target_pairs={{0,24},{8,16},{16,8},{24,0},{1,25},{9,17},{17,9},{25,1},{2,26},{10... | collective-permute-start | bytes 491528 | tf_op jit(solution)/shard_map/ppermute | solution.py:364
  25.8 1.2 %collective-permute-start.12 = (f32[320,128]{1,0:T(8,128)S(1)}, f32[320,128]{1,0:T(8,128)S(1)}, u32[]{:S(2)}, u32[]{:S(2)}) collective-permute-start(f32[320,128]{1,0:T(8,128)S(1)} %get-tuple-element.78.refs_6_), channel_id=1, source_target_pairs={{0,16},{8,24},{16,0},{24,8},{1,17},{9,25},{17,1},{25,9},{2,18},{10... | collective-permute-start | bytes 491528 | tf_op jit(solution)/shard_map/ppermute | solution.py:364
  27.3 1.9 %collective-permute-start.4 = (f32[4,64,128]{2,1,0:T(8,128)S(1)}, f32[4,64,128]{2,1,0:T(8,128)S(1)}, u32[]{:S(2)}, u32[]{:S(2)}) collective-permute-start(f32[4,64,128]{2,1,0:T(8,128)S(1)} %shard_map.122.home.tails), channel_id=1, source_target_pairs={{0,1},{1,0},{2,3},{3,2},{4,5},{5,4},{6,7},{7,6},{8,9},{9,8},{10,11... | collective-permute-start | bytes 393224 | tf_op jit(solution)/shard_map/ppermute | solution.py:361
  29.2 1.0 %collective-permute-done.4.away = f32[4,64,128]{2,1,0:T(8,128)S(1)} collective-permute-done((f32[4,64,128]{2,1,0:T(8,128)S(1)}, f32[4,64,128]{2,1,0:T(8,128)S(1)}, u32[]{:S(2)}, u32[]{:S(2)}) %collective-permute-start.4) | collective-permute-done | bytes 131104 | tf_op jit(solution)/shard_map/ppermute | solution.py:361
  30.6 3.2 %collective-permute-start.15 = (f32[320,128]{1,0:T(8,128)S(1)}, f32[320,128]{1,0:T(8,128)S(1)}, u32[]{:S(2)}, u32[]{:S(2)}) collective-permute-start(f32[320,128]{1,0:T(8,128)S(1)} %collective-permute-done.14.refs_12_), channel_id=1, source_target_pairs={{0,1},{1,0},{2,3},{3,2},{4,5},{5,4},{6,7},{7,6},{8,9},{9,8},{10,11... | collective-permute-start | bytes 491528 | tf_op jit(solution)/shard_map/ppermute | solution.py:361
  33.7 1.5 %collective-permute-done.12.refs_10_ = f32[320,128]{1,0:T(8,128)S(1)} collective-permute-done((f32[320,128]{1,0:T(8,128)S(1)}, f32[320,128]{1,0:T(8,128)S(1)}, u32[]{:S(2)}, u32[]{:S(2)}) %collective-permute-start.12) | collective-permute-done | bytes 163872 | tf_op jit(solution)/shard_map/ppermute | solution.py:364
  35.2 0.5 %collective-permute-start.13 = (f32[320,128]{1,0:T(8,128)S(1)}, f32[320,128]{1,0:T(8,128)S(1)}, u32[]{:S(2)}, u32[]{:S(2)}) collective-permute-start(f32[320,128]{1,0:T(8,128)S(1)} %collective-permute-done.12.refs_10_), channel_id=1, source_target_pairs={{0,1},{1,0},{2,3},{3,2},{4,5},{5,4},{6,7},{7,6},{8,9},{9,8},{10,11... | collective-permute-start | bytes 491528 | tf_op jit(solution)/shard_map/ppermute | solution.py:361
  35.7 0.5 %collective-permute-start.8 = (f32[256,128]{1,0:T(8,128)S(1)}, f32[256,128]{1,0:T(8,128)S(1)}, u32[]{:S(2)}, u32[]{:S(2)}) collective-permute-start(f32[256,128]{1,0:T(8,128)S(1)} %get-tuple-element.77.refs_4_), channel_id=1, source_target_pairs={{0,1},{1,0},{2,3},{3,2},{4,5},{5,4},{6,7},{7,6},{8,9},{9,8},{10,11... | collective-permute-start | bytes 393224 | tf_op jit(solution)/shard_map/ppermute | solution.py:361
  36.3 1.0 %collective-permute-done.8.refs_5_ = f32[256,128]{1,0:T(8,128)S(1)} collective-permute-done((f32[256,128]{1,0:T(8,128)S(1)}, f32[256,128]{1,0:T(8,128)S(1)}, u32[]{:S(2)}, u32[]{:S(2)}) %collective-permute-start.8) | collective-permute-done | bytes 131104 | tf_op jit(solution)/shard_map/ppermute | solution.py:361
  37.3 0.9 %shard_map.126 = (f32[512,128]{1,0:T(8,128)}, f32[3,512,128]{2,1,0:T(8,128)}, f32[512,128]{1,0:T(8,128)}) custom-call(s32[1]{0:T(128)S(6)} %copy.18.child.refs_0_, f32[2,256,128]{2,1,0:T(8,128)S(1)} %get-tuple-element.68.refs_0_.solved, f32[256,128]{1,0:T(8,128)S(1)} %get-tuple-element.74.refs_0_, f32[256,128]{1,0:T(8,128)S(1)} %collective-permute-done.5.refs_1_, ...), custom_call_target="tpu_custom_call" | custom-call | flops 65536 | bytes 2686980 | tf_op jit(solution)/shard_map/pallas_call | solution.py:43
  38.2 1.7 %shard_map.127 = (f32[512,128]{1,0:T(8,128)}, f32[3,512,128]{2,1,0:T(8,128)}, f32[512,128]{1,0:T(8,128)}) custom-call(s32[1]{0:T(128)S(6)} %copy.18.child.refs_0_, f32[2,256,128]{2,1,0:T(8,128)S(1)} %get-tuple-element.68.refs_0_.solved, bf16[384,640]{1,0:T(8,128)(2,1)S(1)} %shard_map.123.wide_maps, ...), custom_call_target="tpu_custom_call", output_to_operand_aliasing={{0}: (17, {}), {1}: (18, {}), {2}: (19, {})} | custom-call | flops 251658240 | bytes 5472260 | tf_op jit(solution)/shard_map/pallas_call | solution.py:43
  (30 shorter events, 3.0 us)
Async XLA Ops:
  2.6 1.8 %collective-permute-start = (f32[320,128]{1,0:T(8,128)S(1)}, f32[320,128]{1,0:T(8,128)S(1)}, u32[]{:S(2)}, u32[]{:S(2)}) collective-permute-start(f32[320,128]{1,0:T(8,128)S(1)} %get-tuple-element.52), channel_id=1, source_target_pairs={{0,1},{1,0},{2,3},{3,2},{4,5},{5,4},{6,7},{7,6},{8,9},{9,8},{10,11... | collective-permute-start | bytes 491528 | tf_op jit(solution)/shard_map/ppermute | solution.py:361
  3.3 3.3 %copy-start = (f32[1,1,3,256,256]{4,3,2,1,0:T(8,128)S(1)}, f32[1,1,3,256,256]{4,3,2,1,0:T(8,128)}, u32[]{:S(2)}) copy-start(f32[1,1,3,256,256]{4,3,2,1,0:T(8,128)} %param.13) | copy-start | bytes 2359300
  4.4 2.3 %copy-start.1 = (f32[1,1,3,128,128]{4,3,2,1,0:T(8,128)S(1)}, f32[1,1,3,128,128]{4,3,2,1,0:T(8,128)}, u32[]{:S(2)}) copy-start(f32[1,1,3,128,128]{4,3,2,1,0:T(8,128)} %param.14) | copy-start | bytes 589828
  4.4 2.3 %copy-start.2 = (f32[1,1,3,128,128]{4,3,2,1,0:T(8,128)S(1)}, f32[1,1,3,128,128]{4,3,2,1,0:T(8,128)}, u32[]{:S(2)}) copy-start(f32[1,1,3,128,128]{4,3,2,1,0:T(8,128)} %param.15) | copy-start | bytes 589828
  4.6 4.7 %collective-permute-start.1 = (f32[256,128]{1,0:T(8,128)S(1)}, f32[256,128]{1,0:T(8,128)S(1)}, u32[]{:S(2)}, u32[]{:S(2)}) collective-permute-start(f32[256,128]{1,0:T(8,128)S(1)} %get-tuple-element.56.home), channel_id=1, source_target_pairs={{0,2},{1,3},{2,0},{3,1},{4,6},{5,7},{6,4},{7,5},{8,10},{9,11},{10,... | collective-permute-start | bytes 393224 | tf_op jit(solution)/shard_map/ppermute | solution.py:361
  9.6 14.8 %collective-permute-start.7 = (f32[256,128]{1,0:T(8,128)S(1)}, f32[256,128]{1,0:T(8,128)S(1)}, u32[]{:S(2)}, u32[]{:S(2)}) collective-permute-start(f32[256,128]{1,0:T(8,128)S(1)} %get-tuple-element.76.home), channel_id=1, source_target_pairs={{0,4},{1,5},{2,6},{3,7},{4,0},{5,1},{6,2},{7,3},{8,12},{9,13},{10,... | collective-permute-start | bytes 393224 | tf_op jit(solution)/shard_map/ppermute | solution.py:361
  9.7 5.7 %collective-permute-start.2 = (f32[64,128]{1,0:T(8,128)S(1)}, f32[64,128]{1,0:T(8,128)S(1)}, u32[]{:S(2)}, u32[]{:S(2)}) collective-permute-start(f32[64,128]{1,0:T(8,128)S(1)} %get-tuple-element.65.refs_0_), channel_id=1, source_target_pairs={{0,4},{1,5},{2,6},{3,7},{4,0},{5,1},{6,2},{7,3},{8,12},{9,13},{10,... | collective-permute-start | bytes 98312 | tf_op jit(solution)/shard_map/ppermute | solution.py:361
  15.4 7.9 %collective-permute-start.3 = (f32[2,64,128]{2,1,0:T(8,128)S(1)}, f32[2,64,128]{2,1,0:T(8,128)S(1)}, u32[]{:S(2)}, u32[]{:S(2)}) collective-permute-start(f32[2,64,128]{2,1,0:T(8,128)S(1)} %shard_map.120.home), channel_id=1, source_target_pairs={{0,2},{1,3},{2,0},{3,1},{4,6},{5,7},{6,4},{7,5},{8,10},{9,11},{10,... | collective-permute-start | bytes 196616 | tf_op jit(solution)/shard_map/ppermute | solution.py:361
  21.4 7.9 %collective-permute-start.5 = (f32[256,128]{1,0:T(8,128)S(1)}, f32[256,128]{1,0:T(8,128)S(1)}, u32[]{:S(2)}, u32[]{:S(2)}) collective-permute-start(f32[256,128]{1,0:T(8,128)S(1)} %get-tuple-element.74.refs_0_), channel_id=1, source_target_pairs={{0,1},{1,0},{2,3},{3,2},{4,5},{5,4},{6,7},{7,6},{8,9},{9,8},{10,11... | collective-permute-start | bytes 393224 | tf_op jit(solution)/shard_map/ppermute | solution.py:361
  24.6 6.0 %collective-permute-start.14 = (f32[320,128]{1,0:T(8,128)S(1)}, f32[320,128]{1,0:T(8,128)S(1)}, u32[]{:S(2)}, u32[]{:S(2)}) collective-permute-start(f32[320,128]{1,0:T(8,128)S(1)} %get-tuple-element.78.refs_6_), channel_id=1, source_target_pairs={{0,24},{8,16},{16,8},{24,0},{1,25},{9,17},{17,9},{25,1},{2,26},{10... | collective-permute-start | bytes 491528 | tf_op jit(solution)/shard_map/ppermute | solution.py:364
  25.8 9.4 %collective-permute-start.12 = (f32[320,128]{1,0:T(8,128)S(1)}, f32[320,128]{1,0:T(8,128)S(1)}, u32[]{:S(2)}, u32[]{:S(2)}) collective-permute-start(f32[320,128]{1,0:T(8,128)S(1)} %get-tuple-element.78.refs_6_), channel_id=1, source_target_pairs={{0,16},{8,24},{16,0},{24,8},{1,17},{9,25},{17,1},{25,9},{2,18},{10... | collective-permute-start | bytes 491528 | tf_op jit(solution)/shard_map/ppermute | solution.py:364
  27.1 8.6 %collective-permute-start.10 = (f32[320,128]{1,0:T(8,128)S(1)}, f32[320,128]{1,0:T(8,128)S(1)}, u32[]{:S(2)}, u32[]{:S(2)}) collective-permute-start(f32[320,128]{1,0:T(8,128)S(1)} %get-tuple-element.78.refs_6_), channel_id=1, source_target_pairs={{0,8},{8,0},{16,24},{24,16},{1,9},{9,1},{17,25},{25,17},{2,10},{10... | collective-permute-start | bytes 491528 | tf_op jit(solution)/shard_map/ppermute | solution.py:364
  27.3 2.9 %collective-permute-start.4 = (f32[4,64,128]{2,1,0:T(8,128)S(1)}, f32[4,64,128]{2,1,0:T(8,128)S(1)}, u32[]{:S(2)}, u32[]{:S(2)}) collective-permute-start(f32[4,64,128]{2,1,0:T(8,128)S(1)} %shard_map.122.home.tails), channel_id=1, source_target_pairs={{0,1},{1,0},{2,3},{3,2},{4,5},{5,4},{6,7},{7,6},{8,9},{9,8},{10,11... | collective-permute-start | bytes 393224 | tf_op jit(solution)/shard_map/ppermute | solution.py:361
  29.2 6.5 %collective-permute-start.6 = (f32[256,128]{1,0:T(8,128)S(1)}, f32[256,128]{1,0:T(8,128)S(1)}, u32[]{:S(2)}, u32[]{:S(2)}) collective-permute-start(f32[256,128]{1,0:T(8,128)S(1)} %get-tuple-element.75.refs_2_), channel_id=1, source_target_pairs={{0,1},{1,0},{2,3},{3,2},{4,5},{5,4},{6,7},{7,6},{8,9},{9,8},{10,11... | collective-permute-start | bytes 393224 | tf_op jit(solution)/shard_map/ppermute | solution.py:361
  30.2 7.1 %collective-permute-start.9 = (f32[320,128]{1,0:T(8,128)S(1)}, f32[320,128]{1,0:T(8,128)S(1)}, u32[]{:S(2)}, u32[]{:S(2)}) collective-permute-start(f32[320,128]{1,0:T(8,128)S(1)} %get-tuple-element.78.refs_6_), channel_id=1, source_target_pairs={{0,1},{1,0},{2,3},{3,2},{4,5},{5,4},{6,7},{7,6},{8,9},{9,8},{10,11... | collective-permute-start | bytes 491528 | tf_op jit(solution)/shard_map/ppermute | solution.py:361
  30.6 7.6 %collective-permute-start.15 = (f32[320,128]{1,0:T(8,128)S(1)}, f32[320,128]{1,0:T(8,128)S(1)}, u32[]{:S(2)}, u32[]{:S(2)}) collective-permute-start(f32[320,128]{1,0:T(8,128)S(1)} %collective-permute-done.14.refs_12_), channel_id=1, source_target_pairs={{0,1},{1,0},{2,3},{3,2},{4,5},{5,4},{6,7},{7,6},{8,9},{9,8},{10,11... | collective-permute-start | bytes 491528 | tf_op jit(solution)/shard_map/ppermute | solution.py:361
  35.2 3.0 %collective-permute-start.13 = (f32[320,128]{1,0:T(8,128)S(1)}, f32[320,128]{1,0:T(8,128)S(1)}, u32[]{:S(2)}, u32[]{:S(2)}) collective-permute-start(f32[320,128]{1,0:T(8,128)S(1)} %collective-permute-done.12.refs_10_), channel_id=1, source_target_pairs={{0,1},{1,0},{2,3},{3,2},{4,5},{5,4},{6,7},{7,6},{8,9},{9,8},{10,11... | collective-permute-start | bytes 491528 | tf_op jit(solution)/shard_map/ppermute | solution.py:361
  35.7 2.5 %collective-permute-start.11 = (f32[320,128]{1,0:T(8,128)S(1)}, f32[320,128]{1,0:T(8,128)S(1)}, u32[]{:S(2)}, u32[]{:S(2)}) collective-permute-start(f32[320,128]{1,0:T(8,128)S(1)} %collective-permute-done.10.refs_8_), channel_id=1, source_target_pairs={{0,1},{1,0},{2,3},{3,2},{4,5},{5,4},{6,7},{7,6},{8,9},{9,8},{10,11... | collective-permute-start | bytes 491528 | tf_op jit(solution)/shard_map/ppermute | solution.py:361
  35.7 1.6 %collective-permute-start.8 = (f32[256,128]{1,0:T(8,128)S(1)}, f32[256,128]{1,0:T(8,128)S(1)}, u32[]{:S(2)}, u32[]{:S(2)}) collective-permute-start(f32[256,128]{1,0:T(8,128)S(1)} %get-tuple-element.77.refs_4_), channel_id=1, source_target_pairs={{0,1},{1,0},{2,3},{3,2},{4,5},{5,4},{6,7},{7,6},{8,9},{9,8},{10,11... | collective-permute-start | bytes 393224 | tf_op jit(solution)/shard_map/ppermute | solution.py:361

commit v6 on v5

--- a/solution.py
+++ b/solution.py
@@ -324,9 +324,9 @@
                 result[chunk, i] = base + change[:, (i - first) * size : (i + 1 - first) * size]
                 copies[chunk][i].start()
 
-    pl.when(late[height])(functools.partial(update, height, count))
-    for i in reversed(range(height)):
-        pl.when(late[i])(functools.partial(update, i, i + 1))
+    for i in range(height + 1):
+        first = jnp.logical_and(late[i], jnp.logical_not(late[i - 1])) if i else late[0]
+        pl.when(first)(functools.partial(update, i, count))
     for i, flag in enumerate(late):
         for chunk in range(4):
             pl.when(flag)(copies[chunk][i].wait)
@@ -503,7 +503,9 @@
             kernel, shapes, args + after, merge_flops, in_specs=specs + [anywhere] * len(after)
         )
         nodes.append(node)
-    received = [level_swap(skeleton, mask) for mask in range(1, fronts)]
+    received = []
+    for mask in range(1, fronts):
+        received.append(level_swap(skeleton, mask))
     roots = [skeleton, blk_swap(skeleton, 1)]
     for value in received:
         roots += [value, blk_swap(value, 1)]

time: 40.1 us -> 40 us (level)
  the two profiles are of different devices: /device:TPU:21 before, /device:TPU:0 now
where the time goes in v6:
time: 40 us; the launch traced here: 39.2 us
  waiting for transfers between devices  18.7 us (47%)
  starting transfers between devices  11.9 us (30%)
  Pallas kernels  7.17 us (18%)
  between operations  1.45 us (4%)
    ppermute x13, waiting for transfers between devices, blk_swap(): return lax.ppermute(value, 'blk', [(i, i ^ mask) for i in range(leaves)])  15 us
    ppermute x13, starting transfers between devices, blk_swap(): return lax.ppermute(value, 'blk', [(i, i ^ mask) for i in range(leaves)])  8.34 us
    pallas_call x16, Pallas kernels, call(): pl.pallas_call(kernel, out_shape=out_shape, in_specs=in_specs or [vmem] *...  7.17 us
    ppermute x3, waiting for transfers between devices, level_swap(): return lax.ppermute(value, 'level', [(i, i ^ mask) for i in range(fronts)])  3.71 us
    ppermute x3, starting transfers between devices, level_swap(): return lax.ppermute(value, 'level', [(i, i ^ mask) for i in range(fronts)])  3.55 us
  transfers between devices with their start and end apart: 16, of which 8 were waited for; matrix products, arithmetic and copies ran while one was open for 0% of the time, Pallas kernels for 12%

profile of v6, /device:TPU:0, one launch (start us, length us, event | category | flops | bytes accessed | tf_op | source)
XLA Modules:
  0.0 39.2 jit_solution(4655905499684794319)
XLA Ops:
  0.6 1.9 %shard_map.112 = (f32[320,128]{1,0:T(8,128)S(1)}, f32[256,128]{1,0:T(8,128)S(1)}, bf16[768,128]{1,0:T(8,128)(2,1)S(1)}, f32[2,256,256]{2,1,0:T(8,128)S(1)}, f32[...) custom-call(f32[512,256]{1,0:T(8,128)} %bitcast.23, ...), custom_call_target="tpu_custom_call" | custom-call | flops 113246208 | bytes 3768320 | tf_op jit(solution)/shard_map/pallas_call | solution.py:43
  2.6 0.6 %collective-permute-start = (f32[320,128]{1,0:T(8,128)S(1)}, f32[320,128]{1,0:T(8,128)S(1)}, u32[]{:S(2)}, u32[]{:S(2)}) collective-permute-start(f32[320,128]{1,0:T(8,128)S(1)} %get-tuple-element.52), channel_id=1, source_target_pairs={{0,1},{1,0},{2,3},{3,2},{4,5},{5,4},{6,7},{7,6},{8,9},{9,8},{10,11... | collective-permute-start | bytes 491528 | tf_op jit(solution)/shard_map/ppermute | solution.py:361
  3.1 0.8 %shard_map.113 = (bf16[1,384,256]{2,1,0:T(8,128)(2,1)S(1)}, bf16[1,384,256]{2,1,0:T(8,128)(2,1)S(1)}, f32[256,256]{1,0:T(8,128)S(1)}, f32[64,128]{1,0:T(8,128)S(1)}) custom-call(f32[256,256]{1,0:T(8,128)S(1)} %get-tuple-element.44.generator, f32[128,128]{1,0:T(8,128)S(1)} %get-tuple-element.45.inverse, f32[128,128]{1,0:T(8,128)S(1)} %get-tuple-element.46.lower, ...), custom_call_target="tpu_custom_call" | custom-call | flops 176160768 | bytes 1933312 | tf_op jit(solution)/shard_map/pallas_call | solution.py:43
  4.4 3.0 %collective-permute-start.1 = (f32[256,128]{1,0:T(8,128)S(1)}, f32[256,128]{1,0:T(8,128)S(1)}, u32[]{:S(2)}, u32[]{:S(2)}) collective-permute-start(f32[256,128]{1,0:T(8,128)S(1)} %get-tuple-element.56.home), channel_id=1, source_target_pairs={{0,2},{1,3},{2,0},{3,1},{4,6},{5,7},{6,4},{7,5},{8,10},{9,11},{10,... | collective-permute-start | bytes 393224 | tf_op jit(solution)/shard_map/ppermute | solution.py:361
  8.1 0.4 shard_map.115
  8.5 0.3 shard_map.117
  9.0 2.2 %collective-permute-done.1.away = f32[256,128]{1,0:T(8,128)S(1)} collective-permute-done((f32[256,128]{1,0:T(8,128)S(1)}, f32[256,128]{1,0:T(8,128)S(1)}, u32[]{:S(2)}, u32[]{:S(2)}) %collective-permute-start.1) | collective-permute-done | bytes 131104 | tf_op jit(solution)/shard_map/ppermute | solution.py:361
  11.4 2.8 %collective-permute-start.7 = (f32[256,128]{1,0:T(8,128)S(1)}, f32[256,128]{1,0:T(8,128)S(1)}, u32[]{:S(2)}, u32[]{:S(2)}) collective-permute-start(f32[256,128]{1,0:T(8,128)S(1)} %get-tuple-element.76.home), channel_id=1, source_target_pairs={{0,4},{1,5},{2,6},{3,7},{4,0},{5,1},{6,2},{7,3},{8,12},{9,13},{10,... | collective-permute-start | bytes 393224 | tf_op jit(solution)/shard_map/ppermute | solution.py:361
  14.4 7.2 %collective-permute-done.2.far = f32[64,128]{1,0:T(8,128)S(1)} collective-permute-done((f32[64,128]{1,0:T(8,128)S(1)}, f32[64,128]{1,0:T(8,128)S(1)}, u32[]{:S(2)}, u32[]{:S(2)}) %collective-permute-start.2) | collective-permute-done | bytes 32800 | tf_op jit(solution)/shard_map/ppermute | solution.py:361
  21.6 0.5 %collective-permute-start.3 = (f32[2,64,128]{2,1,0:T(8,128)S(1)}, f32[2,64,128]{2,1,0:T(8,128)S(1)}, u32[]{:S(2)}, u32[]{:S(2)}) collective-permute-start(f32[2,64,128]{2,1,0:T(8,128)S(1)} %shard_map.120.home), channel_id=1, source_target_pairs={{0,2},{1,3},{2,0},{3,1},{4,6},{5,7},{6,4},{7,5},{8,10},{9,11},{10,... | collective-permute-start | bytes 196616 | tf_op jit(solution)/shard_map/ppermute | solution.py:361
  22.1 0.4 shard_map.121
  22.5 3.3 %collective-permute-done.3.away = f32[2,64,128]{2,1,0:T(8,128)S(1)} collective-permute-done((f32[2,64,128]{2,1,0:T(8,128)S(1)}, f32[2,64,128]{2,1,0:T(8,128)S(1)}, u32[]{:S(2)}, u32[]{:S(2)}) %collective-permute-start.3) | collective-permute-done | bytes 65568 | tf_op jit(solution)/shard_map/ppermute | solution.py:361
  25.9 0.4 shard_map.122.home.tails
  26.5 0.4 %shard_map.119 = (f32[2,256,128]{2,1,0:T(8,128)S(1)}, f32[128,128]{1,0:T(8,128)S(1)}) custom-call(f32[2,256,128]{2,1,0:T(8,128)S(1)} %get-tuple-element.66.solved_early, f32[128,128]{1,0:T(8,128)S(1)} %get-tuple-element.67.map_early, s32[1]{0:T(128)S(6)} %copy.18.child.refs_0_, f32[2,256,256]{2,1,0:T(8,128)S(1)} %get-tuple-element.47.right.refs_1_, ...), custom_call_target="tpu_custom_call" | custom-call | flops 125829120 | bytes 1441796 | tf_op jit(solution)/shard_map/pallas_call | solution.py:43
  27.1 2.4 %collective-permute-start.14 = (f32[320,128]{1,0:T(8,128)S(1)}, f32[320,128]{1,0:T(8,128)S(1)}, u32[]{:S(2)}, u32[]{:S(2)}) collective-permute-start(f32[320,128]{1,0:T(8,128)S(1)} %get-tuple-element.78.refs_6_), channel_id=1, source_target_pairs={{0,24},{8,16},{16,8},{24,0},{1,25},{9,17},{17,9},{25,1},{2,26},{10... | collective-permute-start | bytes 491528 | tf_op jit(solution)/shard_map/ppermute | solution.py:364
  29.5 0.5 %collective-permute-start.12 = (f32[320,128]{1,0:T(8,128)S(1)}, f32[320,128]{1,0:T(8,128)S(1)}, u32[]{:S(2)}, u32[]{:S(2)}) collective-permute-start(f32[320,128]{1,0:T(8,128)S(1)} %get-tuple-element.78.refs_6_), channel_id=1, source_target_pairs={{0,16},{8,24},{16,0},{24,8},{1,17},{9,25},{17,1},{25,9},{2,18},{10... | collective-permute-start | bytes 491528 | tf_op jit(solution)/shard_map/ppermute | solution.py:364
  30.1 0.6 %collective-permute-start.10 = (f32[320,128]{1,0:T(8,128)S(1)}, f32[320,128]{1,0:T(8,128)S(1)}, u32[]{:S(2)}, u32[]{:S(2)}) collective-permute-start(f32[320,128]{1,0:T(8,128)S(1)} %get-tuple-element.78.refs_6_), channel_id=1, source_target_pairs={{0,8},{8,0},{16,24},{24,16},{1,9},{9,1},{17,25},{25,17},{2,10},{10... | collective-permute-start | bytes 491528 | tf_op jit(solution)/shard_map/ppermute | solution.py:364
  30.7 0.5 %collective-permute-start.6 = (f32[256,128]{1,0:T(8,128)S(1)}, f32[256,128]{1,0:T(8,128)S(1)}, u32[]{:S(2)}, u32[]{:S(2)}) collective-permute-start(f32[256,128]{1,0:T(8,128)S(1)} %get-tuple-element.75.refs_2_), channel_id=1, source_target_pairs={{0,1},{1,0},{2,3},{3,2},{4,5},{5,4},{6,7},{7,6},{8,9},{9,8},{10,11... | collective-permute-start | bytes 393224 | tf_op jit(solution)/shard_map/ppermute | solution.py:361
  31.2 0.8 %collective-permute-done.4.away = f32[4,64,128]{2,1,0:T(8,128)S(1)} collective-permute-done((f32[4,64,128]{2,1,0:T(8,128)S(1)}, f32[4,64,128]{2,1,0:T(8,128)S(1)}, u32[]{:S(2)}, u32[]{:S(2)}) %collective-permute-start.4) | collective-permute-done | bytes 131104 | tf_op jit(solution)/shard_map/ppermute | solution.py:361
  32.2 2.3 %collective-permute-done.14.refs_12_ = f32[320,128]{1,0:T(8,128)S(1)} collective-permute-done((f32[320,128]{1,0:T(8,128)S(1)}, f32[320,128]{1,0:T(8,128)S(1)}, u32[]{:S(2)}, u32[]{:S(2)}) %collective-permute-start.14) | collective-permute-done | bytes 163872 | tf_op jit(solution)/shard_map/ppermute | solution.py:364
  34.4 1.5 %collective-permute-done.12.refs_10_ = f32[320,128]{1,0:T(8,128)S(1)} collective-permute-done((f32[320,128]{1,0:T(8,128)S(1)}, f32[320,128]{1,0:T(8,128)S(1)}, u32[]{:S(2)}, u32[]{:S(2)}) %collective-permute-start.12) | collective-permute-done | bytes 163872 | tf_op jit(solution)/shard_map/ppermute | solution.py:364
  35.9 0.5 %collective-permute-start.11 = (f32[320,128]{1,0:T(8,128)S(1)}, f32[320,128]{1,0:T(8,128)S(1)}, u32[]{:S(2)}, u32[]{:S(2)}) collective-permute-start(f32[320,128]{1,0:T(8,128)S(1)} %collective-permute-done.10.refs_8_), channel_id=1, source_target_pairs={{0,1},{1,0},{2,3},{3,2},{4,5},{5,4},{6,7},{7,6},{8,9},{9,8},{10,11... | collective-permute-start | bytes 491528 | tf_op jit(solution)/shard_map/ppermute | solution.py:361
  36.6 1.2 %collective-permute-done.8.refs_5_ = f32[256,128]{1,0:T(8,128)S(1)} collective-permute-done((f32[256,128]{1,0:T(8,128)S(1)}, f32[256,128]{1,0:T(8,128)S(1)}, u32[]{:S(2)}, u32[]{:S(2)}) %collective-permute-start.8) | collective-permute-done | bytes 131104 | tf_op jit(solution)/shard_map/ppermute | solution.py:361
  37.8 1.1 %shard_map.126 = (f32[512,128]{1,0:T(8,128)}, f32[3,512,128]{2,1,0:T(8,128)}, f32[512,128]{1,0:T(8,128)}) custom-call(s32[1]{0:T(128)S(6)} %copy.18.child.refs_0_, f32[2,256,128]{2,1,0:T(8,128)S(1)} %get-tuple-element.68.refs_0_.solved, f32[256,128]{1,0:T(8,128)S(1)} %get-tuple-element.74.refs_0_, f32[256,128]{1,0:T(8,128)S(1)} %collective-permute-done.5.refs_1_, ...), custom_call_target="tpu_custom_call" | custom-call | flops 65536 | bytes 2686980 | tf_op jit(solution)/shard_map/pallas_call | solution.py:43
  (30 shorter events, 2.2 us)
Async XLA Ops:
  2.6 1.6 %collective-permute-start = (f32[320,128]{1,0:T(8,128)S(1)}, f32[320,128]{1,0:T(8,128)S(1)}, u32[]{:S(2)}, u32[]{:S(2)}) collective-permute-start(f32[320,128]{1,0:T(8,128)S(1)} %get-tuple-element.52), channel_id=1, source_target_pairs={{0,1},{1,0},{2,3},{3,2},{4,5},{5,4},{6,7},{7,6},{8,9},{9,8},{10,11... | collective-permute-start | bytes 491528 | tf_op jit(solution)/shard_map/ppermute | solution.py:361
  3.1 4.9 %copy-start = (f32[1,1,3,256,256]{4,3,2,1,0:T(8,128)S(1)}, f32[1,1,3,256,256]{4,3,2,1,0:T(8,128)}, u32[]{:S(2)}) copy-start(f32[1,1,3,256,256]{4,3,2,1,0:T(8,128)} %param.13) | copy-start | bytes 2359300
  4.2 3.9 %copy-start.1 = (f32[1,1,3,128,128]{4,3,2,1,0:T(8,128)S(1)}, f32[1,1,3,128,128]{4,3,2,1,0:T(8,128)}, u32[]{:S(2)}) copy-start(f32[1,1,3,128,128]{4,3,2,1,0:T(8,128)} %param.14) | copy-start | bytes 589828
  4.2 3.9 %copy-start.2 = (f32[1,1,3,128,128]{4,3,2,1,0:T(8,128)S(1)}, f32[1,1,3,128,128]{4,3,2,1,0:T(8,128)}, u32[]{:S(2)}) copy-start(f32[1,1,3,128,128]{4,3,2,1,0:T(8,128)} %param.15) | copy-start | bytes 589828
  4.4 6.8 %collective-permute-start.1 = (f32[256,128]{1,0:T(8,128)S(1)}, f32[256,128]{1,0:T(8,128)S(1)}, u32[]{:S(2)}, u32[]{:S(2)}) collective-permute-start(f32[256,128]{1,0:T(8,128)S(1)} %get-tuple-element.56.home), channel_id=1, source_target_pairs={{0,2},{1,3},{2,0},{3,1},{4,6},{5,7},{6,4},{7,5},{8,10},{9,11},{10,... | collective-permute-start | bytes 393224 | tf_op jit(solution)/shard_map/ppermute | solution.py:361
  11.4 15.5 %collective-permute-start.7 = (f32[256,128]{1,0:T(8,128)S(1)}, f32[256,128]{1,0:T(8,128)S(1)}, u32[]{:S(2)}, u32[]{:S(2)}) collective-permute-start(f32[256,128]{1,0:T(8,128)S(1)} %get-tuple-element.76.home), channel_id=1, source_target_pairs={{0,4},{1,5},{2,6},{3,7},{4,0},{5,1},{6,2},{7,3},{8,12},{9,13},{10,... | collective-permute-start | bytes 393224 | tf_op jit(solution)/shard_map/ppermute | solution.py:361
  14.2 7.3 %collective-permute-start.2 = (f32[64,128]{1,0:T(8,128)S(1)}, f32[64,128]{1,0:T(8,128)S(1)}, u32[]{:S(2)}, u32[]{:S(2)}) collective-permute-start(f32[64,128]{1,0:T(8,128)S(1)} %get-tuple-element.65.refs_0_), channel_id=1, source_target_pairs={{0,4},{1,5},{2,6},{3,7},{4,0},{5,1},{6,2},{7,3},{8,12},{9,13},{10,... | collective-permute-start | bytes 98312 | tf_op jit(solution)/shard_map/ppermute | solution.py:361
  21.6 4.3 %collective-permute-start.3 = (f32[2,64,128]{2,1,0:T(8,128)S(1)}, f32[2,64,128]{2,1,0:T(8,128)S(1)}, u32[]{:S(2)}, u32[]{:S(2)}) collective-permute-start(f32[2,64,128]{2,1,0:T(8,128)S(1)} %shard_map.120.home), channel_id=1, source_target_pairs={{0,2},{1,3},{2,0},{3,1},{4,6},{5,7},{6,4},{7,5},{8,10},{9,11},{10,... | collective-permute-start | bytes 196616 | tf_op jit(solution)/shard_map/ppermute | solution.py:361
  22.1 8.5 %collective-permute-start.5 = (f32[256,128]{1,0:T(8,128)S(1)}, f32[256,128]{1,0:T(8,128)S(1)}, u32[]{:S(2)}, u32[]{:S(2)}) collective-permute-start(f32[256,128]{1,0:T(8,128)S(1)} %get-tuple-element.74.refs_0_), channel_id=1, source_target_pairs={{0,1},{1,0},{2,3},{3,2},{4,5},{5,4},{6,7},{7,6},{8,9},{9,8},{10,11... | collective-permute-start | bytes 393224 | tf_op jit(solution)/shard_map/ppermute | solution.py:361
  27.1 7.3 %collective-permute-start.14 = (f32[320,128]{1,0:T(8,128)S(1)}, f32[320,128]{1,0:T(8,128)S(1)}, u32[]{:S(2)}, u32[]{:S(2)}) collective-permute-start(f32[320,128]{1,0:T(8,128)S(1)} %get-tuple-element.78.refs_6_), channel_id=1, source_target_pairs={{0,24},{8,16},{16,8},{24,0},{1,25},{9,17},{17,9},{25,1},{2,26},{10... | collective-permute-start | bytes 491528 | tf_op jit(solution)/shard_map/ppermute | solution.py:364
  29.5 6.3 %collective-permute-start.12 = (f32[320,128]{1,0:T(8,128)S(1)}, f32[320,128]{1,0:T(8,128)S(1)}, u32[]{:S(2)}, u32[]{:S(2)}) collective-permute-start(f32[320,128]{1,0:T(8,128)S(1)} %get-tuple-element.78.refs_6_), channel_id=1, source_target_pairs={{0,16},{8,24},{16,0},{24,8},{1,17},{9,25},{17,1},{25,9},{2,18},{10... | collective-permute-start | bytes 491528 | tf_op jit(solution)/shard_map/ppermute | solution.py:364
  30.1 5.8 %collective-permute-start.10 = (f32[320,128]{1,0:T(8,128)S(1)}, f32[320,128]{1,0:T(8,128)S(1)}, u32[]{:S(2)}, u32[]{:S(2)}) collective-permute-start(f32[320,128]{1,0:T(8,128)S(1)} %get-tuple-element.78.refs_6_), channel_id=1, source_target_pairs={{0,8},{8,0},{16,24},{24,16},{1,9},{9,1},{17,25},{25,17},{2,10},{10... | collective-permute-start | bytes 491528 | tf_op jit(solution)/shard_map/ppermute | solution.py:364
  30.7 1.3 %collective-permute-start.4 = (f32[4,64,128]{2,1,0:T(8,128)S(1)}, f32[4,64,128]{2,1,0:T(8,128)S(1)}, u32[]{:S(2)}, u32[]{:S(2)}) collective-permute-start(f32[4,64,128]{2,1,0:T(8,128)S(1)} %shard_map.122.home.tails), channel_id=1, source_target_pairs={{0,1},{1,0},{2,3},{3,2},{4,5},{5,4},{6,7},{7,6},{8,9},{9,8},{10,11... | collective-permute-start | bytes 393224 | tf_op jit(solution)/shard_map/ppermute | solution.py:361
  30.7 5.7 %collective-permute-start.6 = (f32[256,128]{1,0:T(8,128)S(1)}, f32[256,128]{1,0:T(8,128)S(1)}, u32[]{:S(2)}, u32[]{:S(2)}) collective-permute-start(f32[256,128]{1,0:T(8,128)S(1)} %get-tuple-element.75.refs_2_), channel_id=1, source_target_pairs={{0,1},{1,0},{2,3},{3,2},{4,5},{5,4},{6,7},{7,6},{8,9},{9,8},{10,11... | collective-permute-start | bytes 393224 | tf_op jit(solution)/shard_map/ppermute | solution.py:361
  32.0 5.7 %collective-permute-start.9 = (f32[320,128]{1,0:T(8,128)S(1)}, f32[320,128]{1,0:T(8,128)S(1)}, u32[]{:S(2)}, u32[]{:S(2)}) collective-permute-start(f32[320,128]{1,0:T(8,128)S(1)} %get-tuple-element.78.refs_6_), channel_id=1, source_target_pairs={{0,1},{1,0},{2,3},{3,2},{4,5},{5,4},{6,7},{7,6},{8,9},{9,8},{10,11... | collective-permute-start | bytes 491528 | tf_op jit(solution)/shard_map/ppermute | solution.py:361
  34.4 4.5 %collective-permute-start.15 = (f32[320,128]{1,0:T(8,128)S(1)}, f32[320,128]{1,0:T(8,128)S(1)}, u32[]{:S(2)}, u32[]{:S(2)}) collective-permute-start(f32[320,128]{1,0:T(8,128)S(1)} %collective-permute-done.14.refs_12_), channel_id=1, source_target_pairs={{0,1},{1,0},{2,3},{3,2},{4,5},{5,4},{6,7},{7,6},{8,9},{9,8},{10,11... | collective-permute-start | bytes 491528 | tf_op jit(solution)/shard_map/ppermute | solution.py:361
  35.9 3.0 %collective-permute-start.13 = (f32[320,128]{1,0:T(8,128)S(1)}, f32[320,128]{1,0:T(8,128)S(1)}, u32[]{:S(2)}, u32[]{:S(2)}) collective-permute-start(f32[320,128]{1,0:T(8,128)S(1)} %collective-permute-done.12.refs_10_), channel_id=1, source_target_pairs={{0,1},{1,0},{2,3},{3,2},{4,5},{5,4},{6,7},{7,6},{8,9},{9,8},{10,11... | collective-permute-start | bytes 491528 | tf_op jit(solution)/shard_map/ppermute | solution.py:361
  35.9 3.0 %collective-permute-start.11 = (f32[320,128]{1,0:T(8,128)S(1)}, f32[320,128]{1,0:T(8,128)S(1)}, u32[]{:S(2)}, u32[]{:S(2)}) collective-permute-start(f32[320,128]{1,0:T(8,128)S(1)} %collective-permute-done.10.refs_8_), channel_id=1, source_target_pairs={{0,1},{1,0},{2,3},{3,2},{4,5},{5,4},{6,7},{7,6},{8,9},{9,8},{10,11... | collective-permute-start | bytes 491528 | tf_op jit(solution)/shard_map/ppermute | solution.py:361
  36.4 1.3 %collective-permute-start.8 = (f32[256,128]{1,0:T(8,128)S(1)}, f32[256,128]{1,0:T(8,128)S(1)}, u32[]{:S(2)}, u32[]{:S(2)}) collective-permute-start(f32[256,128]{1,0:T(8,128)S(1)} %get-tuple-element.77.refs_4_), channel_id=1, source_target_pairs={{0,1},{1,0},{2,3},{3,2},{4,5},{5,4},{6,7},{7,6},{8,9},{9,8},{10,11... | collective-permute-start | bytes 393224 | tf_op jit(solution)/shard_map/ppermute | solution.py:361

commit v7 on v6

--- a/solution.py
+++ b/solution.py
@@ -77,10 +77,12 @@
             ]
         )
     ]
-    for copy in copies:
+    for copy in copies[:5]:
         copy.start()
     for copy in copies[:2]:
         copy.wait()
+    for copy in copies[5:]:
+        copy.start()
     solved = product(generator_here[:, :size], inverse_here[...])
     solve_map[...] = solved
     copies[2].wait()
@@ -503,9 +505,7 @@
             kernel, shapes, args + after, merge_flops, in_specs=specs + [anywhere] * len(after)
         )
         nodes.append(node)
-    received = []
-    for mask in range(1, fronts):
-        received.append(level_swap(skeleton, mask))
+    received = [level_swap(skeleton, mask) for mask in range(1, fronts)]
     roots = [skeleton, blk_swap(skeleton, 1)]
     for value in received:
         roots += [value, blk_swap(value, 1)]

time: 40 us -> 40.1 us (level)
  no operation moved by 1% of the time
where the time goes in v7:
time: 40.1 us; the launch traced here: 39.3 us
  waiting for transfers between devices  18.6 us (46%)
  starting transfers between devices  11.9 us (30%)
  Pallas kernels  7.34 us (18%)
  between operations  1.45 us (4%)
    ppermute x13, waiting for transfers between devices, blk_swap(): return lax.ppermute(value, 'blk', [(i, i ^ mask) for i in range(leaves)])  14.9 us
    ppermute x13, starting transfers between devices, blk_swap(): return lax.ppermute(value, 'blk', [(i, i ^ mask) for i in range(leaves)])  8.34 us
    pallas_call x16, Pallas kernels, call(): pl.pallas_call(kernel, out_shape=out_shape, in_specs=in_specs or [vmem] *...  7.34 us
    ppermute x3, waiting for transfers between devices, level_swap(): return lax.ppermute(value, 'level', [(i, i ^ mask) for i in range(fronts)])  3.7 us
    ppermute x3, starting transfers between devices, level_swap(): return lax.ppermute(value, 'level', [(i, i ^ mask) for i in range(fronts)])  3.55 us
  transfers between devices with their start and end apart: 16, of which 8 were waited for; matrix products, arithmetic and copies ran while one was open for 0% of the time, Pallas kernels for 12%

profile of v7, /device:TPU:0, one launch (start us, length us, event | category | flops | bytes accessed | tf_op | source)
XLA Modules:
  0.0 39.3 jit_solution(9767286834557910944)
XLA Ops:
  0.6 2.1 %shard_map.112 = (f32[320,128]{1,0:T(8,128)S(1)}, f32[256,128]{1,0:T(8,128)S(1)}, bf16[768,128]{1,0:T(8,128)(2,1)S(1)}, f32[2,256,256]{2,1,0:T(8,128)S(1)}, f32[...) custom-call(f32[512,256]{1,0:T(8,128)} %bitcast.23, ...), custom_call_target="tpu_custom_call" | custom-call | flops 113246208 | bytes 3768320 | tf_op jit(solution)/shard_map/pallas_call | solution.py:43
  2.7 0.6 %collective-permute-start = (f32[320,128]{1,0:T(8,128)S(1)}, f32[320,128]{1,0:T(8,128)S(1)}, u32[]{:S(2)}, u32[]{:S(2)}) collective-permute-start(f32[320,128]{1,0:T(8,128)S(1)} %get-tuple-element.52), channel_id=1, source_target_pairs={{0,1},{1,0},{2,3},{3,2},{4,5},{5,4},{6,7},{7,6},{8,9},{9,8},{10,11... | collective-permute-start | bytes 491528 | tf_op jit(solution)/shard_map/ppermute | solution.py:363
  3.3 0.8 %shard_map.113 = (bf16[1,384,256]{2,1,0:T(8,128)(2,1)S(1)}, bf16[1,384,256]{2,1,0:T(8,128)(2,1)S(1)}, f32[256,256]{1,0:T(8,128)S(1)}, f32[64,128]{1,0:T(8,128)S(1)}) custom-call(f32[256,256]{1,0:T(8,128)S(1)} %get-tuple-element.44.generator, f32[128,128]{1,0:T(8,128)S(1)} %get-tuple-element.45.inverse, f32[128,128]{1,0:T(8,128)S(1)} %get-tuple-element.46.lower, ...), custom_call_target="tpu_custom_call" | custom-call | flops 176160768 | bytes 1933312 | tf_op jit(solution)/shard_map/pallas_call | solution.py:43
  4.6 3.0 %collective-permute-start.1 = (f32[256,128]{1,0:T(8,128)S(1)}, f32[256,128]{1,0:T(8,128)S(1)}, u32[]{:S(2)}, u32[]{:S(2)}) collective-permute-start(f32[256,128]{1,0:T(8,128)S(1)} %get-tuple-element.56.home), channel_id=1, source_target_pairs={{0,2},{1,3},{2,0},{3,1},{4,6},{5,7},{6,4},{7,5},{8,10},{9,11},{10,... | collective-permute-start | bytes 393224 | tf_op jit(solution)/shard_map/ppermute | solution.py:363
  8.2 0.4 shard_map.115
  8.6 0.3 shard_map.117
  9.2 2.2 %collective-permute-done.1.away = f32[256,128]{1,0:T(8,128)S(1)} collective-permute-done((f32[256,128]{1,0:T(8,128)S(1)}, f32[256,128]{1,0:T(8,128)S(1)}, u32[]{:S(2)}, u32[]{:S(2)}) %collective-permute-start.1) | collective-permute-done | bytes 131104 | tf_op jit(solution)/shard_map/ppermute | solution.py:363
  11.6 2.8 %collective-permute-start.7 = (f32[256,128]{1,0:T(8,128)S(1)}, f32[256,128]{1,0:T(8,128)S(1)}, u32[]{:S(2)}, u32[]{:S(2)}) collective-permute-start(f32[256,128]{1,0:T(8,128)S(1)} %get-tuple-element.76.home), channel_id=1, source_target_pairs={{0,4},{1,5},{2,6},{3,7},{4,0},{5,1},{6,2},{7,3},{8,12},{9,13},{10,... | collective-permute-start | bytes 393224 | tf_op jit(solution)/shard_map/ppermute | solution.py:363
  14.6 7.2 %collective-permute-done.2.far = f32[64,128]{1,0:T(8,128)S(1)} collective-permute-done((f32[64,128]{1,0:T(8,128)S(1)}, f32[64,128]{1,0:T(8,128)S(1)}, u32[]{:S(2)}, u32[]{:S(2)}) %collective-permute-start.2) | collective-permute-done | bytes 32800 | tf_op jit(solution)/shard_map/ppermute | solution.py:363
  21.7 0.6 %collective-permute-start.3 = (f32[2,64,128]{2,1,0:T(8,128)S(1)}, f32[2,64,128]{2,1,0:T(8,128)S(1)}, u32[]{:S(2)}, u32[]{:S(2)}) collective-permute-start(f32[2,64,128]{2,1,0:T(8,128)S(1)} %shard_map.120.home), channel_id=1, source_target_pairs={{0,2},{1,3},{2,0},{3,1},{4,6},{5,7},{6,4},{7,5},{8,10},{9,11},{10,... | collective-permute-start | bytes 196616 | tf_op jit(solution)/shard_map/ppermute | solution.py:363
  22.3 0.4 shard_map.121
  22.7 3.3 %collective-permute-done.3.away = f32[2,64,128]{2,1,0:T(8,128)S(1)} collective-permute-done((f32[2,64,128]{2,1,0:T(8,128)S(1)}, f32[2,64,128]{2,1,0:T(8,128)S(1)}, u32[]{:S(2)}, u32[]{:S(2)}) %collective-permute-start.3) | collective-permute-done | bytes 65568 | tf_op jit(solution)/shard_map/ppermute | solution.py:363
  26.0 0.4 shard_map.122.home.tails
  26.6 0.4 %shard_map.119 = (f32[2,256,128]{2,1,0:T(8,128)S(1)}, f32[128,128]{1,0:T(8,128)S(1)}) custom-call(f32[2,256,128]{2,1,0:T(8,128)S(1)} %get-tuple-element.66.solved_early, f32[128,128]{1,0:T(8,128)S(1)} %get-tuple-element.67.map_early, s32[1]{0:T(128)S(6)} %copy.18.child.refs_0_, f32[2,256,256]{2,1,0:T(8,128)S(1)} %get-tuple-element.47.right.refs_1_, ...), custom_call_target="tpu_custom_call" | custom-call | flops 125829120 | bytes 1441796 | tf_op jit(solution)/shard_map/pallas_call | solution.py:43
  27.3 2.4 %collective-permute-start.14 = (f32[320,128]{1,0:T(8,128)S(1)}, f32[320,128]{1,0:T(8,128)S(1)}, u32[]{:S(2)}, u32[]{:S(2)}) collective-permute-start(f32[320,128]{1,0:T(8,128)S(1)} %get-tuple-element.78.refs_6_), channel_id=1, source_target_pairs={{0,24},{8,16},{16,8},{24,0},{1,25},{9,17},{17,9},{25,1},{2,26},{10... | collective-permute-start | bytes 491528 | tf_op jit(solution)/shard_map/ppermute | solution.py:366
  29.7 0.5 %collective-permute-start.12 = (f32[320,128]{1,0:T(8,128)S(1)}, f32[320,128]{1,0:T(8,128)S(1)}, u32[]{:S(2)}, u32[]{:S(2)}) collective-permute-start(f32[320,128]{1,0:T(8,128)S(1)} %get-tuple-element.78.refs_6_), channel_id=1, source_target_pairs={{0,16},{8,24},{16,0},{24,8},{1,17},{9,25},{17,1},{25,9},{2,18},{10... | collective-permute-start | bytes 491528 | tf_op jit(solution)/shard_map/ppermute | solution.py:366
  30.2 0.6 %collective-permute-start.10 = (f32[320,128]{1,0:T(8,128)S(1)}, f32[320,128]{1,0:T(8,128)S(1)}, u32[]{:S(2)}, u32[]{:S(2)}) collective-permute-start(f32[320,128]{1,0:T(8,128)S(1)} %get-tuple-element.78.refs_6_), channel_id=1, source_target_pairs={{0,8},{8,0},{16,24},{24,16},{1,9},{9,1},{17,25},{25,17},{2,10},{10... | collective-permute-start | bytes 491528 | tf_op jit(solution)/shard_map/ppermute | solution.py:366
  30.8 0.5 %collective-permute-start.6 = (f32[256,128]{1,0:T(8,128)S(1)}, f32[256,128]{1,0:T(8,128)S(1)}, u32[]{:S(2)}, u32[]{:S(2)}) collective-permute-start(f32[256,128]{1,0:T(8,128)S(1)} %get-tuple-element.75.refs_2_), channel_id=1, source_target_pairs={{0,1},{1,0},{2,3},{3,2},{4,5},{5,4},{6,7},{7,6},{8,9},{9,8},{10,11... | collective-permute-start | bytes 393224 | tf_op jit(solution)/shard_map/ppermute | solution.py:363
  31.4 0.8 %collective-permute-done.4.away = f32[4,64,128]{2,1,0:T(8,128)S(1)} collective-permute-done((f32[4,64,128]{2,1,0:T(8,128)S(1)}, f32[4,64,128]{2,1,0:T(8,128)S(1)}, u32[]{:S(2)}, u32[]{:S(2)}) %collective-permute-start.4) | collective-permute-done | bytes 131104 | tf_op jit(solution)/shard_map/ppermute | solution.py:363
  32.3 2.2 %collective-permute-done.14.refs_12_ = f32[320,128]{1,0:T(8,128)S(1)} collective-permute-done((f32[320,128]{1,0:T(8,128)S(1)}, f32[320,128]{1,0:T(8,128)S(1)}, u32[]{:S(2)}, u32[]{:S(2)}) %collective-permute-start.14) | collective-permute-done | bytes 163872 | tf_op jit(solution)/shard_map/ppermute | solution.py:366
  34.6 1.5 %collective-permute-done.12.refs_10_ = f32[320,128]{1,0:T(8,128)S(1)} collective-permute-done((f32[320,128]{1,0:T(8,128)S(1)}, f32[320,128]{1,0:T(8,128)S(1)}, u32[]{:S(2)}, u32[]{:S(2)}) %collective-permute-start.12) | collective-permute-done | bytes 163872 | tf_op jit(solution)/shard_map/ppermute | solution.py:366
  36.0 0.5 %collective-permute-start.11 = (f32[320,128]{1,0:T(8,128)S(1)}, f32[320,128]{1,0:T(8,128)S(1)}, u32[]{:S(2)}, u32[]{:S(2)}) collective-permute-start(f32[320,128]{1,0:T(8,128)S(1)} %collective-permute-done.10.refs_8_), channel_id=1, source_target_pairs={{0,1},{1,0},{2,3},{3,2},{4,5},{5,4},{6,7},{7,6},{8,9},{9,8},{10,11... | collective-permute-start | bytes 491528 | tf_op jit(solution)/shard_map/ppermute | solution.py:363
  36.7 1.2 %collective-permute-done.8.refs_5_ = f32[256,128]{1,0:T(8,128)S(1)} collective-permute-done((f32[256,128]{1,0:T(8,128)S(1)}, f32[256,128]{1,0:T(8,128)S(1)}, u32[]{:S(2)}, u32[]{:S(2)}) %collective-permute-start.8) | collective-permute-done | bytes 131104 | tf_op jit(solution)/shard_map/ppermute | solution.py:363
  37.9 1.1 %shard_map.126 = (f32[512,128]{1,0:T(8,128)}, f32[3,512,128]{2,1,0:T(8,128)}, f32[512,128]{1,0:T(8,128)}) custom-call(s32[1]{0:T(128)S(6)} %copy.18.child.refs_0_, f32[2,256,128]{2,1,0:T(8,128)S(1)} %get-tuple-element.68.refs_0_.solved, f32[256,128]{1,0:T(8,128)S(1)} %get-tuple-element.74.refs_0_, f32[256,128]{1,0:T(8,128)S(1)} %collective-permute-done.5.refs_1_, ...), custom_call_target="tpu_custom_call" | custom-call | flops 65536 | bytes 2686980 | tf_op jit(solution)/shard_map/pallas_call | solution.py:43
  (30 shorter events, 2.2 us)
Async XLA Ops:
  2.7 1.6 %collective-permute-start = (f32[320,128]{1,0:T(8,128)S(1)}, f32[320,128]{1,0:T(8,128)S(1)}, u32[]{:S(2)}, u32[]{:S(2)}) collective-permute-start(f32[320,128]{1,0:T(8,128)S(1)} %get-tuple-element.52), channel_id=1, source_target_pairs={{0,1},{1,0},{2,3},{3,2},{4,5},{5,4},{6,7},{7,6},{8,9},{9,8},{10,11... | collective-permute-start | bytes 491528 | tf_op jit(solution)/shard_map/ppermute | solution.py:363
  3.3 4.9 %copy-start = (f32[1,1,3,256,256]{4,3,2,1,0:T(8,128)S(1)}, f32[1,1,3,256,256]{4,3,2,1,0:T(8,128)}, u32[]{:S(2)}) copy-start(f32[1,1,3,256,256]{4,3,2,1,0:T(8,128)} %param.13) | copy-start | bytes 2359300
  4.3 3.9 %copy-start.1 = (f32[1,1,3,128,128]{4,3,2,1,0:T(8,128)S(1)}, f32[1,1,3,128,128]{4,3,2,1,0:T(8,128)}, u32[]{:S(2)}) copy-start(f32[1,1,3,128,128]{4,3,2,1,0:T(8,128)} %param.14) | copy-start | bytes 589828
  4.3 3.9 %copy-start.2 = (f32[1,1,3,128,128]{4,3,2,1,0:T(8,128)S(1)}, f32[1,1,3,128,128]{4,3,2,1,0:T(8,128)}, u32[]{:S(2)}) copy-start(f32[1,1,3,128,128]{4,3,2,1,0:T(8,128)} %param.15) | copy-start | bytes 589828
  4.6 6.8 %collective-permute-start.1 = (f32[256,128]{1,0:T(8,128)S(1)}, f32[256,128]{1,0:T(8,128)S(1)}, u32[]{:S(2)}, u32[]{:S(2)}) collective-permute-start(f32[256,128]{1,0:T(8,128)S(1)} %get-tuple-element.56.home), channel_id=1, source_target_pairs={{0,2},{1,3},{2,0},{3,1},{4,6},{5,7},{6,4},{7,5},{8,10},{9,11},{10,... | collective-permute-start | bytes 393224 | tf_op jit(solution)/shard_map/ppermute | solution.py:363
  11.6 15.5 %collective-permute-start.7 = (f32[256,128]{1,0:T(8,128)S(1)}, f32[256,128]{1,0:T(8,128)S(1)}, u32[]{:S(2)}, u32[]{:S(2)}) collective-permute-start(f32[256,128]{1,0:T(8,128)S(1)} %get-tuple-element.76.home), channel_id=1, source_target_pairs={{0,4},{1,5},{2,6},{3,7},{4,0},{5,1},{6,2},{7,3},{8,12},{9,13},{10,... | collective-permute-start | bytes 393224 | tf_op jit(solution)/shard_map/ppermute | solution.py:363
  14.4 7.3 %collective-permute-start.2 = (f32[64,128]{1,0:T(8,128)S(1)}, f32[64,128]{1,0:T(8,128)S(1)}, u32[]{:S(2)}, u32[]{:S(2)}) collective-permute-start(f32[64,128]{1,0:T(8,128)S(1)} %get-tuple-element.65.refs_0_), channel_id=1, source_target_pairs={{0,4},{1,5},{2,6},{3,7},{4,0},{5,1},{6,2},{7,3},{8,12},{9,13},{10,... | collective-permute-start | bytes 98312 | tf_op jit(solution)/shard_map/ppermute | solution.py:363
  21.7 4.3 %collective-permute-start.3 = (f32[2,64,128]{2,1,0:T(8,128)S(1)}, f32[2,64,128]{2,1,0:T(8,128)S(1)}, u32[]{:S(2)}, u32[]{:S(2)}) collective-permute-start(f32[2,64,128]{2,1,0:T(8,128)S(1)} %shard_map.120.home), channel_id=1, source_target_pairs={{0,2},{1,3},{2,0},{3,1},{4,6},{5,7},{6,4},{7,5},{8,10},{9,11},{10,... | collective-permute-start | bytes 196616 | tf_op jit(solution)/shard_map/ppermute | solution.py:363
  22.3 8.5 %collective-permute-start.5 = (f32[256,128]{1,0:T(8,128)S(1)}, f32[256,128]{1,0:T(8,128)S(1)}, u32[]{:S(2)}, u32[]{:S(2)}) collective-permute-start(f32[256,128]{1,0:T(8,128)S(1)} %get-tuple-element.74.refs_0_), channel_id=1, source_target_pairs={{0,1},{1,0},{2,3},{3,2},{4,5},{5,4},{6,7},{7,6},{8,9},{9,8},{10,11... | collective-permute-start | bytes 393224 | tf_op jit(solution)/shard_map/ppermute | solution.py:363
  27.3 7.3 %collective-permute-start.14 = (f32[320,128]{1,0:T(8,128)S(1)}, f32[320,128]{1,0:T(8,128)S(1)}, u32[]{:S(2)}, u32[]{:S(2)}) collective-permute-start(f32[320,128]{1,0:T(8,128)S(1)} %get-tuple-element.78.refs_6_), channel_id=1, source_target_pairs={{0,24},{8,16},{16,8},{24,0},{1,25},{9,17},{17,9},{25,1},{2,26},{10... | collective-permute-start | bytes 491528 | tf_op jit(solution)/shard_map/ppermute | solution.py:366
  29.7 6.4 %collective-permute-start.12 = (f32[320,128]{1,0:T(8,128)S(1)}, f32[320,128]{1,0:T(8,128)S(1)}, u32[]{:S(2)}, u32[]{:S(2)}) collective-permute-start(f32[320,128]{1,0:T(8,128)S(1)} %get-tuple-element.78.refs_6_), channel_id=1, source_target_pairs={{0,16},{8,24},{16,0},{24,8},{1,17},{9,25},{17,1},{25,9},{2,18},{10... | collective-permute-start | bytes 491528 | tf_op jit(solution)/shard_map/ppermute | solution.py:366
  30.2 5.8 %collective-permute-start.10 = (f32[320,128]{1,0:T(8,128)S(1)}, f32[320,128]{1,0:T(8,128)S(1)}, u32[]{:S(2)}, u32[]{:S(2)}) collective-permute-start(f32[320,128]{1,0:T(8,128)S(1)} %get-tuple-element.78.refs_6_), channel_id=1, source_target_pairs={{0,8},{8,0},{16,24},{24,16},{1,9},{9,1},{17,25},{25,17},{2,10},{10... | collective-permute-start | bytes 491528 | tf_op jit(solution)/shard_map/ppermute | solution.py:366
  30.8 1.3 %collective-permute-start.4 = (f32[4,64,128]{2,1,0:T(8,128)S(1)}, f32[4,64,128]{2,1,0:T(8,128)S(1)}, u32[]{:S(2)}, u32[]{:S(2)}) collective-permute-start(f32[4,64,128]{2,1,0:T(8,128)S(1)} %shard_map.122.home.tails), channel_id=1, source_target_pairs={{0,1},{1,0},{2,3},{3,2},{4,5},{5,4},{6,7},{7,6},{8,9},{9,8},{10,11... | collective-permute-start | bytes 393224 | tf_op jit(solution)/shard_map/ppermute | solution.py:363
  30.8 5.7 %collective-permute-start.6 = (f32[256,128]{1,0:T(8,128)S(1)}, f32[256,128]{1,0:T(8,128)S(1)}, u32[]{:S(2)}, u32[]{:S(2)}) collective-permute-start(f32[256,128]{1,0:T(8,128)S(1)} %get-tuple-element.75.refs_2_), channel_id=1, source_target_pairs={{0,1},{1,0},{2,3},{3,2},{4,5},{5,4},{6,7},{7,6},{8,9},{9,8},{10,11... | collective-permute-start | bytes 393224 | tf_op jit(solution)/shard_map/ppermute | solution.py:363
  32.2 5.7 %collective-permute-start.9 = (f32[320,128]{1,0:T(8,128)S(1)}, f32[320,128]{1,0:T(8,128)S(1)}, u32[]{:S(2)}, u32[]{:S(2)}) collective-permute-start(f32[320,128]{1,0:T(8,128)S(1)} %get-tuple-element.78.refs_6_), channel_id=1, source_target_pairs={{0,1},{1,0},{2,3},{3,2},{4,5},{5,4},{6,7},{7,6},{8,9},{9,8},{10,11... | collective-permute-start | bytes 491528 | tf_op jit(solution)/shard_map/ppermute | solution.py:363
  34.6 4.5 %collective-permute-start.15 = (f32[320,128]{1,0:T(8,128)S(1)}, f32[320,128]{1,0:T(8,128)S(1)}, u32[]{:S(2)}, u32[]{:S(2)}) collective-permute-start(f32[320,128]{1,0:T(8,128)S(1)} %collective-permute-done.14.refs_12_), channel_id=1, source_target_pairs={{0,1},{1,0},{2,3},{3,2},{4,5},{5,4},{6,7},{7,6},{8,9},{9,8},{10,11... | collective-permute-start | bytes 491528 | tf_op jit(solution)/shard_map/ppermute | solution.py:363
  36.0 3.0 %collective-permute-start.13 = (f32[320,128]{1,0:T(8,128)S(1)}, f32[320,128]{1,0:T(8,128)S(1)}, u32[]{:S(2)}, u32[]{:S(2)}) collective-permute-start(f32[320,128]{1,0:T(8,128)S(1)} %collective-permute-done.12.refs_10_), channel_id=1, source_target_pairs={{0,1},{1,0},{2,3},{3,2},{4,5},{5,4},{6,7},{7,6},{8,9},{9,8},{10,11... | collective-permute-start | bytes 491528 | tf_op jit(solution)/shard_map/ppermute | solution.py:363
  36.0 3.0 %collective-permute-start.11 = (f32[320,128]{1,0:T(8,128)S(1)}, f32[320,128]{1,0:T(8,128)S(1)}, u32[]{:S(2)}, u32[]{:S(2)}) collective-permute-start(f32[320,128]{1,0:T(8,128)S(1)} %collective-permute-done.10.refs_8_), channel_id=1, source_target_pairs={{0,1},{1,0},{2,3},{3,2},{4,5},{5,4},{6,7},{7,6},{8,9},{9,8},{10,11... | collective-permute-start | bytes 491528 | tf_op jit(solution)/shard_map/ppermute | solution.py:363
  36.6 1.3 %collective-permute-start.8 = (f32[256,128]{1,0:T(8,128)S(1)}, f32[256,128]{1,0:T(8,128)S(1)}, u32[]{:S(2)}, u32[]{:S(2)}) collective-permute-start(f32[256,128]{1,0:T(8,128)S(1)} %get-tuple-element.77.refs_4_), channel_id=1, source_target_pairs={{0,1},{1,0},{2,3},{3,2},{4,5},{5,4},{6,7},{7,6},{8,9},{9,8},{10,11... | collective-permute-start | bytes 393224 | tf_op jit(solution)/shard_map/ppermute | solution.py:363

commit v8 on v7

--- a/solution.py
+++ b/solution.py
@@ -77,12 +77,10 @@
             ]
         )
     ]
-    for copy in copies[:5]:
+    for copy in copies:
         copy.start()
     for copy in copies[:2]:
         copy.wait()
-    for copy in copies[5:]:
-        copy.start()
     solved = product(generator_here[:, :size], inverse_here[...])
     solve_map[...] = solved
     copies[2].wait()
@@ -106,14 +104,14 @@
 
 def leaf_solve_kernel(bit, solved_early, map_early, *refs):
     solved, leaf_map = refs[-2:]
-    early = (lax.axis_index("blk") >> bit) & 1
-
-    @pl.when(early == 1)
+    early = ((lax.axis_index("blk") >> bit) & 3) == 3
+
+    @pl.when(early)
     def _():
         solved[...] = solved_early[...]
         leaf_map[...] = map_early[...]
 
-    @pl.when(early == 0)
+    @pl.when(jnp.logical_not(early))
     def _():
         leaf_solve(*refs)
 
@@ -153,7 +151,7 @@
     node, skeleton, solved, leaf_map = refs[-4:]
     merge_kernel(index, base, away, other_maps, node, skeleton)
 
-    @pl.when((lax.axis_index("blk") >> bit) & 1 == 1)
+    @pl.when(((lax.axis_index("blk") >> bit) & 3) == 3)
     def _():
         leaf_solve(child, right, coupling, solve_map, solved, leaf_map)
 

time: 40.1 us -> 40 us (level)
  no operation moved by 1% of the time
where the time goes in v8:
time: 40 us; the launch traced here: 39.2 us
  waiting for transfers between devices  18.7 us (47%)
  starting transfers between devices  11.9 us (30%)
  Pallas kernels  7.17 us (18%)
  between operations  1.45 us (4%)
    ppermute x13, waiting for transfers between devices, blk_swap(): return lax.ppermute(value, 'blk', [(i, i ^ mask) for i in range(leaves)])  15 us
    ppermute x13, starting transfers between devices, blk_swap(): return lax.ppermute(value, 'blk', [(i, i ^ mask) for i in range(leaves)])  8.34 us
    pallas_call x16, Pallas kernels, call(): pl.pallas_call(kernel, out_shape=out_shape, in_specs=in_specs or [vmem] *...  7.17 us
    ppermute x3, waiting for transfers between devices, level_swap(): return lax.ppermute(value, 'level', [(i, i ^ mask) for i in range(fronts)])  3.7 us
    ppermute x3, starting transfers between devices, level_swap(): return lax.ppermute(value, 'level', [(i, i ^ mask) for i in range(fronts)])  3.55 us
  transfers between devices with their start and end apart: 16, of which 8 were waited for; matrix products, arithmetic and copies ran while one was open for 0% of the time, Pallas kernels for 12%

profile of v8, /device:TPU:0, one launch (start us, length us, event | category | flops | bytes accessed | tf_op | source)
XLA Modules:
  0.0 39.2 jit_solution(12824806286067029793)
XLA Ops:
  0.6 1.9 %shard_map.112 = (f32[320,128]{1,0:T(8,128)S(1)}, f32[256,128]{1,0:T(8,128)S(1)}, bf16[768,128]{1,0:T(8,128)(2,1)S(1)}, f32[2,256,256]{2,1,0:T(8,128)S(1)}, f32[...) custom-call(f32[512,256]{1,0:T(8,128)} %bitcast.23, ...), custom_call_target="tpu_custom_call" | custom-call | flops 113246208 | bytes 3768320 | tf_op jit(solution)/shard_map/pallas_call | solution.py:43
  2.6 0.6 %collective-permute-start = (f32[320,128]{1,0:T(8,128)S(1)}, f32[320,128]{1,0:T(8,128)S(1)}, u32[]{:S(2)}, u32[]{:S(2)}) collective-permute-start(f32[320,128]{1,0:T(8,128)S(1)} %get-tuple-element.52), channel_id=1, source_target_pairs={{0,1},{1,0},{2,3},{3,2},{4,5},{5,4},{6,7},{7,6},{8,9},{9,8},{10,11... | collective-permute-start | bytes 491528 | tf_op jit(solution)/shard_map/ppermute | solution.py:361
  3.1 0.8 %shard_map.113 = (bf16[1,384,256]{2,1,0:T(8,128)(2,1)S(1)}, bf16[1,384,256]{2,1,0:T(8,128)(2,1)S(1)}, f32[256,256]{1,0:T(8,128)S(1)}, f32[64,128]{1,0:T(8,128)S(1)}) custom-call(f32[256,256]{1,0:T(8,128)S(1)} %get-tuple-element.44.generator, f32[128,128]{1,0:T(8,128)S(1)} %get-tuple-element.45.inverse, f32[128,128]{1,0:T(8,128)S(1)} %get-tuple-element.46.lower, ...), custom_call_target="tpu_custom_call" | custom-call | flops 176160768 | bytes 1933312 | tf_op jit(solution)/shard_map/pallas_call | solution.py:43
  4.4 3.0 %collective-permute-start.1 = (f32[256,128]{1,0:T(8,128)S(1)}, f32[256,128]{1,0:T(8,128)S(1)}, u32[]{:S(2)}, u32[]{:S(2)}) collective-permute-start(f32[256,128]{1,0:T(8,128)S(1)} %get-tuple-element.56.home), channel_id=1, source_target_pairs={{0,2},{1,3},{2,0},{3,1},{4,6},{5,7},{6,4},{7,5},{8,10},{9,11},{10,... | collective-permute-start | bytes 393224 | tf_op jit(solution)/shard_map/ppermute | solution.py:361
  8.1 0.4 shard_map.115
  8.5 0.3 shard_map.117
  9.0 2.2 %collective-permute-done.1.away = f32[256,128]{1,0:T(8,128)S(1)} collective-permute-done((f32[256,128]{1,0:T(8,128)S(1)}, f32[256,128]{1,0:T(8,128)S(1)}, u32[]{:S(2)}, u32[]{:S(2)}) %collective-permute-start.1) | collective-permute-done | bytes 131104 | tf_op jit(solution)/shard_map/ppermute | solution.py:361
  11.4 2.8 %collective-permute-start.7 = (f32[256,128]{1,0:T(8,128)S(1)}, f32[256,128]{1,0:T(8,128)S(1)}, u32[]{:S(2)}, u32[]{:S(2)}) collective-permute-start(f32[256,128]{1,0:T(8,128)S(1)} %get-tuple-element.76.home), channel_id=1, source_target_pairs={{0,4},{1,5},{2,6},{3,7},{4,0},{5,1},{6,2},{7,3},{8,12},{9,13},{10,... | collective-permute-start | bytes 393224 | tf_op jit(solution)/shard_map/ppermute | solution.py:361
  14.4 7.2 %collective-permute-done.2.far = f32[64,128]{1,0:T(8,128)S(1)} collective-permute-done((f32[64,128]{1,0:T(8,128)S(1)}, f32[64,128]{1,0:T(8,128)S(1)}, u32[]{:S(2)}, u32[]{:S(2)}) %collective-permute-start.2) | collective-permute-done | bytes 32800 | tf_op jit(solution)/shard_map/ppermute | solution.py:361
  21.6 0.5 %collective-permute-start.3 = (f32[2,64,128]{2,1,0:T(8,128)S(1)}, f32[2,64,128]{2,1,0:T(8,128)S(1)}, u32[]{:S(2)}, u32[]{:S(2)}) collective-permute-start(f32[2,64,128]{2,1,0:T(8,128)S(1)} %shard_map.120.home), channel_id=1, source_target_pairs={{0,2},{1,3},{2,0},{3,1},{4,6},{5,7},{6,4},{7,5},{8,10},{9,11},{10,... | collective-permute-start | bytes 196616 | tf_op jit(solution)/shard_map/ppermute | solution.py:361
  22.1 0.4 shard_map.121
  22.5 3.3 %collective-permute-done.3.away = f32[2,64,128]{2,1,0:T(8,128)S(1)} collective-permute-done((f32[2,64,128]{2,1,0:T(8,128)S(1)}, f32[2,64,128]{2,1,0:T(8,128)S(1)}, u32[]{:S(2)}, u32[]{:S(2)}) %collective-permute-start.3) | collective-permute-done | bytes 65568 | tf_op jit(solution)/shard_map/ppermute | solution.py:361
  25.9 0.4 shard_map.122.home.tails
  26.5 0.4 %shard_map.119 = (f32[2,256,128]{2,1,0:T(8,128)S(1)}, f32[128,128]{1,0:T(8,128)S(1)}) custom-call(f32[2,256,128]{2,1,0:T(8,128)S(1)} %get-tuple-element.66.solved_early, f32[128,128]{1,0:T(8,128)S(1)} %get-tuple-element.67.map_early, s32[1]{0:T(128)S(6)} %copy.18.child.refs_0_, f32[2,256,256]{2,1,0:T(8,128)S(1)} %get-tuple-element.47.right.refs_1_, ...), custom_call_target="tpu_custom_call" | custom-call | flops 125829120 | bytes 1441796 | tf_op jit(solution)/shard_map/pallas_call | solution.py:43
  27.1 2.4 %collective-permute-start.14 = (f32[320,128]{1,0:T(8,128)S(1)}, f32[320,128]{1,0:T(8,128)S(1)}, u32[]{:S(2)}, u32[]{:S(2)}) collective-permute-start(f32[320,128]{1,0:T(8,128)S(1)} %get-tuple-element.78.refs_6_), channel_id=1, source_target_pairs={{0,24},{8,16},{16,8},{24,0},{1,25},{9,17},{17,9},{25,1},{2,26},{10... | collective-permute-start | bytes 491528 | tf_op jit(solution)/shard_map/ppermute | solution.py:364
  29.5 0.5 %collective-permute-start.12 = (f32[320,128]{1,0:T(8,128)S(1)}, f32[320,128]{1,0:T(8,128)S(1)}, u32[]{:S(2)}, u32[]{:S(2)}) collective-permute-start(f32[320,128]{1,0:T(8,128)S(1)} %get-tuple-element.78.refs_6_), channel_id=1, source_target_pairs={{0,16},{8,24},{16,0},{24,8},{1,17},{9,25},{17,1},{25,9},{2,18},{10... | collective-permute-start | bytes 491528 | tf_op jit(solution)/shard_map/ppermute | solution.py:364
  30.0 0.6 %collective-permute-start.10 = (f32[320,128]{1,0:T(8,128)S(1)}, f32[320,128]{1,0:T(8,128)S(1)}, u32[]{:S(2)}, u32[]{:S(2)}) collective-permute-start(f32[320,128]{1,0:T(8,128)S(1)} %get-tuple-element.78.refs_6_), channel_id=1, source_target_pairs={{0,8},{8,0},{16,24},{24,16},{1,9},{9,1},{17,25},{25,17},{2,10},{10... | collective-permute-start | bytes 491528 | tf_op jit(solution)/shard_map/ppermute | solution.py:364
  30.7 0.5 %collective-permute-start.6 = (f32[256,128]{1,0:T(8,128)S(1)}, f32[256,128]{1,0:T(8,128)S(1)}, u32[]{:S(2)}, u32[]{:S(2)}) collective-permute-start(f32[256,128]{1,0:T(8,128)S(1)} %get-tuple-element.75.refs_2_), channel_id=1, source_target_pairs={{0,1},{1,0},{2,3},{3,2},{4,5},{5,4},{6,7},{7,6},{8,9},{9,8},{10,11... | collective-permute-start | bytes 393224 | tf_op jit(solution)/shard_map/ppermute | solution.py:361
  31.2 0.8 %collective-permute-done.4.away = f32[4,64,128]{2,1,0:T(8,128)S(1)} collective-permute-done((f32[4,64,128]{2,1,0:T(8,128)S(1)}, f32[4,64,128]{2,1,0:T(8,128)S(1)}, u32[]{:S(2)}, u32[]{:S(2)}) %collective-permute-start.4) | collective-permute-done | bytes 131104 | tf_op jit(solution)/shard_map/ppermute | solution.py:361
  32.2 2.3 %collective-permute-done.14.refs_12_ = f32[320,128]{1,0:T(8,128)S(1)} collective-permute-done((f32[320,128]{1,0:T(8,128)S(1)}, f32[320,128]{1,0:T(8,128)S(1)}, u32[]{:S(2)}, u32[]{:S(2)}) %collective-permute-start.14) | collective-permute-done | bytes 163872 | tf_op jit(solution)/shard_map/ppermute | solution.py:364
  34.4 1.4 %collective-permute-done.12.refs_10_ = f32[320,128]{1,0:T(8,128)S(1)} collective-permute-done((f32[320,128]{1,0:T(8,128)S(1)}, f32[320,128]{1,0:T(8,128)S(1)}, u32[]{:S(2)}, u32[]{:S(2)}) %collective-permute-start.12) | collective-permute-done | bytes 163872 | tf_op jit(solution)/shard_map/ppermute | solution.py:364
  35.9 0.5 %collective-permute-start.11 = (f32[320,128]{1,0:T(8,128)S(1)}, f32[320,128]{1,0:T(8,128)S(1)}, u32[]{:S(2)}, u32[]{:S(2)}) collective-permute-start(f32[320,128]{1,0:T(8,128)S(1)} %collective-permute-done.10.refs_8_), channel_id=1, source_target_pairs={{0,1},{1,0},{2,3},{3,2},{4,5},{5,4},{6,7},{7,6},{8,9},{9,8},{10,11... | collective-permute-start | bytes 491528 | tf_op jit(solution)/shard_map/ppermute | solution.py:361
  36.6 1.2 %collective-permute-done.8.refs_5_ = f32[256,128]{1,0:T(8,128)S(1)} collective-permute-done((f32[256,128]{1,0:T(8,128)S(1)}, f32[256,128]{1,0:T(8,128)S(1)}, u32[]{:S(2)}, u32[]{:S(2)}) %collective-permute-start.8) | collective-permute-done | bytes 131104 | tf_op jit(solution)/shard_map/ppermute | solution.py:361
  37.8 1.1 %shard_map.126 = (f32[512,128]{1,0:T(8,128)}, f32[3,512,128]{2,1,0:T(8,128)}, f32[512,128]{1,0:T(8,128)}) custom-call(s32[1]{0:T(128)S(6)} %copy.18.child.refs_0_, f32[2,256,128]{2,1,0:T(8,128)S(1)} %get-tuple-element.68.refs_0_.solved, f32[256,128]{1,0:T(8,128)S(1)} %get-tuple-element.74.refs_0_, f32[256,128]{1,0:T(8,128)S(1)} %collective-permute-done.5.refs_1_, ...), custom_call_target="tpu_custom_call" | custom-call | flops 65536 | bytes 2686980 | tf_op jit(solution)/shard_map/pallas_call | solution.py:43
  (30 shorter events, 2.2 us)
Async XLA Ops:
  2.6 1.6 %collective-permute-start = (f32[320,128]{1,0:T(8,128)S(1)}, f32[320,128]{1,0:T(8,128)S(1)}, u32[]{:S(2)}, u32[]{:S(2)}) collective-permute-start(f32[320,128]{1,0:T(8,128)S(1)} %get-tuple-element.52), channel_id=1, source_target_pairs={{0,1},{1,0},{2,3},{3,2},{4,5},{5,4},{6,7},{7,6},{8,9},{9,8},{10,11... | collective-permute-start | bytes 491528 | tf_op jit(solution)/shard_map/ppermute | solution.py:361
  3.1 4.9 %copy-start = (f32[1,1,3,256,256]{4,3,2,1,0:T(8,128)S(1)}, f32[1,1,3,256,256]{4,3,2,1,0:T(8,128)}, u32[]{:S(2)}) copy-start(f32[1,1,3,256,256]{4,3,2,1,0:T(8,128)} %param.13) | copy-start | bytes 2359300
  4.2 3.9 %copy-start.1 = (f32[1,1,3,128,128]{4,3,2,1,0:T(8,128)S(1)}, f32[1,1,3,128,128]{4,3,2,1,0:T(8,128)}, u32[]{:S(2)}) copy-start(f32[1,1,3,128,128]{4,3,2,1,0:T(8,128)} %param.14) | copy-start | bytes 589828
  4.2 3.9 %copy-start.2 = (f32[1,1,3,128,128]{4,3,2,1,0:T(8,128)S(1)}, f32[1,1,3,128,128]{4,3,2,1,0:T(8,128)}, u32[]{:S(2)}) copy-start(f32[1,1,3,128,128]{4,3,2,1,0:T(8,128)} %param.15) | copy-start | bytes 589828
  4.4 6.8 %collective-permute-start.1 = (f32[256,128]{1,0:T(8,128)S(1)}, f32[256,128]{1,0:T(8,128)S(1)}, u32[]{:S(2)}, u32[]{:S(2)}) collective-permute-start(f32[256,128]{1,0:T(8,128)S(1)} %get-tuple-element.56.home), channel_id=1, source_target_pairs={{0,2},{1,3},{2,0},{3,1},{4,6},{5,7},{6,4},{7,5},{8,10},{9,11},{10,... | collective-permute-start | bytes 393224 | tf_op jit(solution)/shard_map/ppermute | solution.py:361
  11.4 15.5 %collective-permute-start.7 = (f32[256,128]{1,0:T(8,128)S(1)}, f32[256,128]{1,0:T(8,128)S(1)}, u32[]{:S(2)}, u32[]{:S(2)}) collective-permute-start(f32[256,128]{1,0:T(8,128)S(1)} %get-tuple-element.76.home), channel_id=1, source_target_pairs={{0,4},{1,5},{2,6},{3,7},{4,0},{5,1},{6,2},{7,3},{8,12},{9,13},{10,... | collective-permute-start | bytes 393224 | tf_op jit(solution)/shard_map/ppermute | solution.py:361
  14.2 7.3 %collective-permute-start.2 = (f32[64,128]{1,0:T(8,128)S(1)}, f32[64,128]{1,0:T(8,128)S(1)}, u32[]{:S(2)}, u32[]{:S(2)}) collective-permute-start(f32[64,128]{1,0:T(8,128)S(1)} %get-tuple-element.65.refs_0_), channel_id=1, source_target_pairs={{0,4},{1,5},{2,6},{3,7},{4,0},{5,1},{6,2},{7,3},{8,12},{9,13},{10,... | collective-permute-start | bytes 98312 | tf_op jit(solution)/shard_map/ppermute | solution.py:361
  21.6 4.3 %collective-permute-start.3 = (f32[2,64,128]{2,1,0:T(8,128)S(1)}, f32[2,64,128]{2,1,0:T(8,128)S(1)}, u32[]{:S(2)}, u32[]{:S(2)}) collective-permute-start(f32[2,64,128]{2,1,0:T(8,128)S(1)} %shard_map.120.home), channel_id=1, source_target_pairs={{0,2},{1,3},{2,0},{3,1},{4,6},{5,7},{6,4},{7,5},{8,10},{9,11},{10,... | collective-permute-start | bytes 196616 | tf_op jit(solution)/shard_map/ppermute | solution.py:361
  22.1 8.5 %collective-permute-start.5 = (f32[256,128]{1,0:T(8,128)S(1)}, f32[256,128]{1,0:T(8,128)S(1)}, u32[]{:S(2)}, u32[]{:S(2)}) collective-permute-start(f32[256,128]{1,0:T(8,128)S(1)} %get-tuple-element.74.refs_0_), channel_id=1, source_target_pairs={{0,1},{1,0},{2,3},{3,2},{4,5},{5,4},{6,7},{7,6},{8,9},{9,8},{10,11... | collective-permute-start | bytes 393224 | tf_op jit(solution)/shard_map/ppermute | solution.py:361
  27.1 7.3 %collective-permute-start.14 = (f32[320,128]{1,0:T(8,128)S(1)}, f32[320,128]{1,0:T(8,128)S(1)}, u32[]{:S(2)}, u32[]{:S(2)}) collective-permute-start(f32[320,128]{1,0:T(8,128)S(1)} %get-tuple-element.78.refs_6_), channel_id=1, source_target_pairs={{0,24},{8,16},{16,8},{24,0},{1,25},{9,17},{17,9},{25,1},{2,26},{10... | collective-permute-start | bytes 491528 | tf_op jit(solution)/shard_map/ppermute | solution.py:364
  29.5 6.4 %collective-permute-start.12 = (f32[320,128]{1,0:T(8,128)S(1)}, f32[320,128]{1,0:T(8,128)S(1)}, u32[]{:S(2)}, u32[]{:S(2)}) collective-permute-start(f32[320,128]{1,0:T(8,128)S(1)} %get-tuple-element.78.refs_6_), channel_id=1, source_target_pairs={{0,16},{8,24},{16,0},{24,8},{1,17},{9,25},{17,1},{25,9},{2,18},{10... | collective-permute-start | bytes 491528 | tf_op jit(solution)/shard_map/ppermute | solution.py:364
  30.0 5.9 %collective-permute-start.10 = (f32[320,128]{1,0:T(8,128)S(1)}, f32[320,128]{1,0:T(8,128)S(1)}, u32[]{:S(2)}, u32[]{:S(2)}) collective-permute-start(f32[320,128]{1,0:T(8,128)S(1)} %get-tuple-element.78.refs_6_), channel_id=1, source_target_pairs={{0,8},{8,0},{16,24},{24,16},{1,9},{9,1},{17,25},{25,17},{2,10},{10... | collective-permute-start | bytes 491528 | tf_op jit(solution)/shard_map/ppermute | solution.py:364
  30.7 1.3 %collective-permute-start.4 = (f32[4,64,128]{2,1,0:T(8,128)S(1)}, f32[4,64,128]{2,1,0:T(8,128)S(1)}, u32[]{:S(2)}, u32[]{:S(2)}) collective-permute-start(f32[4,64,128]{2,1,0:T(8,128)S(1)} %shard_map.122.home.tails), channel_id=1, source_target_pairs={{0,1},{1,0},{2,3},{3,2},{4,5},{5,4},{6,7},{7,6},{8,9},{9,8},{10,11... | collective-permute-start | bytes 393224 | tf_op jit(solution)/shard_map/ppermute | solution.py:361
  30.7 5.7 %collective-permute-start.6 = (f32[256,128]{1,0:T(8,128)S(1)}, f32[256,128]{1,0:T(8,128)S(1)}, u32[]{:S(2)}, u32[]{:S(2)}) collective-permute-start(f32[256,128]{1,0:T(8,128)S(1)} %get-tuple-element.75.refs_2_), channel_id=1, source_target_pairs={{0,1},{1,0},{2,3},{3,2},{4,5},{5,4},{6,7},{7,6},{8,9},{9,8},{10,11... | collective-permute-start | bytes 393224 | tf_op jit(solution)/shard_map/ppermute | solution.py:361
  32.0 5.7 %collective-permute-start.9 = (f32[320,128]{1,0:T(8,128)S(1)}, f32[320,128]{1,0:T(8,128)S(1)}, u32[]{:S(2)}, u32[]{:S(2)}) collective-permute-start(f32[320,128]{1,0:T(8,128)S(1)} %get-tuple-element.78.refs_6_), channel_id=1, source_target_pairs={{0,1},{1,0},{2,3},{3,2},{4,5},{5,4},{6,7},{7,6},{8,9},{9,8},{10,11... | collective-permute-start | bytes 491528 | tf_op jit(solution)/shard_map/ppermute | solution.py:361
  34.4 4.5 %collective-permute-start.15 = (f32[320,128]{1,0:T(8,128)S(1)}, f32[320,128]{1,0:T(8,128)S(1)}, u32[]{:S(2)}, u32[]{:S(2)}) collective-permute-start(f32[320,128]{1,0:T(8,128)S(1)} %collective-permute-done.14.refs_12_), channel_id=1, source_target_pairs={{0,1},{1,0},{2,3},{3,2},{4,5},{5,4},{6,7},{7,6},{8,9},{9,8},{10,11... | collective-permute-start | bytes 491528 | tf_op jit(solution)/shard_map/ppermute | solution.py:361
  35.9 3.0 %collective-permute-start.13 = (f32[320,128]{1,0:T(8,128)S(1)}, f32[320,128]{1,0:T(8,128)S(1)}, u32[]{:S(2)}, u32[]{:S(2)}) collective-permute-start(f32[320,128]{1,0:T(8,128)S(1)} %collective-permute-done.12.refs_10_), channel_id=1, source_target_pairs={{0,1},{1,0},{2,3},{3,2},{4,5},{5,4},{6,7},{7,6},{8,9},{9,8},{10,11... | collective-permute-start | bytes 491528 | tf_op jit(solution)/shard_map/ppermute | solution.py:361
  35.9 3.0 %collective-permute-start.11 = (f32[320,128]{1,0:T(8,128)S(1)}, f32[320,128]{1,0:T(8,128)S(1)}, u32[]{:S(2)}, u32[]{:S(2)}) collective-permute-start(f32[320,128]{1,0:T(8,128)S(1)} %collective-permute-done.10.refs_8_), channel_id=1, source_target_pairs={{0,1},{1,0},{2,3},{3,2},{4,5},{5,4},{6,7},{7,6},{8,9},{9,8},{10,11... | collective-permute-start | bytes 491528 | tf_op jit(solution)/shard_map/ppermute | solution.py:361
  36.4 1.3 %collective-permute-start.8 = (f32[256,128]{1,0:T(8,128)S(1)}, f32[256,128]{1,0:T(8,128)S(1)}, u32[]{:S(2)}, u32[]{:S(2)}) collective-permute-start(f32[256,128]{1,0:T(8,128)S(1)} %get-tuple-element.77.refs_4_), channel_id=1, source_target_pairs={{0,1},{1,0},{2,3},{3,2},{4,5},{5,4},{6,7},{7,6},{8,9},{9,8},{10,11... | collective-permute-start | bytes 393224 | tf_op jit(solution)/shard_map/ppermute | solution.py:361

commit v9 on v7

--- a/solution.py
+++ b/solution.py
@@ -77,12 +77,10 @@
             ]
         )
     ]
-    for copy in copies[:5]:
+    for copy in copies:
         copy.start()
     for copy in copies[:2]:
         copy.wait()
-    for copy in copies[5:]:
-        copy.start()
     solved = product(generator_here[:, :size], inverse_here[...])
     solve_map[...] = solved
     copies[2].wait()
@@ -298,40 +296,37 @@
                 value = both_rows(here ^ front) + product(value, root_maps[here ^ front])
             incoming[...] = wide_left(value)
 
-    step = half // 2
     copies = []
-    for chunk in range(4):
-        first = (core if chunk < 2 else 1 - core) * half + chunk % 2 * step
-        outs = targets(leaf_out, node_out, root_out, pl.ds(pl.multiple_of(first, 8), step))
+    for part in range(2):
+        outs = targets(leaf_out, node_out, root_out, part_rows(part, half))
         copies.append(
             [
-                pltpu.make_async_copy(result.at[chunk, i], out, sems.at[chunk, i])
+                pltpu.make_async_copy(result.at[part, i], out, sems.at[part, i])
                 for i, out in enumerate(outs)
             ]
         )
 
     def update(first, last):
-        for chunk in range(4):
-            part, inner = chunk // 2, slice(chunk % 2 * step, (chunk % 2 + 1) * step)
+        for part in range(2):
             change = wide_dot(
-                incoming[chunk * step : (chunk + 1) * step, :], wide_maps[:, first * size : last * size]
+                incoming[part * half : (part + 1) * half, :], wide_maps[:, first * size : last * size]
             )
             for i in range(first, last):
                 if i == 0:
-                    base = solved[part, inner, :]
+                    base = solved[part]
                 elif i <= height:
-                    base = nodes[2 * (i - 1) + part][inner, :]
+                    base = nodes[2 * (i - 1) + part][...]
                 else:
-                    base = roots[part][inner, :]
-                result[chunk, i] = base + change[:, (i - first) * size : (i + 1 - first) * size]
-                copies[chunk][i].start()
+                    base = roots[part][:half, :]
+                result[part, i] = base + change[:, (i - first) * size : (i + 1 - first) * size]
+                copies[part][i].start()
 
     for i in range(height + 1):
         first = jnp.logical_and(late[i], jnp.logical_not(late[i - 1])) if i else late[0]
         pl.when(first)(functools.partial(update, i, count))
     for i, flag in enumerate(late):
-        for chunk in range(4):
-            pl.when(flag)(copies[chunk][i].wait)
+        for part in range(2):
+            pl.when(flag)(copies[part][i].wait)
 
 
 def shards(
@@ -541,8 +536,8 @@
         scratch_shapes=[
             pltpu.VMEM((fronts, k_rows, size), f32),
             pltpu.VMEM((rows, 3 * size), bf16),
-            pltpu.VMEM((4, height + 2, rows // 4, size), f32),
-            pltpu.SemaphoreType.DMA((4, height + 2)),
+            pltpu.VMEM((2, height + 2, half, size), f32),
+            pltpu.SemaphoreType.DMA((2, height + 2)),
         ],
     )
     return (leaf_out[None], node_out[None, None], root_out[None])

time: 40.1 us -> 39.9 us (level)
  the two profiles are of different devices: /device:TPU:0 before, /device:TPU:21 now
where the time goes in v9:
time: 39.9 us; the launch traced here: 39.8 us
  starting transfers between devices  20.4 us (51%)
  waiting for transfers between devices  9.68 us (24%)
  Pallas kernels  8.25 us (21%)
  between operations  1.45 us (4%)
    ppermute x13, starting transfers between devices, blk_swap(): return lax.ppermute(value, 'blk', [(i, i ^ mask) for i in range(leaves)])  17.7 us
    pallas_call x16, Pallas kernels, call(): pl.pallas_call(kernel, out_shape=out_shape, in_specs=in_specs or [vmem] *...  8.25 us
    ppermute x13, waiting for transfers between devices, blk_swap(): return lax.ppermute(value, 'blk', [(i, i ^ mask) for i in range(leaves)])  8.21 us
    ppermute x3, starting transfers between devices, level_swap(): return lax.ppermute(value, 'level', [(i, i ^ mask) for i in range(fronts)])  2.71 us
    ppermute x3, waiting for transfers between devices, level_swap(): return lax.ppermute(value, 'level', [(i, i ^ mask) for i in range(fronts)])  1.47 us
  transfers between devices with their start and end apart: 16, of which 7 were waited for; matrix products, arithmetic and copies ran while one was open for 0% of the time, Pallas kernels for 11%

profile of v9, /device:TPU:21, one launch (start us, length us, event | category | flops | bytes accessed | tf_op | source)
XLA Modules:
  0.0 39.8 jit_solution(10829174249231358542)
XLA Ops:
  0.6 1.9 %shard_map.112 = (f32[320,128]{1,0:T(8,128)S(1)}, f32[256,128]{1,0:T(8,128)S(1)}, bf16[768,128]{1,0:T(8,128)(2,1)S(1)}, f32[2,256,256]{2,1,0:T(8,128)S(1)}, f32[...) custom-call(f32[512,256]{1,0:T(8,128)} %bitcast.23, ...), custom_call_target="tpu_custom_call" | custom-call | flops 113246208 | bytes 3768320 | tf_op jit(solution)/shard_map/pallas_call | solution.py:43
  2.6 0.7 %collective-permute-start = (f32[320,128]{1,0:T(8,128)S(1)}, f32[320,128]{1,0:T(8,128)S(1)}, u32[]{:S(2)}, u32[]{:S(2)}) collective-permute-start(f32[320,128]{1,0:T(8,128)S(1)} %get-tuple-element.52), channel_id=1, source_target_pairs={{0,1},{1,0},{2,3},{3,2},{4,5},{5,4},{6,7},{7,6},{8,9},{9,8},{10,11... | collective-permute-start | bytes 491528 | tf_op jit(solution)/shard_map/ppermute | solution.py:358
  3.3 0.8 %shard_map.113 = (bf16[1,384,256]{2,1,0:T(8,128)(2,1)S(1)}, bf16[1,384,256]{2,1,0:T(8,128)(2,1)S(1)}, f32[256,256]{1,0:T(8,128)S(1)}, f32[64,128]{1,0:T(8,128)S(1)}) custom-call(f32[256,256]{1,0:T(8,128)S(1)} %get-tuple-element.44.generator, f32[128,128]{1,0:T(8,128)S(1)} %get-tuple-element.45.inverse, f32[128,128]{1,0:T(8,128)S(1)} %get-tuple-element.46.lower, ...), custom_call_target="tpu_custom_call" | custom-call | flops 176160768 | bytes 1933312 | tf_op jit(solution)/shard_map/pallas_call | solution.py:43
  4.6 1.4 %collective-permute-start.1 = (f32[256,128]{1,0:T(8,128)S(1)}, f32[256,128]{1,0:T(8,128)S(1)}, u32[]{:S(2)}, u32[]{:S(2)}) collective-permute-start(f32[256,128]{1,0:T(8,128)S(1)} %get-tuple-element.56.home), channel_id=1, source_target_pairs={{0,2},{1,3},{2,0},{3,1},{4,6},{5,7},{6,4},{7,5},{8,10},{9,11},{10,... | collective-permute-start | bytes 393224 | tf_op jit(solution)/shard_map/ppermute | solution.py:358
  6.6 0.4 shard_map.115
  7.6 1.8 %collective-permute-done.1.away = f32[256,128]{1,0:T(8,128)S(1)} collective-permute-done((f32[256,128]{1,0:T(8,128)S(1)}, f32[256,128]{1,0:T(8,128)S(1)}, u32[]{:S(2)}, u32[]{:S(2)}) %collective-permute-start.1) | collective-permute-done | bytes 131104 | tf_op jit(solution)/shard_map/ppermute | solution.py:358
  9.7 2.3 %collective-permute-start.2 = (f32[64,128]{1,0:T(8,128)S(1)}, f32[64,128]{1,0:T(8,128)S(1)}, u32[]{:S(2)}, u32[]{:S(2)}) collective-permute-start(f32[64,128]{1,0:T(8,128)S(1)} %get-tuple-element.65.refs_0_), channel_id=1, source_target_pairs={{0,4},{1,5},{2,6},{3,7},{4,0},{5,1},{6,2},{7,3},{8,12},{9,13},{10,... | collective-permute-start | bytes 98312 | tf_op jit(solution)/shard_map/ppermute | solution.py:358
  12.0 3.4 %collective-permute-done.2.far = f32[64,128]{1,0:T(8,128)S(1)} collective-permute-done((f32[64,128]{1,0:T(8,128)S(1)}, f32[64,128]{1,0:T(8,128)S(1)}, u32[]{:S(2)}, u32[]{:S(2)}) %collective-permute-start.2) | collective-permute-done | bytes 32800 | tf_op jit(solution)/shard_map/ppermute | solution.py:358
  15.4 5.9 %collective-permute-start.3 = (f32[2,64,128]{2,1,0:T(8,128)S(1)}, f32[2,64,128]{2,1,0:T(8,128)S(1)}, u32[]{:S(2)}, u32[]{:S(2)}) collective-permute-start(f32[2,64,128]{2,1,0:T(8,128)S(1)} %shard_map.120.home), channel_id=1, source_target_pairs={{0,2},{1,3},{2,0},{3,1},{4,6},{5,7},{6,4},{7,5},{8,10},{9,11},{10,... | collective-permute-start | bytes 196616 | tf_op jit(solution)/shard_map/ppermute | solution.py:358
  21.4 0.8 %collective-permute-start.5 = (f32[256,128]{1,0:T(8,128)S(1)}, f32[256,128]{1,0:T(8,128)S(1)}, u32[]{:S(2)}, u32[]{:S(2)}) collective-permute-start(f32[256,128]{1,0:T(8,128)S(1)} %get-tuple-element.74.refs_0_), channel_id=1, source_target_pairs={{0,1},{1,0},{2,3},{3,2},{4,5},{5,4},{6,7},{7,6},{8,9},{9,8},{10,11... | collective-permute-start | bytes 393224 | tf_op jit(solution)/shard_map/ppermute | solution.py:358
  22.1 0.4 shard_map.121
  22.5 0.8 %collective-permute-done.3.away = f32[2,64,128]{2,1,0:T(8,128)S(1)} collective-permute-done((f32[2,64,128]{2,1,0:T(8,128)S(1)}, f32[2,64,128]{2,1,0:T(8,128)S(1)}, u32[]{:S(2)}, u32[]{:S(2)}) %collective-permute-start.3) | collective-permute-done | bytes 65568 | tf_op jit(solution)/shard_map/ppermute | solution.py:358
  23.9 0.4 %shard_map.119 = (f32[2,256,128]{2,1,0:T(8,128)S(1)}, f32[128,128]{1,0:T(8,128)S(1)}) custom-call(f32[2,256,128]{2,1,0:T(8,128)S(1)} %get-tuple-element.66.solved_early, f32[128,128]{1,0:T(8,128)S(1)} %get-tuple-element.67.map_early, s32[1]{0:T(128)S(6)} %copy.18.child.refs_0_, f32[2,256,256]{2,1,0:T(8,128)S(1)} %get-tuple-element.47.right.refs_1_, ...), custom_call_target="tpu_custom_call" | custom-call | flops 125829120 | bytes 1441796 | tf_op jit(solution)/shard_map/pallas_call | solution.py:43
  24.6 1.2 %collective-permute-start.14 = (f32[320,128]{1,0:T(8,128)S(1)}, f32[320,128]{1,0:T(8,128)S(1)}, u32[]{:S(2)}, u32[]{:S(2)}) collective-permute-start(f32[320,128]{1,0:T(8,128)S(1)} %get-tuple-element.78.refs_6_), channel_id=1, source_target_pairs={{0,24},{8,16},{16,8},{24,0},{1,25},{9,17},{17,9},{25,1},{2,26},{10... | collective-permute-start | bytes 491528 | tf_op jit(solution)/shard_map/ppermute | solution.py:361
  25.8 1.2 %collective-permute-start.12 = (f32[320,128]{1,0:T(8,128)S(1)}, f32[320,128]{1,0:T(8,128)S(1)}, u32[]{:S(2)}, u32[]{:S(2)}) collective-permute-start(f32[320,128]{1,0:T(8,128)S(1)} %get-tuple-element.78.refs_6_), channel_id=1, source_target_pairs={{0,16},{8,24},{16,0},{24,8},{1,17},{9,25},{17,1},{25,9},{2,18},{10... | collective-permute-start | bytes 491528 | tf_op jit(solution)/shard_map/ppermute | solution.py:361
  27.3 1.9 %collective-permute-start.4 = (f32[4,64,128]{2,1,0:T(8,128)S(1)}, f32[4,64,128]{2,1,0:T(8,128)S(1)}, u32[]{:S(2)}, u32[]{:S(2)}) collective-permute-start(f32[4,64,128]{2,1,0:T(8,128)S(1)} %shard_map.122.home.tails), channel_id=1, source_target_pairs={{0,1},{1,0},{2,3},{3,2},{4,5},{5,4},{6,7},{7,6},{8,9},{9,8},{10,11... | collective-permute-start | bytes 393224 | tf_op jit(solution)/shard_map/ppermute | solution.py:358
  29.2 1.0 %collective-permute-done.4.away = f32[4,64,128]{2,1,0:T(8,128)S(1)} collective-permute-done((f32[4,64,128]{2,1,0:T(8,128)S(1)}, f32[4,64,128]{2,1,0:T(8,128)S(1)}, u32[]{:S(2)}, u32[]{:S(2)}) %collective-permute-start.4) | collective-permute-done | bytes 131104 | tf_op jit(solution)/shard_map/ppermute | solution.py:358
  30.6 3.2 %collective-permute-start.15 = (f32[320,128]{1,0:T(8,128)S(1)}, f32[320,128]{1,0:T(8,128)S(1)}, u32[]{:S(2)}, u32[]{:S(2)}) collective-permute-start(f32[320,128]{1,0:T(8,128)S(1)} %collective-permute-done.14.refs_12_), channel_id=1, source_target_pairs={{0,1},{1,0},{2,3},{3,2},{4,5},{5,4},{6,7},{7,6},{8,9},{9,8},{10,11... | collective-permute-start | bytes 491528 | tf_op jit(solution)/shard_map/ppermute | solution.py:358
  33.7 1.5 %collective-permute-done.12.refs_10_ = f32[320,128]{1,0:T(8,128)S(1)} collective-permute-done((f32[320,128]{1,0:T(8,128)S(1)}, f32[320,128]{1,0:T(8,128)S(1)}, u32[]{:S(2)}, u32[]{:S(2)}) %collective-permute-start.12) | collective-permute-done | bytes 163872 | tf_op jit(solution)/shard_map/ppermute | solution.py:361
  35.2 0.5 %collective-permute-start.13 = (f32[320,128]{1,0:T(8,128)S(1)}, f32[320,128]{1,0:T(8,128)S(1)}, u32[]{:S(2)}, u32[]{:S(2)}) collective-permute-start(f32[320,128]{1,0:T(8,128)S(1)} %collective-permute-done.12.refs_10_), channel_id=1, source_target_pairs={{0,1},{1,0},{2,3},{3,2},{4,5},{5,4},{6,7},{7,6},{8,9},{9,8},{10,11... | collective-permute-start | bytes 491528 | tf_op jit(solution)/shard_map/ppermute | solution.py:358
  35.7 0.5 %collective-permute-start.8 = (f32[256,128]{1,0:T(8,128)S(1)}, f32[256,128]{1,0:T(8,128)S(1)}, u32[]{:S(2)}, u32[]{:S(2)}) collective-permute-start(f32[256,128]{1,0:T(8,128)S(1)} %get-tuple-element.77.refs_4_), channel_id=1, source_target_pairs={{0,1},{1,0},{2,3},{3,2},{4,5},{5,4},{6,7},{7,6},{8,9},{9,8},{10,11... | collective-permute-start | bytes 393224 | tf_op jit(solution)/shard_map/ppermute | solution.py:358
  36.3 1.0 %collective-permute-done.8.refs_5_ = f32[256,128]{1,0:T(8,128)S(1)} collective-permute-done((f32[256,128]{1,0:T(8,128)S(1)}, f32[256,128]{1,0:T(8,128)S(1)}, u32[]{:S(2)}, u32[]{:S(2)}) %collective-permute-start.8) | collective-permute-done | bytes 131104 | tf_op jit(solution)/shard_map/ppermute | solution.py:358
  37.3 0.9 %shard_map.126 = (f32[512,128]{1,0:T(8,128)}, f32[3,512,128]{2,1,0:T(8,128)}, f32[512,128]{1,0:T(8,128)}) custom-call(s32[1]{0:T(128)S(6)} %copy.18.child.refs_0_, f32[2,256,128]{2,1,0:T(8,128)S(1)} %get-tuple-element.68.refs_0_.solved, f32[256,128]{1,0:T(8,128)S(1)} %get-tuple-element.74.refs_0_, f32[256,128]{1,0:T(8,128)S(1)} %collective-permute-done.5.refs_1_, ...), custom_call_target="tpu_custom_call" | custom-call | flops 65536 | bytes 2686980 | tf_op jit(solution)/shard_map/pallas_call | solution.py:43
  38.2 1.6 %shard_map.127 = (f32[512,128]{1,0:T(8,128)}, f32[3,512,128]{2,1,0:T(8,128)}, f32[512,128]{1,0:T(8,128)}) custom-call(s32[1]{0:T(128)S(6)} %copy.18.child.refs_0_, f32[2,256,128]{2,1,0:T(8,128)S(1)} %get-tuple-element.68.refs_0_.solved, bf16[384,640]{1,0:T(8,128)(2,1)S(1)} %shard_map.123.wide_maps, ...), custom_call_target="tpu_custom_call", output_to_operand_aliasing={{0}: (17, {}), {1}: (18, {}), {2}: (19, {})} | custom-call | flops 251658240 | bytes 5472260 | tf_op jit(solution)/shard_map/pallas_call | solution.py:43
  (30 shorter events, 3.0 us)
Async XLA Ops:
  2.6 1.8 %collective-permute-start = (f32[320,128]{1,0:T(8,128)S(1)}, f32[320,128]{1,0:T(8,128)S(1)}, u32[]{:S(2)}, u32[]{:S(2)}) collective-permute-start(f32[320,128]{1,0:T(8,128)S(1)} %get-tuple-element.52), channel_id=1, source_target_pairs={{0,1},{1,0},{2,3},{3,2},{4,5},{5,4},{6,7},{7,6},{8,9},{9,8},{10,11... | collective-permute-start | bytes 491528 | tf_op jit(solution)/shard_map/ppermute | solution.py:358
  3.3 3.3 %copy-start = (f32[1,1,3,256,256]{4,3,2,1,0:T(8,128)S(1)}, f32[1,1,3,256,256]{4,3,2,1,0:T(8,128)}, u32[]{:S(2)}) copy-start(f32[1,1,3,256,256]{4,3,2,1,0:T(8,128)} %param.13) | copy-start | bytes 2359300
  4.4 2.3 %copy-start.1 = (f32[1,1,3,128,128]{4,3,2,1,0:T(8,128)S(1)}, f32[1,1,3,128,128]{4,3,2,1,0:T(8,128)}, u32[]{:S(2)}) copy-start(f32[1,1,3,128,128]{4,3,2,1,0:T(8,128)} %param.14) | copy-start | bytes 589828
  4.4 2.3 %copy-start.2 = (f32[1,1,3,128,128]{4,3,2,1,0:T(8,128)S(1)}, f32[1,1,3,128,128]{4,3,2,1,0:T(8,128)}, u32[]{:S(2)}) copy-start(f32[1,1,3,128,128]{4,3,2,1,0:T(8,128)} %param.15) | copy-start | bytes 589828
  4.6 4.7 %collective-permute-start.1 = (f32[256,128]{1,0:T(8,128)S(1)}, f32[256,128]{1,0:T(8,128)S(1)}, u32[]{:S(2)}, u32[]{:S(2)}) collective-permute-start(f32[256,128]{1,0:T(8,128)S(1)} %get-tuple-element.56.home), channel_id=1, source_target_pairs={{0,2},{1,3},{2,0},{3,1},{4,6},{5,7},{6,4},{7,5},{8,10},{9,11},{10,... | collective-permute-start | bytes 393224 | tf_op jit(solution)/shard_map/ppermute | solution.py:358
  9.6 14.8 %collective-permute-start.7 = (f32[256,128]{1,0:T(8,128)S(1)}, f32[256,128]{1,0:T(8,128)S(1)}, u32[]{:S(2)}, u32[]{:S(2)}) collective-permute-start(f32[256,128]{1,0:T(8,128)S(1)} %get-tuple-element.76.home), channel_id=1, source_target_pairs={{0,4},{1,5},{2,6},{3,7},{4,0},{5,1},{6,2},{7,3},{8,12},{9,13},{10,... | collective-permute-start | bytes 393224 | tf_op jit(solution)/shard_map/ppermute | solution.py:358
  9.7 5.7 %collective-permute-start.2 = (f32[64,128]{1,0:T(8,128)S(1)}, f32[64,128]{1,0:T(8,128)S(1)}, u32[]{:S(2)}, u32[]{:S(2)}) collective-permute-start(f32[64,128]{1,0:T(8,128)S(1)} %get-tuple-element.65.refs_0_), channel_id=1, source_target_pairs={{0,4},{1,5},{2,6},{3,7},{4,0},{5,1},{6,2},{7,3},{8,12},{9,13},{10,... | collective-permute-start | bytes 98312 | tf_op jit(solution)/shard_map/ppermute | solution.py:358
  15.4 7.9 %collective-permute-start.3 = (f32[2,64,128]{2,1,0:T(8,128)S(1)}, f32[2,64,128]{2,1,0:T(8,128)S(1)}, u32[]{:S(2)}, u32[]{:S(2)}) collective-permute-start(f32[2,64,128]{2,1,0:T(8,128)S(1)} %shard_map.120.home), channel_id=1, source_target_pairs={{0,2},{1,3},{2,0},{3,1},{4,6},{5,7},{6,4},{7,5},{8,10},{9,11},{10,... | collective-permute-start | bytes 196616 | tf_op jit(solution)/shard_map/ppermute | solution.py:358
  21.4 7.9 %collective-permute-start.5 = (f32[256,128]{1,0:T(8,128)S(1)}, f32[256,128]{1,0:T(8,128)S(1)}, u32[]{:S(2)}, u32[]{:S(2)}) collective-permute-start(f32[256,128]{1,0:T(8,128)S(1)} %get-tuple-element.74.refs_0_), channel_id=1, source_target_pairs={{0,1},{1,0},{2,3},{3,2},{4,5},{5,4},{6,7},{7,6},{8,9},{9,8},{10,11... | collective-permute-start | bytes 393224 | tf_op jit(solution)/shard_map/ppermute | solution.py:358
  24.6 6.0 %collective-permute-start.14 = (f32[320,128]{1,0:T(8,128)S(1)}, f32[320,128]{1,0:T(8,128)S(1)}, u32[]{:S(2)}, u32[]{:S(2)}) collective-permute-start(f32[320,128]{1,0:T(8,128)S(1)} %get-tuple-element.78.refs_6_), channel_id=1, source_target_pairs={{0,24},{8,16},{16,8},{24,0},{1,25},{9,17},{17,9},{25,1},{2,26},{10... | collective-permute-start | bytes 491528 | tf_op jit(solution)/shard_map/ppermute | solution.py:361
  25.8 9.4 %collective-permute-start.12 = (f32[320,128]{1,0:T(8,128)S(1)}, f32[320,128]{1,0:T(8,128)S(1)}, u32[]{:S(2)}, u32[]{:S(2)}) collective-permute-start(f32[320,128]{1,0:T(8,128)S(1)} %get-tuple-element.78.refs_6_), channel_id=1, source_target_pairs={{0,16},{8,24},{16,0},{24,8},{1,17},{9,25},{17,1},{25,9},{2,18},{10... | collective-permute-start | bytes 491528 | tf_op jit(solution)/shard_map/ppermute | solution.py:361
  27.1 8.6 %collective-permute-start.10 = (f32[320,128]{1,0:T(8,128)S(1)}, f32[320,128]{1,0:T(8,128)S(1)}, u32[]{:S(2)}, u32[]{:S(2)}) collective-permute-start(f32[320,128]{1,0:T(8,128)S(1)} %get-tuple-element.78.refs_6_), channel_id=1, source_target_pairs={{0,8},{8,0},{16,24},{24,16},{1,9},{9,1},{17,25},{25,17},{2,10},{10... | collective-permute-start | bytes 491528 | tf_op jit(solution)/shard_map/ppermute | solution.py:361
  27.3 2.9 %collective-permute-start.4 = (f32[4,64,128]{2,1,0:T(8,128)S(1)}, f32[4,64,128]{2,1,0:T(8,128)S(1)}, u32[]{:S(2)}, u32[]{:S(2)}) collective-permute-start(f32[4,64,128]{2,1,0:T(8,128)S(1)} %shard_map.122.home.tails), channel_id=1, source_target_pairs={{0,1},{1,0},{2,3},{3,2},{4,5},{5,4},{6,7},{7,6},{8,9},{9,8},{10,11... | collective-permute-start | bytes 393224 | tf_op jit(solution)/shard_map/ppermute | solution.py:358
  29.2 6.5 %collective-permute-start.6 = (f32[256,128]{1,0:T(8,128)S(1)}, f32[256,128]{1,0:T(8,128)S(1)}, u32[]{:S(2)}, u32[]{:S(2)}) collective-permute-start(f32[256,128]{1,0:T(8,128)S(1)} %get-tuple-element.75.refs_2_), channel_id=1, source_target_pairs={{0,1},{1,0},{2,3},{3,2},{4,5},{5,4},{6,7},{7,6},{8,9},{9,8},{10,11... | collective-permute-start | bytes 393224 | tf_op jit(solution)/shard_map/ppermute | solution.py:358
  30.2 7.1 %collective-permute-start.9 = (f32[320,128]{1,0:T(8,128)S(1)}, f32[320,128]{1,0:T(8,128)S(1)}, u32[]{:S(2)}, u32[]{:S(2)}) collective-permute-start(f32[320,128]{1,0:T(8,128)S(1)} %get-tuple-element.78.refs_6_), channel_id=1, source_target_pairs={{0,1},{1,0},{2,3},{3,2},{4,5},{5,4},{6,7},{7,6},{8,9},{9,8},{10,11... | collective-permute-start | bytes 491528 | tf_op jit(solution)/shard_map/ppermute | solution.py:358
  30.6 7.6 %collective-permute-start.15 = (f32[320,128]{1,0:T(8,128)S(1)}, f32[320,128]{1,0:T(8,128)S(1)}, u32[]{:S(2)}, u32[]{:S(2)}) collective-permute-start(f32[320,128]{1,0:T(8,128)S(1)} %collective-permute-done.14.refs_12_), channel_id=1, source_target_pairs={{0,1},{1,0},{2,3},{3,2},{4,5},{5,4},{6,7},{7,6},{8,9},{9,8},{10,11... | collective-permute-start | bytes 491528 | tf_op jit(solution)/shard_map/ppermute | solution.py:358
  35.2 3.0 %collective-permute-start.13 = (f32[320,128]{1,0:T(8,128)S(1)}, f32[320,128]{1,0:T(8,128)S(1)}, u32[]{:S(2)}, u32[]{:S(2)}) collective-permute-start(f32[320,128]{1,0:T(8,128)S(1)} %collective-permute-done.12.refs_10_), channel_id=1, source_target_pairs={{0,1},{1,0},{2,3},{3,2},{4,5},{5,4},{6,7},{7,6},{8,9},{9,8},{10,11... | collective-permute-start | bytes 491528 | tf_op jit(solution)/shard_map/ppermute | solution.py:358
  35.7 2.5 %collective-permute-start.11 = (f32[320,128]{1,0:T(8,128)S(1)}, f32[320,128]{1,0:T(8,128)S(1)}, u32[]{:S(2)}, u32[]{:S(2)}) collective-permute-start(f32[320,128]{1,0:T(8,128)S(1)} %collective-permute-done.10.refs_8_), channel_id=1, source_target_pairs={{0,1},{1,0},{2,3},{3,2},{4,5},{5,4},{6,7},{7,6},{8,9},{9,8},{10,11... | collective-permute-start | bytes 491528 | tf_op jit(solution)/shard_map/ppermute | solution.py:358
  35.7 1.6 %collective-permute-start.8 = (f32[256,128]{1,0:T(8,128)S(1)}, f32[256,128]{1,0:T(8,128)S(1)}, u32[]{:S(2)}, u32[]{:S(2)}) collective-permute-start(f32[256,128]{1,0:T(8,128)S(1)} %get-tuple-element.77.refs_4_), channel_id=1, source_target_pairs={{0,1},{1,0},{2,3},{3,2},{4,5},{5,4},{6,7},{7,6},{8,9},{9,8},{10,11... | collective-permute-start | bytes 393224 | tf_op jit(solution)/shard_map/ppermute | solution.py:358

commit v10 on v7

--- a/solution.py
+++ b/solution.py
@@ -77,12 +77,10 @@
             ]
         )
     ]
-    for copy in copies[:5]:
+    for copy in copies:
         copy.start()
     for copy in copies[:2]:
         copy.wait()
-    for copy in copies[5:]:
-        copy.start()
     solved = product(generator_here[:, :size], inverse_here[...])
     solve_map[...] = solved
     copies[2].wait()
@@ -166,7 +164,7 @@
     node[...] = both[:, :size]
 
 
-def first_merge_kernel(base, away, other_maps, node, skeleton):
+def first_merge_kernel(base, away, other_maps, _, node, skeleton):
     half, size = node.shape
     both = base[...] + wide_dot(wide_left(away[:half, :]), other_maps[0])
     skeleton[...] = both[:, size:]
@@ -408,13 +406,14 @@
         fold_flops + 6 * part * (leaf_size + 2 * size) * size,
         scratch_shapes=[both],
     )
-    *node_params, away = lax.optimization_barrier((*node_params, away))
+    *node_params, child_leaf, away = lax.optimization_barrier((*node_params, child_leaf, away))
     away = blk_swap(away, 1)
     node, skeleton = call(
         first_merge_kernel,
         (array(half, size), array(half, size)),
-        (base, away, first_other),
+        (base, away, first_other, child_leaf),
         merge_flops,
+        in_specs=[vmem] * 3 + [smem],
     )
     nodes, away_first = [node], away
 
@@ -428,7 +427,6 @@
             scratch_shapes=[both],
         )
 
-    child_leaf, skeleton = lax.optimization_barrier((child_leaf, skeleton))
     for tier in range(1, height):
         away = blk_swap(skeleton, 1 << tier)
         after = ()

time: 40.1 us -> 40.8 us (1.017)
  waiting for transfers between devices: 18.6 us -> 19.8 us
    ppermute x13, waiting for transfers between devices: 14.9 us -> 16.1 us  [blk_swap(): return lax.ppermute(value, 'blk', [(i, i ^ mask) for i in range(leaves)])]
  transfers between devices with their start and end apart: 16 -> 16, of which waited for: 8 -> 7; matrix products, arithmetic and copies ran while one was open for 0% -> 0% of each run, Pallas kernels for 12% -> 11%
where the time goes in v10:
time: 40.8 us; the launch traced here: 40 us
  waiting for transfers between devices  19.8 us (49%)
  starting transfers between devices  11.5 us (28%)
  Pallas kernels  7.19 us (18%)
  between operations  1.45 us (4%)
    ppermute x13, waiting for transfers between devices, blk_swap(): return lax.ppermute(value, 'blk', [(i, i ^ mask) for i in range(leaves)])  16.1 us
    ppermute x13, starting transfers between devices, blk_swap(): return lax.ppermute(value, 'blk', [(i, i ^ mask) for i in range(leaves)])  7.99 us
    pallas_call x16, Pallas kernels, call(): pl.pallas_call(kernel, out_shape=out_shape, in_specs=in_specs or [vmem] *...  7.19 us
    ppermute x3, waiting for transfers between devices, level_swap(): return lax.ppermute(value, 'level', [(i, i ^ mask) for i in range(fronts)])  3.69 us
    ppermute x3, starting transfers between devices, level_swap(): return lax.ppermute(value, 'level', [(i, i ^ mask) for i in range(fronts)])  3.55 us
  transfers between devices with their start and end apart: 16, of which 7 were waited for; matrix products, arithmetic and copies ran while one was open for 0% of the time, Pallas kernels for 11%

profile of v10, /device:TPU:0, one launch (start us, length us, event | category | flops | bytes accessed | tf_op | source)
XLA Modules:
  0.0 40.0 jit_solution(11771648183847444150)
XLA Ops:
  0.6 1.9 %shard_map.112 = (f32[320,128]{1,0:T(8,128)S(1)}, f32[256,128]{1,0:T(8,128)S(1)}, bf16[768,128]{1,0:T(8,128)(2,1)S(1)}, f32[2,256,256]{2,1,0:T(8,128)S(1)}, f32[...) custom-call(f32[512,256]{1,0:T(8,128)} %bitcast.23, ...), custom_call_target="tpu_custom_call" | custom-call | flops 113246208 | bytes 3768320 | tf_op jit(solution)/shard_map/pallas_call | solution.py:43
  2.6 0.6 %collective-permute-start = (f32[320,128]{1,0:T(8,128)S(1)}, f32[320,128]{1,0:T(8,128)S(1)}, u32[]{:S(2)}, u32[]{:S(2)}) collective-permute-start(f32[320,128]{1,0:T(8,128)S(1)} %get-tuple-element.52), channel_id=1, source_target_pairs={{0,1},{1,0},{2,3},{3,2},{4,5},{5,4},{6,7},{7,6},{8,9},{9,8},{10,11... | collective-permute-start | bytes 491528 | tf_op jit(solution)/shard_map/ppermute | solution.py:361
  3.8 0.8 %shard_map.113 = (bf16[1,384,256]{2,1,0:T(8,128)(2,1)S(1)}, bf16[1,384,256]{2,1,0:T(8,128)(2,1)S(1)}, f32[256,256]{1,0:T(8,128)S(1)}, f32[64,128]{1,0:T(8,128)S(1)}) custom-call(f32[256,256]{1,0:T(8,128)S(1)} %get-tuple-element.45.generator, f32[128,128]{1,0:T(8,128)S(1)} %get-tuple-element.46.inverse, f32[128,128]{1,0:T(8,128)S(1)} %get-tuple-element.47.lower, ...), custom_call_target="tpu_custom_call" | custom-call | flops 176160768 | bytes 1933312 | tf_op jit(solution)/shard_map/pallas_call | solution.py:43
  4.8 2.7 %collective-permute-start.1 = (f32[256,128]{1,0:T(8,128)S(1)}, f32[256,128]{1,0:T(8,128)S(1)}, u32[]{:S(2)}, u32[]{:S(2)}) collective-permute-start(f32[256,128]{1,0:T(8,128)S(1)} %get-tuple-element.54.home), channel_id=1, source_target_pairs={{0,2},{1,3},{2,0},{3,1},{4,6},{5,7},{6,4},{7,5},{8,10},{9,11},{10,... | collective-permute-start | bytes 393224 | tf_op jit(solution)/shard_map/ppermute | solution.py:361
  7.5 0.4 shard_map.115
  7.9 0.3 shard_map.117
  8.4 3.2 %collective-permute-done.1.away = f32[256,128]{1,0:T(8,128)S(1)} collective-permute-done((f32[256,128]{1,0:T(8,128)S(1)}, f32[256,128]{1,0:T(8,128)S(1)}, u32[]{:S(2)}, u32[]{:S(2)}) %collective-permute-start.1) | collective-permute-done | bytes 131104 | tf_op jit(solution)/shard_map/ppermute | solution.py:361
  11.9 2.8 %collective-permute-start.7 = (f32[256,128]{1,0:T(8,128)S(1)}, f32[256,128]{1,0:T(8,128)S(1)}, u32[]{:S(2)}, u32[]{:S(2)}) collective-permute-start(f32[256,128]{1,0:T(8,128)S(1)} %get-tuple-element.74.home), channel_id=1, source_target_pairs={{0,4},{1,5},{2,6},{3,7},{4,0},{5,1},{6,2},{7,3},{8,12},{9,13},{10,... | collective-permute-start | bytes 393224 | tf_op jit(solution)/shard_map/ppermute | solution.py:361
  14.9 7.5 %collective-permute-done.2.far = f32[64,128]{1,0:T(8,128)S(1)} collective-permute-done((f32[64,128]{1,0:T(8,128)S(1)}, f32[64,128]{1,0:T(8,128)S(1)}, u32[]{:S(2)}, u32[]{:S(2)}) %collective-permute-start.2) | collective-permute-done | bytes 32800 | tf_op jit(solution)/shard_map/ppermute | solution.py:361
  22.4 0.5 %collective-permute-start.3 = (f32[2,64,128]{2,1,0:T(8,128)S(1)}, f32[2,64,128]{2,1,0:T(8,128)S(1)}, u32[]{:S(2)}, u32[]{:S(2)}) collective-permute-start(f32[2,64,128]{2,1,0:T(8,128)S(1)} %shard_map.120.home), channel_id=1, source_target_pairs={{0,2},{1,3},{2,0},{3,1},{4,6},{5,7},{6,4},{7,5},{8,10},{9,11},{10,... | collective-permute-start | bytes 196616 | tf_op jit(solution)/shard_map/ppermute | solution.py:361
  22.9 0.4 shard_map.121
  23.3 3.3 %collective-permute-done.3.away = f32[2,64,128]{2,1,0:T(8,128)S(1)} collective-permute-done((f32[2,64,128]{2,1,0:T(8,128)S(1)}, f32[2,64,128]{2,1,0:T(8,128)S(1)}, u32[]{:S(2)}, u32[]{:S(2)}) %collective-permute-start.3) | collective-permute-done | bytes 65568 | tf_op jit(solution)/shard_map/ppermute | solution.py:361
  26.6 0.4 shard_map.122.home.tails
  27.2 0.4 %shard_map.119 = (f32[2,256,128]{2,1,0:T(8,128)S(1)}, f32[128,128]{1,0:T(8,128)S(1)}) custom-call(f32[2,256,128]{2,1,0:T(8,128)S(1)} %get-tuple-element.64.solved_early, f32[128,128]{1,0:T(8,128)S(1)} %get-tuple-element.65.map_early, s32[1]{0:T(128)S(6)} %copy.18._.child.refs_0_, f32[2,256,256]{2,1,0:T(8,128)S(1)} %get-tuple-element.48.right.refs_1_, ...), custom_call_target="tpu_custom_call" | custom-call | flops 125829120 | bytes 1441796 | tf_op jit(solution)/shard_map/pallas_call | solution.py:43
  27.9 2.4 %collective-permute-start.14 = (f32[320,128]{1,0:T(8,128)S(1)}, f32[320,128]{1,0:T(8,128)S(1)}, u32[]{:S(2)}, u32[]{:S(2)}) collective-permute-start(f32[320,128]{1,0:T(8,128)S(1)} %get-tuple-element.76.refs_6_), channel_id=1, source_target_pairs={{0,24},{8,16},{16,8},{24,0},{1,25},{9,17},{17,9},{25,1},{2,26},{10... | collective-permute-start | bytes 491528 | tf_op jit(solution)/shard_map/ppermute | solution.py:364
  30.3 0.5 %collective-permute-start.12 = (f32[320,128]{1,0:T(8,128)S(1)}, f32[320,128]{1,0:T(8,128)S(1)}, u32[]{:S(2)}, u32[]{:S(2)}) collective-permute-start(f32[320,128]{1,0:T(8,128)S(1)} %get-tuple-element.76.refs_6_), channel_id=1, source_target_pairs={{0,16},{8,24},{16,0},{24,8},{1,17},{9,25},{17,1},{25,9},{2,18},{10... | collective-permute-start | bytes 491528 | tf_op jit(solution)/shard_map/ppermute | solution.py:364
  30.8 0.7 %collective-permute-start.10 = (f32[320,128]{1,0:T(8,128)S(1)}, f32[320,128]{1,0:T(8,128)S(1)}, u32[]{:S(2)}, u32[]{:S(2)}) collective-permute-start(f32[320,128]{1,0:T(8,128)S(1)} %get-tuple-element.76.refs_6_), channel_id=1, source_target_pairs={{0,8},{8,0},{16,24},{24,16},{1,9},{9,1},{17,25},{25,17},{2,10},{10... | collective-permute-start | bytes 491528 | tf_op jit(solution)/shard_map/ppermute | solution.py:364
  31.5 0.5 %collective-permute-start.6 = (f32[256,128]{1,0:T(8,128)S(1)}, f32[256,128]{1,0:T(8,128)S(1)}, u32[]{:S(2)}, u32[]{:S(2)}) collective-permute-start(f32[256,128]{1,0:T(8,128)S(1)} %get-tuple-element.73.refs_2_), channel_id=1, source_target_pairs={{0,1},{1,0},{2,3},{3,2},{4,5},{5,4},{6,7},{7,6},{8,9},{9,8},{10,11... | collective-permute-start | bytes 393224 | tf_op jit(solution)/shard_map/ppermute | solution.py:361
  32.0 0.8 %collective-permute-done.4.away = f32[4,64,128]{2,1,0:T(8,128)S(1)} collective-permute-done((f32[4,64,128]{2,1,0:T(8,128)S(1)}, f32[4,64,128]{2,1,0:T(8,128)S(1)}, u32[]{:S(2)}, u32[]{:S(2)}) %collective-permute-start.4) | collective-permute-done | bytes 131104 | tf_op jit(solution)/shard_map/ppermute | solution.py:361
  33.0 2.2 %collective-permute-done.14.refs_12_ = f32[320,128]{1,0:T(8,128)S(1)} collective-permute-done((f32[320,128]{1,0:T(8,128)S(1)}, f32[320,128]{1,0:T(8,128)S(1)}, u32[]{:S(2)}, u32[]{:S(2)}) %collective-permute-start.14) | collective-permute-done | bytes 163872 | tf_op jit(solution)/shard_map/ppermute | solution.py:364
  35.2 1.4 %collective-permute-done.12.refs_10_ = f32[320,128]{1,0:T(8,128)S(1)} collective-permute-done((f32[320,128]{1,0:T(8,128)S(1)}, f32[320,128]{1,0:T(8,128)S(1)}, u32[]{:S(2)}, u32[]{:S(2)}) %collective-permute-start.12) | collective-permute-done | bytes 163872 | tf_op jit(solution)/shard_map/ppermute | solution.py:364
  36.7 0.5 %collective-permute-start.11 = (f32[320,128]{1,0:T(8,128)S(1)}, f32[320,128]{1,0:T(8,128)S(1)}, u32[]{:S(2)}, u32[]{:S(2)}) collective-permute-start(f32[320,128]{1,0:T(8,128)S(1)} %collective-permute-done.10.refs_8_), channel_id=1, source_target_pairs={{0,1},{1,0},{2,3},{3,2},{4,5},{5,4},{6,7},{7,6},{8,9},{9,8},{10,11... | collective-permute-start | bytes 491528 | tf_op jit(solution)/shard_map/ppermute | solution.py:361
  37.4 1.2 %collective-permute-done.8.refs_5_ = f32[256,128]{1,0:T(8,128)S(1)} collective-permute-done((f32[256,128]{1,0:T(8,128)S(1)}, f32[256,128]{1,0:T(8,128)S(1)}, u32[]{:S(2)}, u32[]{:S(2)}) %collective-permute-start.8) | collective-permute-done | bytes 131104 | tf_op jit(solution)/shard_map/ppermute | solution.py:361
  38.5 1.1 %shard_map.126 = (f32[512,128]{1,0:T(8,128)}, f32[3,512,128]{2,1,0:T(8,128)}, f32[512,128]{1,0:T(8,128)}) custom-call(s32[1]{0:T(128)S(6)} %copy.18._.child.refs_0_, f32[2,256,128]{2,1,0:T(8,128)S(1)} %get-tuple-element.66.refs_0_.solved, f32[256,128]{1,0:T(8,128)S(1)} %get-tuple-element.72.refs_0_, f32[256,128]{1,0:T(8,128)S(1)} %collective-permute-done.5.refs_1_, ...), custom_call_target="tpu_custom_call" | custom-call | flops 65536 | bytes 2686980 | tf_op jit(solution)/shard_map/pallas_call | solution.py:43
  (30 shorter events, 1.9 us)
Async XLA Ops:
  2.6 2.0 %collective-permute-start = (f32[320,128]{1,0:T(8,128)S(1)}, f32[320,128]{1,0:T(8,128)S(1)}, u32[]{:S(2)}, u32[]{:S(2)}) collective-permute-start(f32[320,128]{1,0:T(8,128)S(1)} %get-tuple-element.52), channel_id=1, source_target_pairs={{0,1},{1,0},{2,3},{3,2},{4,5},{5,4},{6,7},{7,6},{8,9},{9,8},{10,11... | collective-permute-start | bytes 491528 | tf_op jit(solution)/shard_map/ppermute | solution.py:361
  3.8 3.7 %copy-start = (f32[1,1,3,256,256]{4,3,2,1,0:T(8,128)S(1)}, f32[1,1,3,256,256]{4,3,2,1,0:T(8,128)}, u32[]{:S(2)}) copy-start(f32[1,1,3,256,256]{4,3,2,1,0:T(8,128)} %param.13) | copy-start | bytes 2359300
  4.6 2.9 %copy-start.1 = (f32[1,1,3,128,128]{4,3,2,1,0:T(8,128)S(1)}, f32[1,1,3,128,128]{4,3,2,1,0:T(8,128)}, u32[]{:S(2)}) copy-start(f32[1,1,3,128,128]{4,3,2,1,0:T(8,128)} %param.14) | copy-start | bytes 589828
  4.6 2.9 %copy-start.2 = (f32[1,1,3,128,128]{4,3,2,1,0:T(8,128)S(1)}, f32[1,1,3,128,128]{4,3,2,1,0:T(8,128)}, u32[]{:S(2)}) copy-start(f32[1,1,3,128,128]{4,3,2,1,0:T(8,128)} %param.15) | copy-start | bytes 589828
  4.8 6.8 %collective-permute-start.1 = (f32[256,128]{1,0:T(8,128)S(1)}, f32[256,128]{1,0:T(8,128)S(1)}, u32[]{:S(2)}, u32[]{:S(2)}) collective-permute-start(f32[256,128]{1,0:T(8,128)S(1)} %get-tuple-element.54.home), channel_id=1, source_target_pairs={{0,2},{1,3},{2,0},{3,1},{4,6},{5,7},{6,4},{7,5},{8,10},{9,11},{10,... | collective-permute-start | bytes 393224 | tf_op jit(solution)/shard_map/ppermute | solution.py:361
  11.9 15.8 %collective-permute-start.7 = (f32[256,128]{1,0:T(8,128)S(1)}, f32[256,128]{1,0:T(8,128)S(1)}, u32[]{:S(2)}, u32[]{:S(2)}) collective-permute-start(f32[256,128]{1,0:T(8,128)S(1)} %get-tuple-element.74.home), channel_id=1, source_target_pairs={{0,4},{1,5},{2,6},{3,7},{4,0},{5,1},{6,2},{7,3},{8,12},{9,13},{10,... | collective-permute-start | bytes 393224 | tf_op jit(solution)/shard_map/ppermute | solution.py:361
  14.7 7.7 %collective-permute-start.2 = (f32[64,128]{1,0:T(8,128)S(1)}, f32[64,128]{1,0:T(8,128)S(1)}, u32[]{:S(2)}, u32[]{:S(2)}) collective-permute-start(f32[64,128]{1,0:T(8,128)S(1)} %get-tuple-element.63.refs_0_), channel_id=1, source_target_pairs={{0,4},{1,5},{2,6},{3,7},{4,0},{5,1},{6,2},{7,3},{8,12},{9,13},{10,... | collective-permute-start | bytes 98312 | tf_op jit(solution)/shard_map/ppermute | solution.py:361
  22.4 4.3 %collective-permute-start.3 = (f32[2,64,128]{2,1,0:T(8,128)S(1)}, f32[2,64,128]{2,1,0:T(8,128)S(1)}, u32[]{:S(2)}, u32[]{:S(2)}) collective-permute-start(f32[2,64,128]{2,1,0:T(8,128)S(1)} %shard_map.120.home), channel_id=1, source_target_pairs={{0,2},{1,3},{2,0},{3,1},{4,6},{5,7},{6,4},{7,5},{8,10},{9,11},{10,... | collective-permute-start | bytes 196616 | tf_op jit(solution)/shard_map/ppermute | solution.py:361
  22.9 8.6 %collective-permute-start.5 = (f32[256,128]{1,0:T(8,128)S(1)}, f32[256,128]{1,0:T(8,128)S(1)}, u32[]{:S(2)}, u32[]{:S(2)}) collective-permute-start(f32[256,128]{1,0:T(8,128)S(1)} %get-tuple-element.72.refs_0_), channel_id=1, source_target_pairs={{0,1},{1,0},{2,3},{3,2},{4,5},{5,4},{6,7},{7,6},{8,9},{9,8},{10,11... | collective-permute-start | bytes 393224 | tf_op jit(solution)/shard_map/ppermute | solution.py:361
  27.9 7.3 %collective-permute-start.14 = (f32[320,128]{1,0:T(8,128)S(1)}, f32[320,128]{1,0:T(8,128)S(1)}, u32[]{:S(2)}, u32[]{:S(2)}) collective-permute-start(f32[320,128]{1,0:T(8,128)S(1)} %get-tuple-element.76.refs_6_), channel_id=1, source_target_pairs={{0,24},{8,16},{16,8},{24,0},{1,25},{9,17},{17,9},{25,1},{2,26},{10... | collective-permute-start | bytes 491528 | tf_op jit(solution)/shard_map/ppermute | solution.py:364
  30.3 6.4 %collective-permute-start.12 = (f32[320,128]{1,0:T(8,128)S(1)}, f32[320,128]{1,0:T(8,128)S(1)}, u32[]{:S(2)}, u32[]{:S(2)}) collective-permute-start(f32[320,128]{1,0:T(8,128)S(1)} %get-tuple-element.76.refs_6_), channel_id=1, source_target_pairs={{0,16},{8,24},{16,0},{24,8},{1,17},{9,25},{17,1},{25,9},{2,18},{10... | collective-permute-start | bytes 491528 | tf_op jit(solution)/shard_map/ppermute | solution.py:364
  30.8 5.9 %collective-permute-start.10 = (f32[320,128]{1,0:T(8,128)S(1)}, f32[320,128]{1,0:T(8,128)S(1)}, u32[]{:S(2)}, u32[]{:S(2)}) collective-permute-start(f32[320,128]{1,0:T(8,128)S(1)} %get-tuple-element.76.refs_6_), channel_id=1, source_target_pairs={{0,8},{8,0},{16,24},{24,16},{1,9},{9,1},{17,25},{25,17},{2,10},{10... | collective-permute-start | bytes 491528 | tf_op jit(solution)/shard_map/ppermute | solution.py:364
  31.5 1.3 %collective-permute-start.4 = (f32[4,64,128]{2,1,0:T(8,128)S(1)}, f32[4,64,128]{2,1,0:T(8,128)S(1)}, u32[]{:S(2)}, u32[]{:S(2)}) collective-permute-start(f32[4,64,128]{2,1,0:T(8,128)S(1)} %shard_map.122.home.tails), channel_id=1, source_target_pairs={{0,1},{1,0},{2,3},{3,2},{4,5},{5,4},{6,7},{7,6},{8,9},{9,8},{10,11... | collective-permute-start | bytes 393224 | tf_op jit(solution)/shard_map/ppermute | solution.py:361
  31.5 5.7 %collective-permute-start.6 = (f32[256,128]{1,0:T(8,128)S(1)}, f32[256,128]{1,0:T(8,128)S(1)}, u32[]{:S(2)}, u32[]{:S(2)}) collective-permute-start(f32[256,128]{1,0:T(8,128)S(1)} %get-tuple-element.73.refs_2_), channel_id=1, source_target_pairs={{0,1},{1,0},{2,3},{3,2},{4,5},{5,4},{6,7},{7,6},{8,9},{9,8},{10,11... | collective-permute-start | bytes 393224 | tf_op jit(solution)/shard_map/ppermute | solution.py:361
  32.8 5.7 %collective-permute-start.9 = (f32[320,128]{1,0:T(8,128)S(1)}, f32[320,128]{1,0:T(8,128)S(1)}, u32[]{:S(2)}, u32[]{:S(2)}) collective-permute-start(f32[320,128]{1,0:T(8,128)S(1)} %get-tuple-element.76.refs_6_), channel_id=1, source_target_pairs={{0,1},{1,0},{2,3},{3,2},{4,5},{5,4},{6,7},{7,6},{8,9},{9,8},{10,11... | collective-permute-start | bytes 491528 | tf_op jit(solution)/shard_map/ppermute | solution.py:361
  35.2 4.5 %collective-permute-start.15 = (f32[320,128]{1,0:T(8,128)S(1)}, f32[320,128]{1,0:T(8,128)S(1)}, u32[]{:S(2)}, u32[]{:S(2)}) collective-permute-start(f32[320,128]{1,0:T(8,128)S(1)} %collective-permute-done.14.refs_12_), channel_id=1, source_target_pairs={{0,1},{1,0},{2,3},{3,2},{4,5},{5,4},{6,7},{7,6},{8,9},{9,8},{10,11... | collective-permute-start | bytes 491528 | tf_op jit(solution)/shard_map/ppermute | solution.py:361
  36.7 3.0 %collective-permute-start.13 = (f32[320,128]{1,0:T(8,128)S(1)}, f32[320,128]{1,0:T(8,128)S(1)}, u32[]{:S(2)}, u32[]{:S(2)}) collective-permute-start(f32[320,128]{1,0:T(8,128)S(1)} %collective-permute-done.12.refs_10_), channel_id=1, source_target_pairs={{0,1},{1,0},{2,3},{3,2},{4,5},{5,4},{6,7},{7,6},{8,9},{9,8},{10,11... | collective-permute-start | bytes 491528 | tf_op jit(solution)/shard_map/ppermute | solution.py:361
  36.7 3.0 %collective-permute-start.11 = (f32[320,128]{1,0:T(8,128)S(1)}, f32[320,128]{1,0:T(8,128)S(1)}, u32[]{:S(2)}, u32[]{:S(2)}) collective-permute-start(f32[320,128]{1,0:T(8,128)S(1)} %collective-permute-done.10.refs_8_), channel_id=1, source_target_pairs={{0,1},{1,0},{2,3},{3,2},{4,5},{5,4},{6,7},{7,6},{8,9},{9,8},{10,11... | collective-permute-start | bytes 491528 | tf_op jit(solution)/shard_map/ppermute | solution.py:361
  37.2 1.3 %collective-permute-start.8 = (f32[256,128]{1,0:T(8,128)S(1)}, f32[256,128]{1,0:T(8,128)S(1)}, u32[]{:S(2)}, u32[]{:S(2)}) collective-permute-start(f32[256,128]{1,0:T(8,128)S(1)} %get-tuple-element.75.refs_4_), channel_id=1, source_target_pairs={{0,1},{1,0},{2,3},{3,2},{4,5},{5,4},{6,7},{7,6},{8,9},{9,8},{10,11... | collective-permute-start | bytes 393224 | tf_op jit(solution)/shard_map/ppermute | solution.py:361
